TPU v7x, 128 devices: a whole 4x4x4 slice. The times are simulated.
128 devices in a mesh: seq: 16 (over z, x), exp: 8 (over y, core).
Axes of the slice: x: 4, y: 4, z: 4, core: 2. Of those that a mesh axis runs over, the one named last changes fastest.
Arguments:
- residual: bfloat16 [8192, 8192], P('seq', 'exp'), may hold values from -16 to 16
- queries: bfloat16 [8192, 4096], P('seq', 'exp'), may hold values from -6 to 6
- keys: bfloat16 [8192, 4096], P('seq', 'exp'), may hold values from -10 to 10
- values: bfloat16 [8192, 4096], P('seq', 'exp'), may hold values from -6 to 6
- documents: int32 [8192], replicated, may hold values from 0 to 1, as said below
- out_proj: bfloat16 [4096, 8192], P(None, 'exp'), may hold values from -0.09375 to 0.09375
- modality: int32 [8192], P('seq'), may hold values from 0 to 1, as said below
- norm_gain: float32 [2, 8192], P(None, 'exp'), may hold values from 0.25 to 1.75
- picks: int32 [8, 128], replicated, may hold values from 0 to 8191, as said below
- router: bfloat16 [8192, 8], P(None, 'exp'), may hold values from -0.0625 to 0.0625
- w_gate: bfloat16 [8, 8192, 4096], P('exp', None, 'seq'), may hold values from -0.0625 to 0.0625
- w_up: bfloat16 [8, 8192, 4096], P('exp', None, 'seq'), may hold values from -0.0625 to 0.0625
- w_down: bfloat16 [8, 4096, 8192], P('exp', 'seq'), may hold values from -0.09375 to 0.09375
Outputs:
- layer_out: bfloat16 [8192, 8192], P('seq', 'exp')
Inputs may be any that keep to these rules, and one draw needn't show every extreme that they name: `modality`: 0 marks a text token, 1 an image token. `documents`: 0 for the first document, 1 for the second; the second begins between position 2048 and 6144. `picks`: row e lists 128 different positions in ascending order; all carry modality 0 for e < 4 and modality 1 otherwise. Within each aligned block of 512 positions (the tokens of one index of seq) a row lists at most 16 positions, and every row lists exactly 16 in some block.
All inputs are finite; a program needn't handle non-finite values.
Results may differ from a plain program's by a relative error of at most 0.0035.
Values may be sent and summed in bfloat16 or wider, within the bound.
No kernel may reach another device: no remote copies, remote signals or barrier semaphores. Data moves between devices by JAX's collectives and lax.ppermute only.
A program may use at most 128 MiB of HBM per device.

v0:
```python
import math

import jax
import jax.numpy as jnp
from jax import lax
from jax.sharding import Mesh
from jax.sharding import PartitionSpec as P

D = 8192
HD = 128
SEQ = ("seq_0", "seq_1")


block_rows = 512


def in_one_piece(arrays, axis, dim, along):
    widths = [a.shape[along] for a in arrays]
    both = jnp.concatenate(arrays, axis=along)
    whole = lax.all_gather(both, axis, axis=dim, tiled=True)
    return tuple(jnp.split(whole, [sum(widths[:k]) for k in range(1, len(widths))], axis=along))


def from_everyone(shard, axis):
    size = lax.axis_size(axis)
    return lax.all_to_all(
        jnp.broadcast_to(shard[None], (size, *shard.shape)), axis, 0, 0, tiled=True
    )


def of_everyone(shard, axis):
    everything = from_everyone(shard, axis)
    return jnp.sum(everything, axis=0)


def own_rows(terms, axes):
    running = terms.astype(jnp.bfloat16)
    for axis in axes:
        running = lax.psum_scatter(running, axis, scatter_dimension=0, tiled=True)
    return running.astype(jnp.float32)


def shards(
    residual,
    queries,
    keys,
    values,
    documents,
    out_proj,
    modality,
    norm_gain,
    picks,
    router,
    w_gate,
    w_up,
    w_down,
):
    tokens = queries.shape[0]
    heads_here = queries.shape[1] // HD
    seq_pos = lax.axis_index(SEQ)
    start_row = seq_pos * tokens
    query_pos = start_row + jnp.arange(tokens, dtype=jnp.int32)
    query_doc = lax.dynamic_slice_in_dim(documents, start_row, tokens, 0)
    query_heads = queries.reshape(tokens, heads_here, HD)
    score_scale = 1.0 / math.sqrt(HD)

    def attend(state, key_rows, value_rows, key_start):
        row_count = key_rows.shape[0]
        key_pos = key_start + jnp.arange(row_count, dtype=jnp.int32)
        key_doc = lax.dynamic_slice_in_dim(documents, key_start, row_count, 0)
        scores = (
            jnp.einsum(
                "qhd,khd->qhk",
                query_heads,
                key_rows.reshape(row_count, heads_here, HD),
                preferred_element_type=jnp.float32,
            )
            * score_scale
        )
        allowed = (key_pos[None, :] <= query_pos[:, None]) & (
            key_doc[None, :] == query_doc[:, None]
        )
        scores = jnp.where(allowed[:, None, :], scores, -jnp.inf)
        running_max, running_sum, running_out = state
        new_max = jnp.maximum(running_max, jnp.max(scores, axis=2))
        factor = jnp.exp(running_max - new_max)
        weights = jnp.exp(scores - new_max[:, :, None])
        running_sum = running_sum * factor + jnp.sum(weights, axis=2)
        running_out = running_out * factor[:, :, None] + jnp.einsum(
            "qhk,khd->qhd",
            weights.astype(jnp.bfloat16),
            value_rows.reshape(row_count, heads_here, HD),
            preferred_element_type=jnp.float32,
        )
        return (new_max, running_sum, running_out)

    def visit_block(state, key_rows, value_rows, key_start):
        row_count = key_rows.shape[0]
        last_doc = lax.dynamic_index_in_dim(documents, key_start + row_count - 1, 0, keepdims=False)
        beyond = (key_start > query_pos[tokens - 1]) | (last_doc < query_doc[0])
        return lax.cond(
            beyond,
            lambda inner_state: inner_state,
            lambda inner_state: attend(inner_state, key_rows, value_rows, key_start),
            state,
        )

    initial = (
        jnp.full((tokens, heads_here), -1e30, jnp.float32),
        jnp.zeros((tokens, heads_here), jnp.float32),
        jnp.zeros((tokens, heads_here, HD), jnp.float32),
    )
    state = initial
    key_piece, value_piece = in_one_piece((keys, values), SEQ, 0, 1)
    row_count = key_piece.shape[0]
    blocks = row_count // block_rows
    key_stack = key_piece.reshape(blocks, block_rows, key_piece.shape[1])
    value_stack = value_piece.reshape(blocks, block_rows, value_piece.shape[1])

    def scan_step(inner_state, block_item):
        block_index, key_rows, value_rows = block_item
        return (visit_block(inner_state, key_rows, value_rows, block_index * block_rows), None)

    state, unused = lax.scan(
        scan_step, state, (jnp.arange(blocks, dtype=jnp.int32), key_stack, value_stack)
    )
    running_max, running_sum, running_out = state
    attended = (
        (running_out / running_sum[:, :, None])
        .reshape(tokens, heads_here * HD)
        .astype(jnp.bfloat16)
    )
    mixed = jnp.dot(
        lax.all_gather(attended, "exp", axis=1, tiled=True),
        out_proj,
        preferred_element_type=jnp.float32,
    )
    hidden_state = (residual.astype(jnp.float32) + mixed).astype(jnp.bfloat16)
    hidden_wide = hidden_state.astype(jnp.float32)
    square_total = of_everyone(jnp.sum(hidden_wide * hidden_wide, axis=1), "exp")
    inverse = lax.rsqrt(square_total / D + 1e-05)
    gain_rows = jnp.where(modality[:, None] == 0, norm_gain[0][None, :], norm_gain[1][None, :])
    normed = (hidden_wide * inverse[:, None] * gain_rows).astype(jnp.bfloat16)
    experts = picks.shape[0]
    capacity = tokens // 32
    inside = (picks >= start_row) & (picks < start_row + tokens)
    slot_index = jnp.cumsum(inside.astype(jnp.int32), axis=1) - 1
    matched = inside[:, None, :] & (
        slot_index[:, None, :] == jnp.arange(capacity, dtype=jnp.int32)[None, :, None]
    )
    local_index = jnp.sum(jnp.where(matched, picks[:, None, :] - start_row, 0), axis=2)
    filled = jnp.any(matched, axis=2)
    rows_out = jnp.take(normed, local_index.T, axis=0)
    rows_out = jnp.where(filled.T[:, :, None], rows_out, jnp.zeros_like(rows_out))
    arrived = lax.all_to_all(rows_out, "exp", split_axis=1, concat_axis=1, tiled=True)
    expert_rows = arrived.reshape(capacity, D)
    logits = jnp.dot(expert_rows, router, preferred_element_type=jnp.float32)[:, 0]
    piece = lax.all_gather(expert_rows, SEQ, axis=0, tiled=True)
    gate_part = jnp.dot(piece, w_gate[0], preferred_element_type=jnp.float32)
    up_part = jnp.dot(piece, w_up[0], preferred_element_type=jnp.float32)
    inner_act = (jax.nn.silu(gate_part) * up_part).astype(jnp.bfloat16)
    summed = own_rows(jnp.dot(inner_act, w_down[0], preferred_element_type=jnp.float32), SEQ)
    weighted = (jax.nn.sigmoid(logits)[:, None] * summed).astype(jnp.bfloat16)
    returned = lax.all_to_all(
        weighted.reshape(capacity, experts, D // experts),
        "exp",
        split_axis=1,
        concat_axis=1,
        tiled=True,
    )
    placing = (
        (jnp.arange(tokens, dtype=jnp.int32)[:, None, None] == local_index.T[None, :, :])
        & filled.T[None, :, :]
    ).astype(jnp.bfloat16)
    expert_add = jnp.einsum("tce,ced->td", placing, returned, preferred_element_type=jnp.float32)
    return (hidden_wide + expert_add).astype(jnp.bfloat16)


def solution(mesh):
    finer = Mesh(mesh.devices.reshape(4, 4, mesh.shape["exp"]), ("seq_0", "seq_1", "exp"))
    in_specs = (
        P(SEQ, "exp"),
        P(SEQ, "exp"),
        P(SEQ, "exp"),
        P(SEQ, "exp"),
        P(),
        P(None, "exp"),
        P(SEQ),
        P(None, "exp"),
        P(),
        P(None, "exp"),
        P("exp", None, SEQ),
        P("exp", None, SEQ),
        P("exp", SEQ, None),
    )
    out_specs = P(SEQ, "exp")
    return jax.shard_map(
        shards, mesh=finer, in_specs=in_specs, out_specs=out_specs, check_vma=False
    )
```

profile of v0, /device:TPU:1, one launch (start us, length us, event | category | flops | bytes accessed | tf_op | source)
XLA Modules:
  0.0 535.6 jit_solution(2753093686895501892)
XLA Ops:
  6.5 2.3 pad_maximum_fusion
  8.9 1.3 copy.78
  10.4 0.8 dynamic_slice.47
  11.2 113.0 %all-gather.4.cloned.1.call-done = bf16[8192,1024]{1,0:T(8,128)(2,1)} async-done(((bf16[512,1024]{1,0:T(8,128)(2,1)}), bf16[8192,1024]{1,0:T(8,128)(2,1)}) %all-gather.4.cloned.1.call-update) | async-done | bytes 16777232 | tf_op jit(solution)/shard_map/all_gather | solution.py:20
  124.2 11.3 %fusion.44 = (bf16[8192,512]{1,0:T(8,128)(2,1)}, bf16[8192,512]{1,0:T(8,128)(2,1)}) fusion(bf16[8192,1024]{1,0:T(8,128)(2,1)} %all-gather.4.cloned.1.call-done), kind=kLoop, calls=%fused_computation.66 | loop fusion | bytes 33554432 | tf_op jit(solution)/shard_map/split | solution.py:21
  135.5 12.3 %copy.79 = bf16[16,512,512]{1,2,0:T(8,128)(2,1)} copy(bf16[16,512,512]{2,1,0:T(8,128)(2,1)} %bitcast.84) | data formatting | bytes 16777216 | tf_op jit(solution)/shard_map/while | solution.py:124
  147.8 12.3 %copy.81 = bf16[16,512,512]{1,2,0:T(8,128)(2,1)} copy(bf16[16,512,512]{2,1,0:T(8,128)(2,1)} %bitcast.83) | data formatting | bytes 16777216 | tf_op jit(solution)/shard_map/while | solution.py:124
  160.2 97.3 %while.18 = (s32[]{:T(128)}, f32[512,4]{0,1:T(4,128)S(1)}, f32[512,4]{0,1:T(4,128)S(1)}, f32[512,4,128]{2,0,1:T(8,128)S(1)}, s32[16]{0:T(128)S(1)}, /*index=5*/s...) while((s32[]{:T(128)}, f32[512,4]{0,1:T(4,128)S(1)}, ...), condition=%wide.region_5.6_spmd, body=%wide.region_0.5_spmd.sunk | while | flops 549720576 | bytes 19544520 | solution.py:124
  161.5 1.3 dynamic_slice.53
  165.9 6.0 %conditional.2 = (f32[512,4]{0,1:T(4,128)S(1)}, f32[512,4]{0,1:T(4,128)S(1)}, f32[512,4,128]{2,0,1:T(8,128)S(1)}) conditional(s32[]{:T(128)} %convert_element_type.91, (s32[]{:T(128)}, s32[512]{0:T(512)S(1)}, s32[8192]{0:T(1024)}, s32[512]{0:T(512)S(1)}, bf16[16,512,512]{1,2,0:T(8,128)(2,1)}, /*index=5*/s32[]{:T(128)}, ...), branch_computations={%region_1.3_spmd, %region_4.4_spmd} | conditional | flops 549720576 | bytes 19527750 | solution.py:101
  165.9 0.8 dynamic_slice.41
  167.0 1.3 constant_dynamic-slice_fusion
  168.2 1.0 fusion.2
  169.3 0.9 fusion.1
  170.2 1.7 fusion.12
  173.2 1.3 dynamic_slice.53
  178.9 1.3 dynamic_slice.53
  184.6 1.3 dynamic_slice.53
  190.3 1.3 dynamic_slice.53
  196.0 1.3 dynamic_slice.53
  201.7 1.3 dynamic_slice.53
  207.4 1.3 dynamic_slice.53
  213.1 1.3 dynamic_slice.53
  218.8 1.3 dynamic_slice.53
  224.5 1.3 dynamic_slice.53
  230.2 1.3 dynamic_slice.53
  235.9 1.3 dynamic_slice.53
  241.6 1.3 dynamic_slice.53
  247.3 1.3 dynamic_slice.53
  253.0 1.3 dynamic_slice.53
  257.9 0.9 divide_convert_fusion
  259.8 90.1 %all-gather.6.cloned.1.call-done = bf16[512,4096]{0,1:T(8,128)(2,1)} async-done(((bf16[512,512]{0,1:T(8,128)(2,1)}), bf16[512,4096]{0,1:T(8,128)(2,1)}) %all-gather.6.cloned.1.call-update) | async-done | bytes 4194320 | tf_op jit(solution)/shard_map/all_gather | solution.py:134
  349.9 9.4 %fusion.22 = (f32[512]{0:T(512)S(1)}, bf16[512,1024]{1,0:T(8,128)(2,1)S(1)}) fusion(bf16[512,4096]{0,1:T(8,128)(2,1)} %all-gather.6.cloned.1.call-done, bf16[4096,1024]{1,0:T(8,128)(2,1)} %param.22, bf16[512,1024]{1,0:T(8,128)(2,1)} %param.17), kind=kOutput, calls=%fused_computation.30 | convolution fusion | flops 4298112512 | bytes 14682112 | tf_op jit(solution)/shard_map/dot_general | solution.py:133
  359.9 3.5 all-to-all-start
  363.4 4.7 all-to-all-done
  368.5 0.9 gather_fusion
  369.6 9.6 %all_to_all.16 = bf16[16,8,1024]{2,0,1:T(8,128)(2,1)S(1)} all-to-all(bf16[16,8,1024]{2,0,1:T(8,128)(2,1)S(1)} %fusion.36), channel_id=1, replica_groups=mesh['seq_0'=4,'seq_1'=4,'exp'=8] {'exp'}, dimensions={1} | all-to-all | bytes 524288 | tf_op jit(solution)/shard_map/all_to_all | solution.py:155
  380.2 51.4 %all-gather.8.cloned.1.call-done = bf16[256,8192]{1,0:T(8,128)(2,1)} async-done(((bf16[16,8192]{1,0:T(8,128)(2,1)}), bf16[256,8192]{1,0:T(8,128)(2,1)}) %all-gather.8.cloned.1.call-update) | async-done | bytes 4194320 | tf_op jit(solution)/shard_map/all_gather | solution.py:158
  431.5 4.8 fusion.20
  436.4 1.1 copy-done.7
  437.5 1.3 fusion.29
  438.8 0.9 copy-done.1
  439.7 3.2 convolution_convert_fusion
  442.9 46.8 %reduce-scatter.3.cloned.1.call-done = bf16[64,8192]{1,0:T(8,128)(2,1)} async-done(((bf16[256,8192]{1,0:T(8,128)(2,1)}), bf16[64,8192]{1,0:T(8,128)(2,1)}) %reduce-scatter.3.cloned.1.call-update) | async-done | bytes 1048592 | tf_op jit(solution)/shard_map/reduce_scatter | solution.py:39
  490.0 23.8 %reduce-scatter.5.cloned.1.call-done = bf16[16,8192]{1,0:T(8,128)(2,1)} async-done(((bf16[64,8192]{1,0:T(8,128)(2,1)}), bf16[16,8192]{1,0:T(8,128)(2,1)}) %reduce-scatter.5.cloned.1.call-update) | async-done | bytes 262160 | tf_op jit(solution)/shard_map/reduce_scatter | solution.py:39
  513.7 1.1 multiply_convert_fusion
  514.8 12.7 %all_to_all.17 = bf16[16,8,1024]{2,0,1:T(8,128)(2,1)S(1)} all-to-all(bf16[16,8,1024]{2,0,1:T(8,128)(2,1)S(1)} %bitcast.93), channel_id=1, replica_groups=mesh['seq_0'=4,'seq_1'=4,'exp'=8] {'exp'}, dimensions={1} | all-to-all | bytes 524288 | tf_op jit(solution)/shard_map/all_to_all | solution.py:164
  527.5 1.5 fusion.25
  (149 shorter events, 33.3 us)
Async XLA Ops:
  6.5 483.2 %copy-start = (bf16[8192,1]{0,1:T(2,128)(2,1)S(1)}, bf16[8192,1]{0,1:T(2,128)(2,1)}, u32[]{:S(2)}) copy-start(bf16[8192,1]{0,1:T(2,128)(2,1)} %param.26) | copy-start | bytes 49156
  6.5 117.6 %all-gather.4.cloned.1.call-start = ((), (), s32[]{:S(2)}) async-start(), calls=%async_computation.5 | async-start | bytes 17825792 | tf_op jit(solution)/shard_map/all_gather | solution.py:20
  8.9 341.0 %all-gather.6.cloned.1.call-start = ((), (), s32[]{:S(2)}) async-start(), calls=%async_computation.6 | async-start | bytes 4718592 | tf_op jit(solution)/shard_map/all_gather | solution.py:134
  257.5 1.3 copy-start.3
  257.5 2.2 copy-start.5
  257.5 2.3 copy-start.4
  359.9 8.2 %all-to-all-start = ((f32[8,1,512]{2,1,0:T(1,128)}), f32[8,1,512]{2,1,0:T(1,128)S(1)}, u32[]{:S(2)}, u32[]{:S(2)}) async-start(f32[8,1,512]{2,1,0:T(1,128)} %broadcast_in_dim.121), calls=%async_computation | async-start | bytes 32768 | tf_op jit(solution)/shard_map/all_to_all | solution.py:26
  363.4 68.1 %all-gather.8.cloned.1.call-start = ((), (), s32[]{:S(2)}) async-start(), calls=%async_computation.7 | async-start | bytes 4456448 | tf_op jit(solution)/shard_map/all_gather | solution.py:158
  379.9 109.8 %reduce-scatter.3.cloned.1.call-start = ((), (), s32[]{:S(2)}) async-start(), calls=%async_computation.8 | async-start | bytes 5242880 | tf_op jit(solution)/shard_map/reduce_scatter | solution.py:39
  431.5 4.9 copy-start.6
  431.5 5.9 %copy-start.7 = (bf16[256,8192]{1,0:T(8,128)(2,1)S(1)}, bf16[256,8192]{1,0:T(8,128)(2,1)}, u32[]{:S(2)}) copy-start(bf16[256,8192]{1,0:T(8,128)(2,1)} %all-gather.8.cloned.1.call-done) | copy-start | bytes 12582916
  437.5 2.2 copy-start.1
  442.9 46.9 %copy-start.2 = (bf16[8,2,8,1024]{3,2,0,1:T(8,128)(2,1)S(1)}, bf16[8,2,8,1024]{3,2,0,1:T(8,128)(2,1)}, u32[]{:S(2)}) copy-start(bf16[8,2,8,1024]{3,2,0,1:T(8,128)(2,1)} %copy.93) | copy-start | bytes 786436
  442.9 70.9 %reduce-scatter.5.cloned.1.call-start = ((), (), s32[]{:S(2)}) async-start(), calls=%async_computation.9 | async-start | bytes 1310720 | tf_op jit(solution)/shard_map/reduce_scatter | solution.py:39
Sparse Core Ops, SparseCore 0:
  9.5 114.6 all-gather.3
  258.9 90.8 all-gather.5
  380.1 51.4 all-gather.7
  443.0 46.6 reduce-scatter.2
  492.1 21.6 reduce-scatter.4
where the time goes:
time: 538 us; the launch traced here: 536 us
  waiting for transfers between devices  330 us (61%)
  local copies, waits for them, and re-layouts  94.1 us (17%)
  loops' own time  42.2 us (8%)
  matrix products  23.2 us (4%)
  blocking collectives  22.3 us (4%)
  between operations  13.4 us (2%)
  other arithmetic  6.84 us (1%)
    all_gather x1, waiting for transfers between devices, in_one_piece(): whole = lax.all_gather(both, axis, axis=dim, tiled=True)  113 us
    all_gather x1, waiting for transfers between devices, shards(): lax.all_gather(attended, 'exp', axis=1, tiled=True)  90.1 us
    reduce_scatter x2, waiting for transfers between devices, own_rows(): running = lax.psum_scatter(running, axis, scatter_dimension=0, tiled=True)  70.6 us
    all_gather x1, waiting for transfers between devices, shards(): piece = lax.all_gather(expert_rows, SEQ, axis=0, tiled=True)  51.4 us
    another operation x1, loops' own time, shards(): lax.scan(scan_step, state, (jnp.arange(blocks, dtype=jnp.int32), key_stac...  41.8 us
    while x4, local copies, waits for them, and re-layouts, shards(): lax.scan(scan_step, state, (jnp.arange(blocks, dtype=jnp.int32), key_stac...  25.3 us
    dynamic_slice x16, local copies, waits for them, and re-layouts, visit_block(): lax.dynamic_index_in_dim(documents, key_start + row_count - 1, 0, keepdim...  20.7 us
    slice x32, local copies, waits for them, and re-layouts, visit_block(): beyond = (key_start > query_pos[tokens - 1]) | (last_doc < query_doc[0])  18.9 us
  transfers between devices with their start and end apart: 6, of which 6 were waited for; matrix products, arithmetic and copies ran while one was open for 1% of the time, Pallas kernels for 0%

commit v1 on v0

v1 whole, which is shorter than its diff:
```python
import math

import jax
import jax.numpy as jnp
import numpy as np
from jax import lax
from jax.experimental import pallas as pl
from jax.experimental.pallas import tpu as pltpu
from jax.sharding import Mesh
from jax.sharding import PartitionSpec as P

D = 8192
HD = 128
TOK = 512
BLOCKS = 16
ALL = ("z", "x", "y", "c")
SEQ = ("z", "x")
EXP = ("y", "c")
NEG = -1e30
SCALE = math.log2(math.e) / math.sqrt(HD)

IDS = np.arange(128).reshape(4, 4, 4, 2)


def _groups(first):
    rows = []
    for y in range(4):
        for k in range(4):
            along_z, along_x = IDS[:, k, y, :], IDS[k, :, y, :]
            rows.append([int(i) for i in (along_z if first else along_x)[:, 0]])
            rows.append([int(i) for i in (along_x if first else along_z)[:, 1]])
    return rows


def _group16():
    rows = []
    for y in range(4):
        rows.append([int(i) for i in IDS[:, :, y, 0].reshape(-1)])
        rows.append([int(i) for i in IDS[:, :, y, 1].T.reshape(-1)])
    return rows


GROUP_A = _groups(True)
GROUP_B = _groups(False)
GROUP_AB = _group16()


def exchange(array, groups):
    return lax.all_to_all(array, ALL, 0, 0, tiled=True, axis_index_groups=groups)


def spread(array, groups):
    return exchange(jnp.broadcast_to(array[None], (4, *array.shape)), groups)


def attend_kernel(tab, r, o, vt, s, acc, m, l):
    bound = tab[32]
    sub = tab[33]

    def turn(t, carry):
        vt[t] = r[t, 512:1024, :].T
        return carry

    lax.fori_loop(0, BLOCKS, turn, 0)
    col = lax.broadcasted_iota(jnp.int32, (1, 256), 1)
    row = lax.broadcasted_iota(jnp.int32, (TOK, 1), 0)

    def score(t, q):
        return lax.dot_general(
            r[tab[t], 0:512, :], q, (((1,), (1,)), ((), ())), preferred_element_type=jnp.float32
        )

    def pair(pair_index, carry):
        j = 2 * pair_index
        q = jnp.concatenate([r[tab[j], 1024:1152, :], r[tab[j + 1], 1024:1152, :]], axis=0)
        first = j * TOK + sub * 128
        last = first + TOK + 127
        qpos = first + jnp.where(col < 128, col, col + (TOK - 128))
        qlow = jnp.where(qpos >= bound, bound, 0)
        lo = jnp.where(first >= bound, bound // TOK, 0)
        hi = j + 2
        m[...] = jnp.full((1, 256), NEG, jnp.float32)
        l[...] = jnp.zeros((1, 256), jnp.float32)
        acc[...] = jnp.zeros((HD, 256), jnp.float32)
        s[0] = score(lo, q)

        def step(t, inner):
            now = lax.rem(t - lo, 2)

            def go(masked):
                s[1 - now] = score(jnp.minimum(t + 1, hi - 1), q)
                here = s[now]
                if masked:
                    kpos = t * TOK + row
                    here = jnp.where((kpos <= qpos) & (kpos >= qlow), here, NEG)
                old = m[...]
                new = jnp.maximum(old, jnp.max(here, axis=0, keepdims=True))
                p = jnp.exp2(here * SCALE - new * SCALE)
                f = jnp.exp2((old - new) * SCALE)
                m[...] = new
                l[...] = l[...] * f + jnp.sum(p, axis=0, keepdims=True)
                acc[...] = acc[...] * f + jnp.dot(
                    vt[tab[t]], p.astype(jnp.bfloat16), preferred_element_type=jnp.float32
                )

            need = ((t + 1) * TOK - 1 > first) | ((t * TOK < bound) & (last >= bound))
            pl.when(need)(lambda: go(True))
            pl.when(jnp.logical_not(need))(lambda: go(False))
            return inner

        lax.fori_loop(lo, hi, step, 0)
        out = (acc[...] / l[...]).T.astype(jnp.bfloat16)
        o[tab[16 + j]] = out[:128]
        o[tab[17 + j]] = out[128:]
        return carry

    lax.fori_loop(0, BLOCKS // 2, pair, 0)


def attend(tab, received):
    return pl.pallas_call(
        attend_kernel,
        out_shape=jax.ShapeDtypeStruct((BLOCKS, 128, HD), jnp.bfloat16),
        in_specs=[
            pl.BlockSpec(memory_space=pltpu.SMEM),
            pl.BlockSpec(memory_space=pltpu.VMEM),
        ],
        out_specs=pl.BlockSpec(memory_space=pltpu.VMEM),
        scratch_shapes=[
            pltpu.VMEM((BLOCKS, HD, TOK), jnp.bfloat16),
            pltpu.VMEM((2, TOK, 256), jnp.float32),
            pltpu.VMEM((HD, 256), jnp.float32),
            pltpu.VMEM((1, 256), jnp.float32),
            pltpu.VMEM((1, 256), jnp.float32),
        ],
        compiler_params=pltpu.CompilerParams(vmem_limit_bytes=24 << 20),
        cost_estimate=pl.CostEstimate(
            flops=4_000_000_000, bytes_accessed=5_000_000, transcendentals=6_000_000
        ),
        name="attend",
    )(tab, received)


def project_kernel(c, x, w, base, o, acc, *, last):
    k = pl.program_id(0)

    @pl.when(k == 0)
    def _():
        acc[...] = base[...].astype(jnp.float32)

    acc[...] += jnp.dot(x[0], w[...], preferred_element_type=jnp.float32)

    @pl.when(k == 3)
    def _():
        o[...] = acc[...].astype(o.dtype)


def project(c, x, w, base, last):
    def kernel(c_ref, *refs):
        project_kernel(c_ref, *refs, last=last)

    return pl.pallas_call(
        kernel,
        grid_spec=pltpu.PrefetchScalarGridSpec(
            num_scalar_prefetch=1,
            grid=(4,),
            in_specs=[
                pl.BlockSpec((1, TOK, 512), lambda k, c_ref: (k, 0, 0)),
                pl.BlockSpec((512, 1024), lambda k, c_ref: (2 * k + c_ref[0], 0)),
                pl.BlockSpec((TOK, 1024), lambda k, c_ref: (0, 0), pipeline_mode=pl.Buffered(1)),
            ],
            out_specs=pl.BlockSpec((TOK, 1024), lambda k, c_ref: (0, 0)),
            scratch_shapes=[pltpu.VMEM((TOK, 1024), jnp.float32)],
        ),
        out_shape=jax.ShapeDtypeStruct((TOK, 1024), jnp.bfloat16 if last else jnp.float32),
        compiler_params=pltpu.CompilerParams(vmem_limit_bytes=24 << 20),
        cost_estimate=pl.CostEstimate(
            flops=2_200_000_000, bytes_accessed=9_000_000, transcendentals=0
        ),
        name="project",
    )(c, x, w, base)


def shards(
    residual,
    queries,
    keys,
    values,
    documents,
    out_proj,
    modality,
    norm_gain,
    picks,
    router,
    w_gate,
    w_up,
    w_down,
):
    z, x, y, c = (lax.axis_index(name) for name in ALL)
    seq = z * 4 + x
    expert = y * 2 + c
    b = jnp.where(c == 0, x, z)

    gain_sent = jnp.concatenate(
        [jnp.broadcast_to(norm_gain[k][None], (4, 1024)) for k in range(2)], axis=0
    ).reshape(8, 8, 128)
    gain = lax.all_to_all(gain_sent, EXP, 0, 0, tiled=True).reshape(1, D)

    sent = jnp.stack([a.reshape(TOK, 4, HD) for a in (queries, keys, values)], axis=0)
    got = exchange(sent.transpose(2, 0, 1, 3), GROUP_A)
    both = jnp.broadcast_to(got[:, 1:].reshape(1, 4, 1024, HD), (4, 4, 1024, HD))
    part = got[:, 0].reshape(4, 4, 128, HD).transpose(1, 0, 2, 3)
    received = exchange(jnp.concatenate([both, part], axis=2), GROUP_B)
    received = received.reshape(BLOCKS, 1152, HD)

    index = jnp.arange(BLOCKS, dtype=jnp.int32)
    swapped = (index % 4) * 4 + index // 4
    bound = documents.shape[0] - jnp.sum(documents)
    tab = jnp.concatenate(
        [
            jnp.where(c == 0, swapped, index),
            jnp.where(c == 0, index, swapped),
            jnp.stack([bound, b]).astype(jnp.int32),
        ]
    ).astype(jnp.int32)
    attended = exchange(attend(tab, received), GROUP_AB)
    attended = attended.reshape(4, TOK, HD).transpose(1, 0, 2).reshape(TOK, 4 * HD)

    mine = lax.all_to_all(
        jnp.broadcast_to(attended[None], (4, TOK, 512)), "y", 0, 0, tiled=True
    )
    theirs = lax.ppermute(mine, "c", [(0, 1), (1, 0)])
    core = jnp.reshape(c, (1,)).astype(jnp.int32)
    mixed = project(core, mine, out_proj, residual, False)
    hidden = project(1 - core, theirs, out_proj, mixed, True)

    ranked = picks.reshape(8, 8, 16)
    inside = (ranked // TOK) == seq
    local = jnp.sum(jnp.where(inside, ranked - seq * TOK, 0), axis=1).T.reshape(128, 1)
    filled = jnp.any(inside, axis=1).T.reshape(128, 1)
    hot = ((jnp.arange(TOK, dtype=jnp.int32)[None, :] == local) & filled).astype(jnp.bfloat16)
    rows = jnp.dot(hot, hidden, preferred_element_type=jnp.float32).astype(jnp.bfloat16)
    arrived = lax.all_to_all(rows.reshape(128, 8, 128), ALL, 0, 0, tiled=True)
    own = lax.dynamic_index_in_dim(ranked, expert, 0, keepdims=False)
    own = lax.dynamic_index_in_dim(own, seq, 1, keepdims=False)
    source = (own // TOK)[:, None] == jnp.arange(16, dtype=jnp.int32)[None, :]
    source = source.astype(jnp.bfloat16)
    taken = jnp.dot(source, arrived.reshape(16, D), preferred_element_type=jnp.float32)
    inverse = lax.rsqrt(jnp.mean(taken * taken, axis=1, keepdims=True) + 1e-05)
    chosen = (taken * inverse * gain).astype(jnp.bfloat16)
    logits = jnp.dot(chosen, router, preferred_element_type=jnp.float32)
    near = spread(chosen, GROUP_A)
    far = spread(near.reshape(32, D), GROUP_B)
    piece = far.reshape(128, D)
    gate_part = jnp.dot(piece, w_gate[0], preferred_element_type=jnp.float32)
    up_part = jnp.dot(piece, w_up[0], preferred_element_type=jnp.float32)
    inner_act = (jax.nn.silu(gate_part) * up_part).astype(jnp.bfloat16)
    partial = jnp.dot(inner_act, w_down[0], preferred_element_type=jnp.float32)
    partial = exchange(partial.astype(jnp.bfloat16).reshape(4, 32, D), GROUP_B)
    partial = jnp.sum(partial.astype(jnp.float32), axis=0).astype(jnp.bfloat16)
    partial = exchange(partial.reshape(4, 8, D), GROUP_A)
    summed = jnp.sum(partial.astype(jnp.float32), axis=0)
    weighted = (jax.nn.sigmoid(logits) * summed).astype(jnp.bfloat16)
    back = lax.dot_general(
        source, weighted, (((0,), (0,)), ((), ())), preferred_element_type=jnp.float32
    ).astype(jnp.bfloat16)
    returned = lax.all_to_all(back.reshape(128, 8, 128), ALL, 0, 0, tiled=True)
    expert_add = lax.dot_general(
        hot, returned.reshape(128, 1024), (((0,), (0,)), ((), ())), preferred_element_type=jnp.float32
    )
    return (hidden.astype(jnp.float32) + expert_add).astype(jnp.bfloat16)


def solution(mesh):
    finer = Mesh(mesh.devices.reshape(4, 4, 4, 2), ALL)
    in_specs = (
        P(SEQ, EXP),
        P(SEQ, EXP),
        P(SEQ, EXP),
        P(SEQ, EXP),
        P(),
        P(None, EXP),
        P(SEQ),
        P(None, EXP),
        P(),
        P(None, EXP),
        P(EXP, None, SEQ),
        P(EXP, None, SEQ),
        P(EXP, SEQ, None),
    )
    return jax.shard_map(
        shards, mesh=finer, in_specs=in_specs, out_specs=P(SEQ, EXP), check_vma=False
    )
```

time: 538 us -> 268 us (0.50)
  waiting for transfers between devices: 330 us -> 50.2 us
  blocking collectives: 22.3 us -> 120 us
  local copies, waits for them, and re-layouts: 94.1 us -> 16.2 us
  Pallas kernels: 0 us -> 43.2 us
  loops' own time: 42.2 us -> 0 us
  starting transfers between devices: 3.81 us -> 22.6 us
  between operations: 13.4 us -> 0.93 us
  matrix products: 23.2 us -> 10.8 us
    all_gather x3 -> x0, waiting for transfers between devices: 254 us -> none  [the longest x1 113 us: in_one_piece(): whole = lax.all_gather(both, axis, axis=dim, tiled=True)]
    all_to_all x2 -> x7, blocking collectives: 22.3 us -> 120 us  [the longest x5 76.1 us: exchange(): lax.all_to_all(array, ALL, 0, 0, tiled=True, axis_index_groups=groups)]
    reduce_scatter x2 -> x0, waiting for transfers between devices: 70.6 us -> none  [own_rows(): running = lax.psum_scatter(running, axis, scatter_dimension=0, tiled=True)]
    all_to_all x1 -> x4, waiting for transfers between devices: 4.66 us -> 50.2 us  [the longest x2 35.6 us: exchange(): lax.all_to_all(array, ALL, 0, 0, tiled=True, axis_index_groups=groups)]
    pallas_call x0 -> x3, Pallas kernels: none -> 43.2 us  [the longest x1 35.5 us: attend(): pl.pallas_call(attend_kernel, out_shape=jax.ShapeDtypeStruct((BLOCKS, 128...]
    another operation x17 -> x0, loops' own time: 42.2 us -> none  [the longest x1 41.8 us: shards(): lax.scan(scan_step, state, (jnp.arange(blocks, dtype=jnp.int32), key_stac...]
    dynamic_slice x35 -> x1, local copies, waits for them, and re-layouts: 33 us -> 0.08 us  [shards(): own = lax.dynamic_index_in_dim(own, seq, 1, keepdims=False)]
    while x20 -> x0, local copies, waits for them, and re-layouts: 25.3 us -> none  [the longest x4 25.3 us: shards(): lax.scan(scan_step, state, (jnp.arange(blocks, dtype=jnp.int32), key_stac...]
  transfers between devices with their start and end apart: 6 -> 5, of which waited for: 6 -> 4; matrix products, arithmetic and copies ran while one was open for 1% -> 1% of each run, Pallas kernels for 0% -> 1%
where the time goes in v1:
time: 268 us; the launch traced here: 269 us
  blocking collectives  120 us (45%)
  waiting for transfers between devices  50.2 us (19%)
  Pallas kernels  43.2 us (16%)
  starting transfers between devices  22.6 us (8%)
  local copies, waits for them, and re-layouts  16.2 us (6%)
  matrix products  10.8 us (4%)
  other arithmetic  4.9 us (2%)
    all_to_all x5, blocking collectives, exchange(): lax.all_to_all(array, ALL, 0, 0, tiled=True, axis_index_groups=groups)  76.1 us
    all_to_all x2, waiting for transfers between devices, exchange(): lax.all_to_all(array, ALL, 0, 0, tiled=True, axis_index_groups=groups)  35.6 us
    pallas_call x1, Pallas kernels, attend(): pl.pallas_call(attend_kernel, out_shape=jax.ShapeDtypeStruct((BLOCKS, 128...  35.5 us
    all_to_all x1, blocking collectives, shards(): lax.all_to_all(jnp.broadcast_to(attended[None], (4, TOK, 512)), 'y', 0, 0...  25.2 us
    all_to_all x1, blocking collectives, shards(): returned = lax.all_to_all(back.reshape(128, 8, 128), ALL, 0, 0, tiled=True)  18.8 us
    unnamed x26, local copies, waits for them, and re-layouts  12.9 us
    all_to_all x1, waiting for transfers between devices, shards(): arrived = lax.all_to_all(rows.reshape(128, 8, 128), ALL, 0, 0, tiled=True)  10.3 us
    all_to_all x2, starting transfers between devices, exchange(): lax.all_to_all(array, ALL, 0, 0, tiled=True, axis_index_groups=groups)  8.54 us
  transfers between devices with their start and end apart: 5, of which 4 were waited for; matrix products, arithmetic and copies ran while one was open for 1% of the time, Pallas kernels for 1%

profile of v1, /device:TPU:1, one launch (start us, length us, event | category | flops | bytes accessed | tf_op | source)
XLA Modules:
  0.0 268.9 jit_solution(6386199077233550086)
XLA Ops:
  0.0 1.3 copy.38
  1.3 1.3 copy.39
  2.6 0.2 copy.40
  2.8 0.2 maximum_bitcast_fusion
  3.0 0.1 copy.41
  3.1 17.5 %all_to_all.55 = bf16[4,3,512,128]{2,3,1,0:T(8,128)(2,1)S(1)} all-to-all(bf16[4,3,512,128]{2,3,1,0:T(8,128)(2,1)S(1)} %copy.41), channel_id=1, replica_groups={{0,32,64,96},{1,9,17,25},{8,40,72,104},{33,41,49,57},{16,48,80,112},{65..., dimensions={0} | all-to-all | bytes 3145728 | tf_op jit(solution)/shard_map/all_to_all | solution.py:49
  20.6 1.1 slice.16
  21.7 1.6 copy.49
  23.3 0.3 copy.50
  23.6 0.8 broadcast_in_dim.48
  24.4 2.5 pad_maximum_fusion
  26.9 5.1 %all-to-all-start.1 = ((bf16[4,4,1152,128]{3,2,1,0:T(8,128)(2,1)}), bf16[4,4,1152,128]{3,2,1,0:T(8,128)(2,1)}, u32[]{:S(2)}, u32[]{:S(2)}) async-start(bf16[4,4,1152,128]{3,2,1,0:T(8,128)(2,1)} %pad_maximum_fusion), calls=%async_computation.1 | async-start | bytes 9437184 | tf_op jit(solution)/shard_map/all_to_all | solution.py:49
  32.0 0.6 reduce_sum.48
  33.3 28.9 %all-to-all-done.1 = bf16[4,4,1152,128]{3,2,1,0:T(8,128)(2,1)} async-done(((bf16[4,4,1152,128]{3,2,1,0:T(8,128)(2,1)}), bf16[4,4,1152,128]{3,2,1,0:T(8,128)(2,1)}, u32[]{:S(2)}, u32[]{:S(2)}) %all-to-all-start.1) | async-done | bytes 4718624 | tf_op jit(solution)/shard_map/all_to_all | solution.py:49
  62.2 35.5 %attend.1 = bf16[16,128,128]{2,1,0:T(8,128)(2,1)S(1)} custom-call(s32[34]{0:T(128)S(1)} %pad_add_fusion.tab, bf16[16,1152,128]{2,1,0:T(8,128)(2,1)} %bitcast.10.r), custom_call_target="tpu_custom_call" | custom-call | flops 4000000000 | bytes 5000000 | tf_op jit(solution)/shard_map/attend/pallas_call | solution.py:121
  97.8 11.6 %all_to_all.56 = bf16[16,128,128]{2,1,0:T(8,128)(2,1)S(1)} all-to-all(bf16[16,128,128]{2,1,0:T(8,128)(2,1)S(1)} %attend.1), channel_id=1, replica_groups={{0,8,16,24,32,40,48,56,64,72,80,88,96,104,112,120},{1,33,65,97,9,41,73,..., dimensions={0} | all-to-all | bytes 1048576 | tf_op jit(solution)/shard_map/all_to_all | solution.py:49
  109.5 0.2 broadcast_in_dim.50
  109.7 25.2 %all_to_all.57.refs_0_ = bf16[4,512,512]{2,1,0:T(8,128)(2,1)S(1)} all-to-all(bf16[4,512,512]{2,1,0:T(8,128)(2,1)S(1)} %broadcast_in_dim.50), channel_id=1, replica_groups=mesh['z'=4,'x'=4,'y'=4,'c'=2] {'y'}, dimensions={0} | all-to-all | bytes 4194304 | tf_op jit(solution)/shard_map/all_to_all | solution.py:229
  135.0 6.2 %collective-permute-start = (bf16[4,512,512]{2,1,0:T(8,128)(2,1)S(1)}, bf16[4,512,512]{2,1,0:T(8,128)(2,1)}, u32[]{:S(2)}, u32[]{:S(2)}) collective-permute-start(bf16[4,512,512]{2,1,0:T(8,128)(2,1)S(1)} %all_to_all.57.refs_0_), channel_id=1, source_target_pairs={{0,1},{1,0},{2,3},{3,2},{4,5},{5,4},{6,7},{7,6},{8,9},{9,8},{10,11... | collective-permute-start | bytes 6291464 | tf_op jit(solution)/shard_map/ppermute | solution.py:232
  141.5 0.1 and.49
  141.7 3.4 %copy-done.1 = bf16[4096,1024]{1,0:T(8,128)(2,1)S(1)} copy-done((bf16[4096,1024]{1,0:T(8,128)(2,1)S(1)}, bf16[4096,1024]{1,0:T(8,128)(2,1)}, u32[]{:S(2)}) %copy-start.1) | copy-done | bytes 8388632
  145.1 3.2 %project.2.refs_2_ = f32[512,1024]{1,0:T(8,128)S(1)} custom-call(s32[1]{0:T(128)} %bitcast.c_ref, bf16[4,512,512]{2,1,0:T(8,128)(2,1)S(1)} %all_to_all.57.refs_0_, bf16[4096,1024]{1,0:T(8,128)(2,1)S(1)} %copy-done.1, bf16[512,1024]{1,0:T(8,128)(2,1)S(1)} %copy-done.3), custom_call_target="tpu_custom_call" | custom-call | flops 2200000000 | bytes 9000000 | tf_op jit(solution)/shard_map/project/pallas_call | solution.py:162
  148.3 3.4 %copy-done.2 = bf16[4096,1024]{1,0:T(8,128)(2,1)S(1)} copy-done((bf16[4096,1024]{1,0:T(8,128)(2,1)S(1)}, bf16[4096,1024]{1,0:T(8,128)(2,1)}, u32[]{:S(2)}) %copy-start.2) | copy-done | bytes 8388632
  151.7 4.5 %project.3 = bf16[512,1024]{1,0:T(8,128)(2,1)S(1)} custom-call(s32[1]{0:T(128)S(6)} %sub.28.c_ref, bf16[4,512,512]{2,1,0:T(8,128)(2,1)} %collective-permute-done.refs_0_, bf16[4096,1024]{1,0:T(8,128)(2,1)S(1)} %copy-done.2, f32[512,1024]{1,0:T(8,128)S(1)} %project.2.refs_2_), custom_call_target="tpu_custom_call" | custom-call | flops 2200000000 | bytes 9000000 | tf_op jit(solution)/shard_map/project/pallas_call | solution.py:162
  156.2 0.4 fusion.5
  156.6 0.8 copy.53
  157.3 3.9 %all-to-all-start.4 = ((bf16[128,8,128]{2,1,0:T(8,128)(2,1)}), bf16[128,8,128]{2,1,0:T(8,128)(2,1)S(1)}, u32[]{:S(2)}, u32[]{:S(2)}) async-start(bf16[128,8,128]{2,1,0:T(8,128)(2,1)} %bitcast.32), calls=%async_computation.4 | async-start | bytes 524288 | tf_op jit(solution)/shard_map/all_to_all | solution.py:243
  161.4 0.6 copy.65
  162.0 10.3 %all-to-all-done.4 = bf16[128,8,128]{2,1,0:T(8,128)(2,1)S(1)} async-done(((bf16[128,8,128]{2,1,0:T(8,128)(2,1)}), bf16[128,8,128]{2,1,0:T(8,128)(2,1)S(1)}, u32[]{:S(2)}, u32[]{:S(2)}) %all-to-all-start.4) | async-done | bytes 262176 | tf_op jit(solution)/shard_map/all_to_all | solution.py:243
  172.3 3.9 %all-to-all-start.5 = ((f32[8,8,128]{2,1,0:T(8,128)}), f32[8,8,128]{2,1,0:T(8,128)S(1)}, u32[]{:S(2)}, u32[]{:S(2)}) async-start(f32[8,8,128]{2,1,0:T(8,128)} %bitcast.81), calls=%async_computation.5 | async-start | bytes 65536 | tf_op jit(solution)/shard_map/all_to_all | solution.py:207
  176.3 0.1 reshape.99
  176.4 0.4 multiply_reduce_fusion
  176.8 4.2 %all-to-all-done.5 = f32[8,8,128]{2,1,0:T(8,128)S(1)} async-done(((f32[8,8,128]{2,1,0:T(8,128)}), f32[8,8,128]{2,1,0:T(8,128)S(1)}, u32[]{:S(2)}, u32[]{:S(2)}) %all-to-all-start.5) | async-done | bytes 32800 | tf_op jit(solution)/shard_map/all_to_all | solution.py:207
  181.0 0.1 multiply_convert_fusion.1
  181.2 9.4 %all_to_all.58 = bf16[4,8,8192]{2,1,0:T(8,128)(2,1)S(1)} all-to-all(bf16[4,8,8192]{2,1,0:T(8,128)(2,1)S(1)} %broadcast_in_dim.55), channel_id=1, replica_groups={{0,32,64,96},{1,9,17,25},{8,40,72,104},{33,41,49,57},{16,48,80,112},{65..., dimensions={0} | all-to-all | bytes 1048576 | tf_op jit(solution)/shard_map/all_to_all | solution.py:49
  190.6 0.2 broadcast_in_dim.57
  190.8 18.4 %all_to_all.59 = bf16[4,32,8192]{2,1,0:T(8,128)(2,1)S(1)} all-to-all(bf16[4,32,8192]{2,1,0:T(8,128)(2,1)S(1)} %broadcast_in_dim.57), channel_id=1, replica_groups={{0,8,16,24},{1,33,65,97},{32,40,48,56},{9,41,73,105},{64,72,80,88},{17,..., dimensions={0} | all-to-all | bytes 4194304 | tf_op jit(solution)/shard_map/all_to_all | solution.py:49
  209.2 0.8 fusion.3
  210.0 7.2 %convolution_convert_fusion = bf16[128,8192]{1,0:T(8,128)(2,1)} fusion(bf16[1,256,8192]{2,1,0:T(8,128)(2,1)} %param.24, bf16[128,8192]{1,0:T(8,128)(2,1)S(1)} %bitcast.83, bf16[1,8192,256]{2,1,0:T(8,128)(2,1)} %param.23, f32[128,256]{1,0:T(8,128)S(1)} %fusion.3), kind=kOutput, calls=%fused_computation | convolution fusion | flops 1074987008 | bytes 12713984 | tf_op jit(solution)/shard_map/dot_general | solution.py:258
  217.2 19.2 %all_to_all.60 = bf16[4,32,8192]{2,1,0:T(8,128)(2,1)S(1)} all-to-all(bf16[4,32,8192]{2,1,0:T(8,128)(2,1)} %bitcast.84), channel_id=1, replica_groups={{0,8,16,24},{1,33,65,97},{32,40,48,56},{9,41,73,105},{64,72,80,88},{17,..., dimensions={0} | all-to-all | bytes 4194304 | tf_op jit(solution)/shard_map/all_to_all | solution.py:49
  236.4 1.3 reduce_sum.51
  237.7 3.5 %all-to-all-start.9 = ((bf16[4,8,8192]{2,1,0:T(8,128)(2,1)}), bf16[4,8,8192]{2,1,0:T(8,128)(2,1)S(1)}, u32[]{:S(2)}, u32[]{:S(2)}) async-start(bf16[4,8,8192]{2,1,0:T(8,128)(2,1)} %bitcast.90), calls=%async_computation.9 | async-start | bytes 1048576 | tf_op jit(solution)/shard_map/all_to_all | solution.py:49
  241.2 0.2 fusion.15
  241.4 6.7 %all-to-all-done.9 = bf16[4,8,8192]{2,1,0:T(8,128)(2,1)S(1)} async-done(((bf16[4,8,8192]{2,1,0:T(8,128)(2,1)}), bf16[4,8,8192]{2,1,0:T(8,128)(2,1)S(1)}, u32[]{:S(2)}, u32[]{:S(2)}) %all-to-all-start.9) | async-done | bytes 524320 | tf_op jit(solution)/shard_map/all_to_all | solution.py:49
  248.1 0.3 convolution_convert_fusion.1
  248.5 0.1 reshape.105
  248.6 18.8 %all_to_all.61 = bf16[128,8,128]{2,1,0:T(8,128)(2,1)S(1)} all-to-all(bf16[128,8,128]{2,1,0:T(8,128)(2,1)S(1)} %reshape.105), channel_id=1, replica_groups=mesh['z'=4,'x'=4,'y'=4,'c'=2] {'z','x','y','c'}, dimensions={0} | all-to-all | bytes 524288 | tf_op jit(solution)/shard_map/all_to_all | solution.py:267
  267.4 1.5 add_convert_fusion
  (37 shorter events, 1.0 us)
Async XLA Ops:
  0.0 241.2 %copy-start = (bf16[8192,1]{0,1:T(2,128)(2,1)S(1)}, bf16[8192,1]{0,1:T(2,128)(2,1)}, u32[]{:S(2)}) copy-start(bf16[8192,1]{0,1:T(2,128)(2,1)} %param.21) | copy-start | bytes 49156
  0.0 2.6 copy-start.5
  26.9 5.1 %copy-start.6 = (s32[8192]{0:T(1024)S(1)}, s32[8192]{0:T(1024)}, u32[]{:S(2)}) copy-start(s32[8192]{0:T(1024)} %param.17) | copy-start | bytes 98308
  26.9 35.3 %all-to-all-start.1 = ((bf16[4,4,1152,128]{3,2,1,0:T(8,128)(2,1)}), bf16[4,4,1152,128]{3,2,1,0:T(8,128)(2,1)}, u32[]{:S(2)}, u32[]{:S(2)}) async-start(bf16[4,4,1152,128]{3,2,1,0:T(8,128)(2,1)} %pad_maximum_fusion), calls=%async_computation.1 | async-start | bytes 9437184 | tf_op jit(solution)/shard_map/all_to_all | solution.py:49
  109.7 31.4 %copy-start.8 = (s32[8,128]{1,0:T(8,128)S(1)}, s32[8,128]{1,0:T(8,128)}, u32[]{:S(2)}) copy-start(s32[8,128]{1,0:T(8,128)} %param.20) | copy-start | bytes 12292
  109.7 32.0 %copy-start.7 = (f32[2,1024]{1,0:T(2,128)S(1)}, f32[2,1024]{1,0:T(2,128)}, u32[]{:S(2)}) copy-start(f32[2,1024]{1,0:T(2,128)} %param.19) | copy-start | bytes 24580
  109.7 32.0 %copy-start.3 = (bf16[512,1024]{1,0:T(8,128)(2,1)S(1)}, bf16[512,1024]{1,0:T(8,128)(2,1)}, u32[]{:S(2)}) copy-start(bf16[512,1024]{1,0:T(8,128)(2,1)} %refs_2_.1) | copy-start | bytes 3145732
  135.0 13.3 %collective-permute-start = (bf16[4,512,512]{2,1,0:T(8,128)(2,1)S(1)}, bf16[4,512,512]{2,1,0:T(8,128)(2,1)}, u32[]{:S(2)}, u32[]{:S(2)}) collective-permute-start(bf16[4,512,512]{2,1,0:T(8,128)(2,1)S(1)} %all_to_all.57.refs_0_), channel_id=1, source_target_pairs={{0,1},{1,0},{2,3},{3,2},{4,5},{5,4},{6,7},{7,6},{8,9},{9,8},{10,11... | collective-permute-start | bytes 6291464 | tf_op jit(solution)/shard_map/ppermute | solution.py:232
  141.7 3.4 %copy-start.1 = (bf16[4096,1024]{1,0:T(8,128)(2,1)S(1)}, bf16[4096,1024]{1,0:T(8,128)(2,1)}, u32[]{:S(2)}) copy-start(bf16[4096,1024]{1,0:T(8,128)(2,1)} %refs_1_.3) | copy-start | bytes 25165828
  148.3 3.4 %copy-start.2 = (bf16[4096,1024]{1,0:T(8,128)(2,1)S(1)}, bf16[4096,1024]{1,0:T(8,128)(2,1)}, u32[]{:S(2)}) copy-start(bf16[4096,1024]{1,0:T(8,128)(2,1)} %refs_1_.3) | copy-start | bytes 25165828
  157.3 15.0 %all-to-all-start.4 = ((bf16[128,8,128]{2,1,0:T(8,128)(2,1)}), bf16[128,8,128]{2,1,0:T(8,128)(2,1)S(1)}, u32[]{:S(2)}, u32[]{:S(2)}) async-start(bf16[128,8,128]{2,1,0:T(8,128)(2,1)} %bitcast.32), calls=%async_computation.4 | async-start | bytes 524288 | tf_op jit(solution)/shard_map/all_to_all | solution.py:243
  172.3 8.7 %all-to-all-start.5 = ((f32[8,8,128]{2,1,0:T(8,128)}), f32[8,8,128]{2,1,0:T(8,128)S(1)}, u32[]{:S(2)}, u32[]{:S(2)}) async-start(f32[8,8,128]{2,1,0:T(8,128)} %bitcast.81), calls=%async_computation.5 | async-start | bytes 65536 | tf_op jit(solution)/shard_map/all_to_all | solution.py:207
  190.8 18.4 %copy-start.4 = (bf16[1,8192,256]{2,1,0:T(8,128)(2,1)S(1)}, bf16[1,8192,256]{2,1,0:T(8,128)(2,1)}, u32[]{:S(2)}) copy-start(bf16[1,8192,256]{2,1,0:T(8,128)(2,1)} %param.22) | copy-start | bytes 12582916
  237.7 10.4 %all-to-all-start.9 = ((bf16[4,8,8192]{2,1,0:T(8,128)(2,1)}), bf16[4,8,8192]{2,1,0:T(8,128)(2,1)S(1)}, u32[]{:S(2)}, u32[]{:S(2)}) async-start(bf16[4,8,8192]{2,1,0:T(8,128)(2,1)} %bitcast.90), calls=%async_computation.9 | async-start | bytes 1048576 | tf_op jit(solution)/shard_map/all_to_all | solution.py:49

commit v2 on v1

v2 whole, which is shorter than its diff:
```python
import math

import jax
import jax.numpy as jnp
import numpy as np
from jax import lax
from jax.experimental import pallas as pl
from jax.experimental.pallas import tpu as pltpu
from jax.sharding import Mesh
from jax.sharding import PartitionSpec as P

D = 8192
HD = 128
TOK = 512
BLOCKS = 16
ALL = ("z", "x", "y", "c")
SEQ = ("z", "x")
EXP = ("y", "c")
NEG = -1e30
SCALE = math.log2(math.e) / math.sqrt(HD)

IDS = np.arange(128).reshape(4, 4, 4, 2)


def _groups(first):
    rows = []
    for y in range(4):
        for k in range(4):
            along_z, along_x = IDS[:, k, y, :], IDS[k, :, y, :]
            rows.append([int(i) for i in (along_z if first else along_x)[:, 0]])
            rows.append([int(i) for i in (along_x if first else along_z)[:, 1]])
    return rows


def _group16():
    rows = []
    for y in range(4):
        rows.append([int(i) for i in IDS[:, :, y, 0].reshape(-1)])
        rows.append([int(i) for i in IDS[:, :, y, 1].T.reshape(-1)])
    return rows


GROUP_A = _groups(True)
GROUP_B = _groups(False)
GROUP_AB = _group16()


def exchange(array, groups):
    return lax.all_to_all(array, ALL, 0, 0, tiled=True, axis_index_groups=groups)


def spread(array, groups):
    return exchange(jnp.broadcast_to(array[None], (4, *array.shape)), groups)


def pack_heads_kernel(q, k, v, o):
    for i, ref in enumerate((q, k, v)):
        o[0, i] = ref[...]


def pack_heads(queries, keys, values):
    column = pl.BlockSpec((TOK, HD), lambda h: (0, h))
    return pl.pallas_call(
        pack_heads_kernel,
        grid=(4,),
        in_specs=[column] * 3,
        out_specs=pl.BlockSpec((1, 3, TOK, HD), lambda h: (h, 0, 0, 0)),
        out_shape=jax.ShapeDtypeStruct((4, 3, TOK, HD), jnp.bfloat16),
        name="pack_heads",
    )(queries, keys, values)


def pack_parts_kernel(got, q, o):
    for i in range(4):
        o[0, i, 0:TOK] = got[i, 1]
        o[0, i, TOK : 2 * TOK] = got[i, 2]
        o[0, i, 2 * TOK :] = q[i, 0]


def pack_parts(got):
    return pl.pallas_call(
        pack_parts_kernel,
        grid=(4,),
        in_specs=[
            pl.BlockSpec((4, 3, TOK, HD), lambda p: (0, 0, 0, 0)),
            pl.BlockSpec((4, 1, 128, HD), lambda p: (0, 0, p, 0)),
        ],
        out_specs=pl.BlockSpec((1, 4, 1152, HD), lambda p: (p, 0, 0, 0)),
        out_shape=jax.ShapeDtypeStruct((4, 4, 1152, HD), jnp.bfloat16),
        compiler_params=pltpu.CompilerParams(vmem_limit_bytes=16 << 20),
        name="pack_parts",
    )(got, got)


QW = 512
TILE = QW // 128


def attend_kernel(tab, r, o, vt, s0, s1, acc, m, l, qt):
    bound = tab[32]
    sub = tab[33]

    def turn(t, carry):
        vt[t] = r[t, TOK : 2 * TOK, :].T
        return carry

    lax.fori_loop(0, BLOCKS, turn, 0)
    col = lax.broadcasted_iota(jnp.int32, (1, QW), 1)
    row = lax.broadcasted_iota(jnp.int32, (TOK, 1), 0)

    def score(t):
        return jnp.dot(r[tab[t], 0:TOK, :], qt[...], preferred_element_type=jnp.float32)

    def tile(index, carry):
        j = TILE * index
        for i in range(TILE):
            qt[:, i * 128 : (i + 1) * 128] = r[tab[j + i], 2 * TOK :, :].T
        first = j * TOK + sub * 128
        last = first + (TILE - 1) * TOK + 127
        qpos = first + (col // 128) * TOK + col % 128
        qlow = jnp.where(qpos >= bound, bound, 0)
        lo = jnp.where(first >= bound, bound // (2 * TOK), 0)
        hi = (j + TILE) // 2
        m[...] = jnp.full((1, QW), NEG, jnp.float32)
        l[...] = jnp.zeros((1, QW), jnp.float32)
        acc[...] = jnp.zeros((HD, QW), jnp.float32)
        s0[...] = score(2 * lo)

        def soft(s, t, masked):
            here = s[...]
            if masked:
                kpos = t * TOK + row
                here = jnp.where((kpos <= qpos) & (kpos >= qlow), here, NEG)
            old = m[...]
            new = jnp.maximum(old, jnp.max(here, axis=0, keepdims=True))
            p = jnp.exp2(here * SCALE - new * SCALE)
            f = jnp.exp2((old - new) * SCALE)
            m[...] = new
            l[...] = l[...] * f + jnp.sum(p, axis=0, keepdims=True)
            acc[...] = acc[...] * f + jnp.dot(
                vt[tab[t]], p.astype(jnp.bfloat16), preferred_element_type=jnp.float32
            )

        def step(u, inner):
            t = 2 * u

            def go(masked):
                s1[...] = score(t + 1)
                soft(s0, t, masked)
                s0[...] = score(jnp.minimum(t + 2, j + TILE - 1))
                soft(s1, t + 1, masked)

            need = ((t + 2) * TOK - 1 > first) | ((t * TOK < bound) & (last >= bound))
            pl.when(need)(lambda: go(True))
            pl.when(jnp.logical_not(need))(lambda: go(False))
            return inner

        lax.fori_loop(lo, hi, step, 0)
        out = (acc[...] / l[...]).T.astype(jnp.bfloat16)
        for i in range(TILE):
            o[tab[16 + j + i]] = out[i * 128 : (i + 1) * 128]
        return carry

    lax.fori_loop(0, BLOCKS // TILE, tile, 0)


def attend(tab, received):
    return pl.pallas_call(
        attend_kernel,
        out_shape=jax.ShapeDtypeStruct((BLOCKS, 128, HD), jnp.bfloat16),
        in_specs=[
            pl.BlockSpec(memory_space=pltpu.SMEM),
            pl.BlockSpec(memory_space=pltpu.VMEM),
        ],
        out_specs=pl.BlockSpec(memory_space=pltpu.VMEM),
        scratch_shapes=[
            pltpu.VMEM((BLOCKS, HD, TOK), jnp.bfloat16),
            pltpu.VMEM((TOK, QW), jnp.float32),
            pltpu.VMEM((TOK, QW), jnp.float32),
            pltpu.VMEM((HD, QW), jnp.float32),
            pltpu.VMEM((1, QW), jnp.float32),
            pltpu.VMEM((1, QW), jnp.float32),
            pltpu.VMEM((HD, QW), jnp.bfloat16),
        ],
        compiler_params=pltpu.CompilerParams(vmem_limit_bytes=32 << 20),
        cost_estimate=pl.CostEstimate(
            flops=10_000_000_000, bytes_accessed=5_000_000, transcendentals=8_000_000
        ),
        name="attend",
    )(tab, received)


def project_kernel(order, mine, theirs, w, base, o, acc):
    k = pl.program_id(0)

    @pl.when(k == 0)
    def _():
        acc[...] = base[...].astype(jnp.float32)

    @pl.when(k < 4)
    def _():
        acc[...] += jnp.dot(mine[0], w[...], preferred_element_type=jnp.float32)

    @pl.when(k >= 4)
    def _():
        acc[...] += jnp.dot(theirs[0], w[...], preferred_element_type=jnp.float32)

    @pl.when(k == 7)
    def _():
        o[...] = acc[...].astype(jnp.bfloat16)


def project(order, mine, theirs, w, base):
    rows = base.shape[0]
    return pl.pallas_call(
        project_kernel,
        grid_spec=pltpu.PrefetchScalarGridSpec(
            num_scalar_prefetch=1,
            grid=(8,),
            in_specs=[
                pl.BlockSpec((1, rows, 512), lambda k, order: (jnp.minimum(k, 3), 0, 0)),
                pl.BlockSpec((1, rows, 512), lambda k, order: (jnp.maximum(k - 4, 0), 0, 0)),
                pl.BlockSpec((512, 1024), lambda k, order: (order[k], 0)),
                pl.BlockSpec((rows, 1024), lambda k, order: (0, 0)),
            ],
            out_specs=pl.BlockSpec((rows, 1024), lambda k, order: (0, 0)),
            scratch_shapes=[pltpu.VMEM((rows, 1024), jnp.float32)],
        ),
        out_shape=jax.ShapeDtypeStruct((rows, 1024), jnp.bfloat16),
        compiler_params=pltpu.CompilerParams(vmem_limit_bytes=24 << 20),
        cost_estimate=pl.CostEstimate(
            flops=rows * 8_388_608, bytes_accessed=8_388_608 + rows * 12_288, transcendentals=0
        ),
        name="project",
    )(order, mine, theirs, w, base)


def swap(array):
    return lax.ppermute(array, "c", [(0, 1), (1, 0)])


def ring(array, step):
    return lax.ppermute(array, "y", [(i, (i + step) % 4) for i in range(4)])


def in_three(array):
    parts = []
    for _ in range(3):
        part = lax.reduce_precision(array, 8, 7)
        parts.append(part.astype(jnp.bfloat16))
        array = array - part
    return parts


def shards(
    residual,
    queries,
    keys,
    values,
    documents,
    out_proj,
    modality,
    norm_gain,
    picks,
    router,
    w_gate,
    w_up,
    w_down,
):
    z, x, y, c = (lax.axis_index(name) for name in ALL)
    seq = z * 4 + x
    expert = y * 2 + c
    b = jnp.where(c == 0, x, z)

    got = exchange(pack_heads(queries, keys, values), GROUP_A)
    received = exchange(pack_parts(got), GROUP_B).reshape(BLOCKS, 1152, HD)

    index = jnp.arange(BLOCKS, dtype=jnp.int32)
    swapped = (index % 4) * 4 + index // 4
    bound = documents.shape[0] - jnp.sum(documents)
    tab = jnp.concatenate(
        [
            jnp.where(c == 0, swapped, index),
            jnp.where(c == 0, index, swapped),
            jnp.stack([bound, b]).astype(jnp.int32),
        ]
    ).astype(jnp.int32)
    attended = exchange(attend(tab, received), GROUP_AB)
    attended = attended.reshape(4, TOK, HD).transpose(1, 0, 2).reshape(TOK, 4 * HD)

    ranked = picks.reshape(8, 8, 16)
    inside = (ranked // TOK) == seq
    local = jnp.sum(jnp.where(inside, ranked - seq * TOK, 0), axis=1).T.reshape(128, 1)
    filled = jnp.any(inside, axis=1).T.reshape(128, 1)
    hot = ((jnp.arange(TOK, dtype=jnp.int32)[None, :] == local) & filled).astype(jnp.bfloat16)

    early = jnp.dot(hot, attended, preferred_element_type=jnp.float32).astype(jnp.bfloat16)
    gain_sent = jnp.stack(in_three(norm_gain), axis=1).reshape(12, 512)
    gain_sent = jnp.pad(gain_sent, ((0, 4), (0, 0)))
    early = jnp.concatenate([early, gain_sent], axis=0)
    mine = lax.all_to_all(jnp.broadcast_to(early[None], (4, 144, 512)), "y", 0, 0, tiled=True)
    theirs = swap(mine)
    chip = jnp.arange(4, dtype=jnp.int32)
    order = jnp.concatenate([2 * chip + c, 2 * chip + 1 - c]).astype(jnp.int32)
    base = jnp.dot(hot, residual, preferred_element_type=jnp.float32).astype(jnp.bfloat16)
    rows = project(order, mine, theirs, out_proj, base)
    gains = jnp.stack([mine[:, 128:140], theirs[:, 128:140]]).reshape(2, 4, 2, 3, 1024)
    gains = jnp.where(expert < 4, gains[:, :, 0], gains[:, :, 1]).astype(jnp.float32)
    gains = gains[:, :, 0] + (gains[:, :, 1] + gains[:, :, 2])
    gains = jnp.where(c == 0, gains, gains[::-1])
    gain = gains.transpose(1, 0, 2).reshape(1, D)

    held, rows = lax.optimization_barrier((attended, rows))
    arrived = lax.all_to_all(rows.reshape(128, 8, 128), ALL, 0, 0, tiled=True)
    before = ring(held, 1)
    after = ring(held, -1)
    half = TOK // 2
    opposite = jnp.concatenate([ring(before[:half], 1), ring(after[half:], -1)], axis=0)
    mine = jnp.stack([held, before, after, opposite])
    theirs = swap(mine)
    chip = jnp.remainder(y + jnp.array([0, 3, 1, 2], jnp.int32), 4)
    order = jnp.concatenate([2 * chip + c, 2 * chip + 1 - c]).astype(jnp.int32)
    hidden = project(order, mine, theirs, out_proj, residual)

    own = lax.dynamic_index_in_dim(ranked, expert, 0, keepdims=False)
    own = lax.dynamic_index_in_dim(own, seq, 1, keepdims=False)
    source = (own // TOK)[:, None] == jnp.arange(16, dtype=jnp.int32)[None, :]
    source = source.astype(jnp.bfloat16)
    taken = jnp.dot(source, arrived.reshape(16, D), preferred_element_type=jnp.float32)
    inverse = lax.rsqrt(jnp.mean(taken * taken, axis=1, keepdims=True) + 1e-05)
    chosen = (taken * inverse * gain).astype(jnp.bfloat16)
    logits = jnp.dot(chosen, router, preferred_element_type=jnp.float32)
    near = spread(chosen, GROUP_A)
    far = spread(near.reshape(32, D), GROUP_B)
    piece = far.reshape(128, D)
    gate_part = jnp.dot(piece, w_gate[0], preferred_element_type=jnp.float32)
    up_part = jnp.dot(piece, w_up[0], preferred_element_type=jnp.float32)
    inner_act = (jax.nn.silu(gate_part) * up_part).astype(jnp.bfloat16)
    partial = jnp.dot(inner_act, w_down[0], preferred_element_type=jnp.float32)
    partial = exchange(partial.astype(jnp.bfloat16).reshape(4, 32, D), GROUP_B)
    partial = jnp.sum(partial.astype(jnp.float32), axis=0).astype(jnp.bfloat16)
    partial = exchange(partial.reshape(4, 8, D), GROUP_A)
    summed = jnp.sum(partial.astype(jnp.float32), axis=0)
    weighted = (jax.nn.sigmoid(logits) * summed).astype(jnp.bfloat16)
    back = lax.dot_general(
        source, weighted, (((0,), (0,)), ((), ())), preferred_element_type=jnp.float32
    ).astype(jnp.bfloat16)
    returned = lax.all_to_all(back.reshape(128, 8, 128), ALL, 0, 0, tiled=True)
    expert_add = lax.dot_general(
        hot, returned.reshape(128, 1024), (((0,), (0,)), ((), ())), preferred_element_type=jnp.float32
    )
    return (hidden.astype(jnp.float32) + expert_add).astype(jnp.bfloat16)


def solution(mesh):
    finer = Mesh(mesh.devices.reshape(4, 4, 4, 2), ALL)
    in_specs = (
        P(SEQ, EXP),
        P(SEQ, EXP),
        P(SEQ, EXP),
        P(SEQ, EXP),
        P(),
        P(None, EXP),
        P(SEQ),
        P(None, EXP),
        P(),
        P(None, EXP),
        P(EXP, None, SEQ),
        P(EXP, None, SEQ),
        P(EXP, SEQ, None),
    )
    return jax.shard_map(
        shards, mesh=finer, in_specs=in_specs, out_specs=P(SEQ, EXP), check_vma=False
    )
```

time: 268 us -> 241 us (0.90); the launches traced: 269 us -> 239 us
  blocking collectives: 120 us -> 27.1 us
  waiting for transfers between devices: 50.2 us -> 84.3 us
  starting transfers between devices: 22.6 us -> 50.5 us
  Pallas kernels: 43.2 us -> 36.3 us
  other arithmetic: 4.9 us -> 9.29 us
    all_to_all x5 -> x2, blocking collectives: 76.1 us -> 27.1 us  [exchange(): lax.all_to_all(array, ALL, 0, 0, tiled=True, axis_index_groups=groups)]
    all_to_all x2 -> x0, blocking collectives: 44 us -> none  [the longest x1 25.2 us: shards(): lax.all_to_all(jnp.broadcast_to(attended[None], (4, TOK, 512)), 'y', 0, 0...]
    all_to_all x2 -> x5, waiting for transfers between devices: 35.6 us -> 55.6 us  [exchange(): lax.all_to_all(array, ALL, 0, 0, tiled=True, axis_index_groups=groups)]
    pallas_call x1, Pallas kernels: 35.5 us -> 20.6 us  [attend(): pl.pallas_call(attend_kernel, out_shape=jax.ShapeDtypeStruct((BLOCKS, 128...]
    all_to_all x2 -> x5, starting transfers between devices: 8.54 us -> 22.8 us  [exchange(): lax.all_to_all(array, ALL, 0, 0, tiled=True, axis_index_groups=groups)]
    ppermute x1 -> x6, waiting for transfers between devices: 0.01 us -> 10.7 us  [the longest x4 10.4 us: ring(): return lax.ppermute(array, 'y', [(i, (i + step) % 4) for i in range(4)])]
    pallas_call x2 -> x4, Pallas kernels: 7.7 us -> 15.8 us  [the longest x2 11.7 us: project(): pl.pallas_call(project_kernel, grid_spec=pltpu.PrefetchScalarGridSpec(num...]
    all_to_all x1 -> x2, starting transfers between devices: 3.94 us -> 10.9 us  [the longest x1 6.69 us: shards(): returned = lax.all_to_all(back.reshape(128, 8, 128), ALL, 0, 0, tiled=True)]
  transfers between devices with their start and end apart: 5 -> 14, of which waited for: 4 -> 8; matrix products, arithmetic and copies ran while one was open for 1% -> 10% of each run, Pallas kernels for 1% -> 3%
where the time goes in v2:
time: 241 us; the launch traced here: 239 us
  waiting for transfers between devices  84.3 us (35%)
  starting transfers between devices  50.5 us (21%)
  Pallas kernels  36.3 us (15%)
  blocking collectives  27.1 us (11%)
  local copies, waits for them, and re-layouts  18.4 us (8%)
  matrix products  12.2 us (5%)
  other arithmetic  9.29 us (4%)
    all_to_all x5, waiting for transfers between devices, exchange(): lax.all_to_all(array, ALL, 0, 0, tiled=True, axis_index_groups=groups)  55.6 us
    all_to_all x2, blocking collectives, exchange(): lax.all_to_all(array, ALL, 0, 0, tiled=True, axis_index_groups=groups)  27.1 us
    all_to_all x5, starting transfers between devices, exchange(): lax.all_to_all(array, ALL, 0, 0, tiled=True, axis_index_groups=groups)  22.8 us
    pallas_call x1, Pallas kernels, attend(): pl.pallas_call(attend_kernel, out_shape=jax.ShapeDtypeStruct((BLOCKS, 128...  20.6 us
    unnamed x32, local copies, waits for them, and re-layouts  12.5 us
    pallas_call x2, Pallas kernels, project(): pl.pallas_call(project_kernel, grid_spec=pltpu.PrefetchScalarGridSpec(num...  11.7 us
    all_to_all x1, waiting for transfers between devices, shards(): arrived = lax.all_to_all(rows.reshape(128, 8, 128), ALL, 0, 0, tiled=True)  11 us
    ppermute x4, waiting for transfers between devices, ring(): return lax.ppermute(array, 'y', [(i, (i + step) % 4) for i in range(4)])  10.4 us
  transfers between devices with their start and end apart: 14, of which 8 were waited for; matrix products, arithmetic and copies ran while one was open for 10% of the time, Pallas kernels for 3%

profile of v2, /device:TPU:1, one launch (start us, length us, event | category | flops | bytes accessed | tf_op | source)
XLA Modules:
  0.0 239.0 jit_solution(312873004522845487)
XLA Ops:
  0.0 3.6 %pack_heads.1 = bf16[4,3,512,128]{3,2,1,0:T(8,128)(2,1)} custom-call(bf16[512,512]{1,0:T(8,128)(2,1)} %q.1, bf16[512,512]{1,0:T(8,128)(2,1)} %k.1, bf16[512,512]{1,0:T(8,128)(2,1)} %v.1), custom_call_target="tpu_custom_call" | custom-call | tf_op jit(solution)/shard_map/pack_heads/pallas_call | solution.py:63
  3.6 17.7 %all_to_all.50.got.q = bf16[4,3,512,128]{3,2,1,0:T(8,128)(2,1)S(1)} all-to-all(bf16[4,3,512,128]{3,2,1,0:T(8,128)(2,1)} %pack_heads.1), channel_id=1, replica_groups={{0,32,64,96},{1,9,17,25},{8,40,72,104},{33,41,49,57},{16,48,80,112},{65..., dimensions={0} | all-to-all | bytes 3145728 | tf_op jit(solution)/shard_map/all_to_all | solution.py:49
  21.3 0.4 pack_parts.1
  21.8 2.2 copy-done.1
  24.0 5.1 %all-to-all-start.1 = ((bf16[4,4,1152,128]{3,2,1,0:T(8,128)(2,1)}), bf16[4,4,1152,128]{3,2,1,0:T(8,128)(2,1)}, u32[]{:S(2)}, u32[]{:S(2)}) async-start(bf16[4,4,1152,128]{3,2,1,0:T(8,128)(2,1)} %copy-done.1), calls=%async_computation.1 | async-start | bytes 9437184 | tf_op jit(solution)/shard_map/all_to_all | solution.py:49
  29.1 0.6 reduce_sum.48
  30.5 28.8 %all-to-all-done.1 = bf16[4,4,1152,128]{3,2,1,0:T(8,128)(2,1)} async-done(((bf16[4,4,1152,128]{3,2,1,0:T(8,128)(2,1)}), bf16[4,4,1152,128]{3,2,1,0:T(8,128)(2,1)}, u32[]{:S(2)}, u32[]{:S(2)}) %all-to-all-start.1) | async-done | bytes 4718624 | tf_op jit(solution)/shard_map/all_to_all | solution.py:49
  59.3 20.6 %attend.1 = bf16[16,128,128]{2,1,0:T(8,128)(2,1)} custom-call(s32[34]{0:T(128)S(1)} %pad_add_fusion.1.tab, bf16[16,1152,128]{2,1,0:T(8,128)(2,1)} %bitcast.2.r), custom_call_target="tpu_custom_call" | custom-call | flops 10000000000 | bytes 5000000 | tf_op jit(solution)/shard_map/attend/pallas_call | solution.py:168
  79.9 3.6 %all-to-all-start.2 = ((bf16[16,128,128]{2,1,0:T(8,128)(2,1)}), bf16[16,128,128]{2,1,0:T(8,128)(2,1)S(1)}, u32[]{:S(2)}, u32[]{:S(2)}) async-start(bf16[16,128,128]{2,1,0:T(8,128)(2,1)} %attend.1), calls=%async_computation.2 | async-start | bytes 1048576 | tf_op jit(solution)/shard_map/all_to_all | solution.py:49
  84.0 8.4 %all-to-all-done.2 = bf16[16,128,128]{2,1,0:T(8,128)(2,1)S(1)} async-done(((bf16[16,128,128]{2,1,0:T(8,128)(2,1)}), bf16[16,128,128]{2,1,0:T(8,128)(2,1)S(1)}, u32[]{:S(2)}, u32[]{:S(2)}) %all-to-all-start.2) | async-done | bytes 524320 | tf_op jit(solution)/shard_map/all_to_all | solution.py:49
  92.4 0.4 copy.27
  93.1 0.9 broadcast_in_dim.10
  94.0 4.2 %all-to-all-start.3 = ((bf16[4,144,512]{2,1,0:T(8,128)(2,1)}), bf16[4,144,512]{2,1,0:T(8,128)(2,1)S(1)}, u32[]{:S(2)}, u32[]{:S(2)}) async-start(bf16[4,144,512]{2,1,0:T(8,128)(2,1)} %broadcast_in_dim.10), calls=%async_computation.3 | async-start | bytes 1179648 | tf_op jit(solution)/shard_map/all_to_all | solution.py:301
  98.4 7.0 %all-to-all-done.3.mine = bf16[4,144,512]{2,1,0:T(8,128)(2,1)S(1)} async-done(((bf16[4,144,512]{2,1,0:T(8,128)(2,1)}), bf16[4,144,512]{2,1,0:T(8,128)(2,1)S(1)}, u32[]{:S(2)}, u32[]{:S(2)}) %all-to-all-start.3) | async-done | bytes 589856 | tf_op jit(solution)/shard_map/all_to_all | solution.py:301
  105.5 6.0 %collective-permute-start = (bf16[4,144,512]{2,1,0:T(8,128)(2,1)S(1)}, bf16[4,144,512]{2,1,0:T(8,128)(2,1)S(1)}, u32[]{:S(2)}, u32[]{:S(2)}) collective-permute-start(bf16[4,144,512]{2,1,0:T(8,128)(2,1)S(1)} %all-to-all-done.3.mine), channel_id=1, source_target_pairs={{0,1},{1,0},{2,3},{3,2},{4,5},{5,4},{6,7},{7,6},{8,9},{9,8},{10,11... | collective-permute-start | bytes 1769480 | tf_op jit(solution)/shard_map/ppermute | solution.py:239
  111.9 0.9 copy.47
  113.1 3.4 %copy-done.2 = bf16[4096,1024]{1,0:T(8,128)(2,1)S(1)} copy-done((bf16[4096,1024]{1,0:T(8,128)(2,1)S(1)}, bf16[4096,1024]{1,0:T(8,128)(2,1)}, u32[]{:S(2)}) %copy-start.2) | copy-done | bytes 8388632
  116.5 3.3 %project.2 = bf16[128,1024]{1,0:T(8,128)(2,1)S(1)} custom-call(s32[8]{0:T(128)S(1)} %pad_add_fusion.2.order, bf16[4,144,512]{2,1,0:T(8,128)(2,1)S(1)} %all-to-all-done.3.mine, bf16[4,144,512]{2,1,0:T(8,128)(2,1)S(1)} %collective-permute-done.theirs, bf16[4096,1024]{1,0:T(8,128)(2,1)S(1)} %copy-done.2, bf16[128,1024]{1,0:T(8,128)(2,1)S(1)} %convolution_convert_fusion.2.base), custom_call_target="tpu_custom_call" | custom-call | flops 1073741824 | bytes 9961472 | tf_op jit(solution)/shard_map/project/pallas_call | solution.py:215
  119.9 0.7 copy.36
  120.7 3.8 %all-to-all-start.4 = ((bf16[128,8,128]{2,1,0:T(8,128)(2,1)}), bf16[128,8,128]{2,1,0:T(8,128)(2,1)S(1)}, u32[]{:S(2)}, u32[]{:S(2)}) async-start(bf16[128,8,128]{2,1,0:T(8,128)(2,1)} %bitcast.30), calls=%async_computation.4 | async-start | bytes 524288 | tf_op jit(solution)/shard_map/all_to_all | solution.py:314
  124.7 11.0 %all-to-all-done.4 = bf16[128,8,128]{2,1,0:T(8,128)(2,1)S(1)} async-done(((bf16[128,8,128]{2,1,0:T(8,128)(2,1)}), bf16[128,8,128]{2,1,0:T(8,128)(2,1)S(1)}, u32[]{:S(2)}, u32[]{:S(2)}) %all-to-all-start.4) | async-done | bytes 262176 | tf_op jit(solution)/shard_map/all_to_all | solution.py:314
  136.3 9.4 %all_to_all.51 = bf16[4,8,8192]{2,1,0:T(8,128)(2,1)S(1)} all-to-all(bf16[4,8,8192]{2,1,0:T(8,128)(2,1)S(1)} %broadcast_in_dim.11), channel_id=1, replica_groups={{0,32,64,96},{1,9,17,25},{8,40,72,104},{33,41,49,57},{16,48,80,112},{65..., dimensions={0} | all-to-all | bytes 1048576 | tf_op jit(solution)/shard_map/all_to_all | solution.py:49
  145.7 1.5 broadcast_in_dim.13
  147.2 3.6 %all-to-all-start.6 = ((bf16[4,32,8192]{2,1,0:T(8,128)(2,1)}), bf16[4,32,8192]{2,1,0:T(8,128)(2,1)S(1)}, u32[]{:S(2)}, u32[]{:S(2)}) async-start(bf16[4,32,8192]{2,1,0:T(8,128)(2,1)} %broadcast_in_dim.13), calls=%async_computation.6 | async-start | bytes 4194304 | tf_op jit(solution)/shard_map/all_to_all | solution.py:49
  151.2 2.4 %collective-permute-start.2 = (bf16[512,512]{1,0:T(8,128)(2,1)}, bf16[512,512]{1,0:T(8,128)(2,1)S(1)}, u32[]{:S(2)}, u32[]{:S(2)}) collective-permute-start(bf16[512,512]{1,0:T(8,128)(2,1)} %bitcast.96), channel_id=1, source_target_pairs={{0,6},{2,0},{4,2},{6,4},{1,7},{3,1},{5,3},{7,5},{8,14},{10,8},{12,... | collective-permute-start | bytes 1572872 | tf_op jit(solution)/shard_map/ppermute | solution.py:243
  153.6 10.4 %collective-permute-done.1 = bf16[512,512]{1,0:T(8,128)(2,1)S(1)} collective-permute-done((bf16[512,512]{1,0:T(8,128)(2,1)}, bf16[512,512]{1,0:T(8,128)(2,1)S(1)}, u32[]{:S(2)}, u32[]{:S(2)}) %collective-permute-start.1) | collective-permute-done | bytes 524320 | tf_op jit(solution)/shard_map/ppermute | solution.py:243
  164.0 0.8 slice.36
  164.7 0.7 slice.37
  165.6 2.7 %collective-permute-start.4 = (bf16[256,512]{1,0:T(8,128)(2,1)}, bf16[256,512]{1,0:T(8,128)(2,1)}, u32[]{:S(2)}, u32[]{:S(2)}) collective-permute-start(bf16[256,512]{1,0:T(8,128)(2,1)} %slice.37), channel_id=1, source_target_pairs={{0,6},{2,0},{4,2},{6,4},{1,7},{3,1},{5,3},{7,5},{8,14},{10,8},{12,... | collective-permute-start | bytes 786440 | tf_op jit(solution)/shard_map/ppermute | solution.py:243
  168.3 2.9 %fusion.3 = f32[128,256]{1,0:T(8,128)S(1)} fusion(bf16[128,8192]{1,0:T(8,128)(2,1)S(1)} %bitcast.87, bf16[1,8192,256]{2,1,0:T(8,128)(2,1)} %param.23), kind=kOutput, calls=%fused_computation.5 | convolution fusion | flops 536870912 | bytes 6422528 | tf_op jit(solution)/shard_map/dot_general | solution.py:336
  171.2 7.2 %convolution_convert_fusion = bf16[128,8192]{1,0:T(8,128)(2,1)} fusion(bf16[1,256,8192]{2,1,0:T(8,128)(2,1)} %param.25, bf16[128,8192]{1,0:T(8,128)(2,1)S(1)} %bitcast.88, bf16[1,8192,256]{2,1,0:T(8,128)(2,1)} %param.24, f32[128,256]{1,0:T(8,128)S(1)} %fusion.3), kind=kOutput, calls=%fused_computation | convolution fusion | flops 1074987008 | bytes 12713984 | tf_op jit(solution)/shard_map/dot_general | solution.py:339
  178.4 6.4 %all-to-all-start.7 = ((bf16[4,32,8192]{2,1,0:T(8,128)(2,1)}), bf16[4,32,8192]{2,1,0:T(8,128)(2,1)}, u32[]{:S(2)}, u32[]{:S(2)}) async-start(bf16[4,32,8192]{2,1,0:T(8,128)(2,1)} %bitcast.89), calls=%async_computation.7 | async-start | bytes 4194304 | tf_op jit(solution)/shard_map/all_to_all | solution.py:49
  184.8 1.1 maximum_bitcast_fusion
  185.9 1.6 pad_maximum_fusion.mine
  187.5 1.6 collective-permute-start.5
  189.1 11.6 %all-to-all-done.7 = bf16[4,32,8192]{2,1,0:T(8,128)(2,1)} async-done(((bf16[4,32,8192]{2,1,0:T(8,128)(2,1)}), bf16[4,32,8192]{2,1,0:T(8,128)(2,1)}, u32[]{:S(2)}, u32[]{:S(2)}) %all-to-all-start.7) | async-done | bytes 2097184 | tf_op jit(solution)/shard_map/all_to_all | solution.py:49
  200.7 2.8 %reduce_sum.51 = bf16[32,8192]{1,0:T(8,128)(2,1)} reduce(bf16[4,32,8192]{2,1,0:T(8,128)(2,1)} %all-to-all-done.7, bf16[]{:T(256)} %constant.121.clone.1), dimensions={0}, to_apply=%region_4.5 | reduce | flops 786432 | bytes 2621442 | tf_op jit(solution)/shard_map/reduce_sum | solution.py:341
  203.6 4.1 %all-to-all-start.8 = ((bf16[4,8,8192]{2,1,0:T(8,128)(2,1)}), bf16[4,8,8192]{2,1,0:T(8,128)(2,1)}, u32[]{:S(2)}, u32[]{:S(2)}) async-start(bf16[4,8,8192]{2,1,0:T(8,128)(2,1)} %bitcast.94), calls=%async_computation.8 | async-start | bytes 1048576 | tf_op jit(solution)/shard_map/all_to_all | solution.py:49
  208.0 6.7 %all-to-all-done.8 = bf16[4,8,8192]{2,1,0:T(8,128)(2,1)} async-done(((bf16[4,8,8192]{2,1,0:T(8,128)(2,1)}), bf16[4,8,8192]{2,1,0:T(8,128)(2,1)}, u32[]{:S(2)}, u32[]{:S(2)}) %all-to-all-start.8) | async-done | bytes 524320 | tf_op jit(solution)/shard_map/all_to_all | solution.py:49
  214.7 1.1 convert_reduce_fusion
  216.2 0.8 reshape.114
  217.0 6.7 %all-to-all-start.9 = ((bf16[128,8,128]{2,1,0:T(8,128)(2,1)}), bf16[128,8,128]{2,1,0:T(8,128)(2,1)S(1)}, u32[]{:S(2)}, u32[]{:S(2)}) async-start(bf16[128,8,128]{2,1,0:T(8,128)(2,1)} %reshape.114), calls=%async_computation.9 | async-start | bytes 524288 | tf_op jit(solution)/shard_map/all_to_all | solution.py:348
  223.7 3.4 %copy-done.3 = bf16[4096,1024]{1,0:T(8,128)(2,1)S(1)} copy-done((bf16[4096,1024]{1,0:T(8,128)(2,1)S(1)}, bf16[4096,1024]{1,0:T(8,128)(2,1)}, u32[]{:S(2)}) %copy-start.3) | copy-done | bytes 8388632
  227.1 8.3 %project.3 = bf16[512,1024]{1,0:T(8,128)(2,1)S(1)} custom-call(s32[8]{0:T(128)S(1)} %pad_add_fusion.order, bf16[4,512,512]{2,1,0:T(8,128)(2,1)S(1)} %pad_maximum_fusion.mine, bf16[4,512,512]{2,1,0:T(8,128)(2,1)} %collective-permute-done.5.theirs, bf16[4096,1024]{1,0:T(8,128)(2,1)S(1)} %copy-done.3, bf16[512,1024]{1,0:T(8,128)(2,1)S(1)} %copy-done.4), custom_call_target="tpu_custom_call" | custom-call | flops 4294967296 | bytes 14680064 | tf_op jit(solution)/shard_map/project/pallas_call | solution.py:215
  235.5 1.0 copy-done.5
  236.4 0.6 fusion.18
  237.0 0.7 copy-done.6
  237.6 1.4 add_convert_fusion
  (73 shorter events, 3.9 us)
Async XLA Ops:
  0.0 207.8 %copy-start = (bf16[8192,1]{0,1:T(2,128)(2,1)S(1)}, bf16[8192,1]{0,1:T(2,128)(2,1)}, u32[]{:S(2)}) copy-start(bf16[8192,1]{0,1:T(2,128)(2,1)} %param.22) | copy-start | bytes 49156
  21.8 2.2 copy-start.1
  24.0 5.1 %copy-start.9 = (s32[8192]{0:T(1024)S(1)}, s32[8192]{0:T(1024)}, u32[]{:S(2)}) copy-start(s32[8192]{0:T(1024)} %param.18) | copy-start | bytes 98308
  24.0 5.8 %copy-start.11 = (s32[8,128]{1,0:T(8,128)S(1)}, s32[8,128]{1,0:T(8,128)}, u32[]{:S(2)}) copy-start(s32[8,128]{1,0:T(8,128)} %param.21) | copy-start | bytes 12292
  24.0 35.4 %all-to-all-start.1 = ((bf16[4,4,1152,128]{3,2,1,0:T(8,128)(2,1)}), bf16[4,4,1152,128]{3,2,1,0:T(8,128)(2,1)}, u32[]{:S(2)}, u32[]{:S(2)}) async-start(bf16[4,4,1152,128]{3,2,1,0:T(8,128)(2,1)} %copy-done.1), calls=%async_computation.1 | async-start | bytes 9437184 | tf_op jit(solution)/shard_map/all_to_all | solution.py:49
  59.3 24.6 %copy-start.10 = (f32[2,1024]{1,0:T(2,128)S(1)}, f32[2,1024]{1,0:T(2,128)}, u32[]{:S(2)}) copy-start(f32[2,1024]{1,0:T(2,128)} %param.20) | copy-start | bytes 24580
  79.9 12.5 %all-to-all-start.2 = ((bf16[16,128,128]{2,1,0:T(8,128)(2,1)}), bf16[16,128,128]{2,1,0:T(8,128)(2,1)S(1)}, u32[]{:S(2)}, u32[]{:S(2)}) async-start(bf16[16,128,128]{2,1,0:T(8,128)(2,1)} %attend.1), calls=%async_computation.2 | async-start | bytes 1048576 | tf_op jit(solution)/shard_map/all_to_all | solution.py:49
  84.0 27.5 %copy-start.4 = (bf16[512,1024]{1,0:T(8,128)(2,1)S(1)}, bf16[512,1024]{1,0:T(8,128)(2,1)}, u32[]{:S(2)}) copy-start(bf16[512,1024]{1,0:T(8,128)(2,1)} %base.1) | copy-start | bytes 3145732
  94.0 11.5 %all-to-all-start.3 = ((bf16[4,144,512]{2,1,0:T(8,128)(2,1)}), bf16[4,144,512]{2,1,0:T(8,128)(2,1)S(1)}, u32[]{:S(2)}, u32[]{:S(2)}) async-start(bf16[4,144,512]{2,1,0:T(8,128)(2,1)} %broadcast_in_dim.10), calls=%async_computation.3 | async-start | bytes 1179648 | tf_op jit(solution)/shard_map/all_to_all | solution.py:301
  105.5 7.7 %collective-permute-start = (bf16[4,144,512]{2,1,0:T(8,128)(2,1)S(1)}, bf16[4,144,512]{2,1,0:T(8,128)(2,1)S(1)}, u32[]{:S(2)}, u32[]{:S(2)}) collective-permute-start(bf16[4,144,512]{2,1,0:T(8,128)(2,1)S(1)} %all-to-all-done.3.mine), channel_id=1, source_target_pairs={{0,1},{1,0},{2,3},{3,2},{4,5},{5,4},{6,7},{7,6},{8,9},{9,8},{10,11... | collective-permute-start | bytes 1769480 | tf_op jit(solution)/shard_map/ppermute | solution.py:239
  113.1 3.4 %copy-start.2 = (bf16[4096,1024]{1,0:T(8,128)(2,1)S(1)}, bf16[4096,1024]{1,0:T(8,128)(2,1)}, u32[]{:S(2)}) copy-start(bf16[4096,1024]{1,0:T(8,128)(2,1)} %w.3) | copy-start | bytes 25165828
  120.7 15.0 %all-to-all-start.4 = ((bf16[128,8,128]{2,1,0:T(8,128)(2,1)}), bf16[128,8,128]{2,1,0:T(8,128)(2,1)S(1)}, u32[]{:S(2)}, u32[]{:S(2)}) async-start(bf16[128,8,128]{2,1,0:T(8,128)(2,1)} %bitcast.30), calls=%async_computation.4 | async-start | bytes 524288 | tf_op jit(solution)/shard_map/all_to_all | solution.py:314
  147.2 21.1 %all-to-all-start.6 = ((bf16[4,32,8192]{2,1,0:T(8,128)(2,1)}), bf16[4,32,8192]{2,1,0:T(8,128)(2,1)S(1)}, u32[]{:S(2)}, u32[]{:S(2)}) async-start(bf16[4,32,8192]{2,1,0:T(8,128)(2,1)} %broadcast_in_dim.13), calls=%async_computation.6 | async-start | bytes 4194304 | tf_op jit(solution)/shard_map/all_to_all | solution.py:49
  150.8 13.1 %collective-permute-start.1 = (bf16[512,512]{1,0:T(8,128)(2,1)}, bf16[512,512]{1,0:T(8,128)(2,1)S(1)}, u32[]{:S(2)}, u32[]{:S(2)}) collective-permute-start(bf16[512,512]{1,0:T(8,128)(2,1)} %bitcast.95), channel_id=1, source_target_pairs={{0,2},{2,4},{4,6},{6,0},{1,3},{3,5},{5,7},{7,1},{8,10},{10,12},{12... | collective-permute-start | bytes 1572872 | tf_op jit(solution)/shard_map/ppermute | solution.py:243
  151.2 13.6 %collective-permute-start.2 = (bf16[512,512]{1,0:T(8,128)(2,1)}, bf16[512,512]{1,0:T(8,128)(2,1)S(1)}, u32[]{:S(2)}, u32[]{:S(2)}) collective-permute-start(bf16[512,512]{1,0:T(8,128)(2,1)} %bitcast.96), channel_id=1, source_target_pairs={{0,6},{2,0},{4,2},{6,4},{1,7},{3,1},{5,3},{7,5},{8,14},{10,8},{12,... | collective-permute-start | bytes 1572872 | tf_op jit(solution)/shard_map/ppermute | solution.py:243
  164.0 1.5 copy-start.7
  164.7 20.0 %collective-permute-start.3 = (bf16[256,512]{1,0:T(8,128)(2,1)}, bf16[256,512]{1,0:T(8,128)(2,1)}, u32[]{:S(2)}, u32[]{:S(2)}) collective-permute-start(bf16[256,512]{1,0:T(8,128)(2,1)} %slice.36), channel_id=1, source_target_pairs={{0,2},{2,4},{4,6},{6,0},{1,3},{3,5},{5,7},{7,1},{8,10},{10,12},{12... | collective-permute-start | bytes 786440 | tf_op jit(solution)/shard_map/ppermute | solution.py:243
  164.7 0.9 copy-start.8
  165.6 19.2 %collective-permute-start.4 = (bf16[256,512]{1,0:T(8,128)(2,1)}, bf16[256,512]{1,0:T(8,128)(2,1)}, u32[]{:S(2)}, u32[]{:S(2)}) collective-permute-start(bf16[256,512]{1,0:T(8,128)(2,1)} %slice.37), channel_id=1, source_target_pairs={{0,6},{2,0},{4,2},{6,4},{1,7},{3,1},{5,3},{7,5},{8,14},{10,8},{12,... | collective-permute-start | bytes 786440 | tf_op jit(solution)/shard_map/ppermute | solution.py:243
  178.4 22.3 %all-to-all-start.7 = ((bf16[4,32,8192]{2,1,0:T(8,128)(2,1)}), bf16[4,32,8192]{2,1,0:T(8,128)(2,1)}, u32[]{:S(2)}, u32[]{:S(2)}) async-start(bf16[4,32,8192]{2,1,0:T(8,128)(2,1)} %bitcast.89), calls=%async_computation.7 | async-start | bytes 4194304 | tf_op jit(solution)/shard_map/all_to_all | solution.py:49
  185.8 3.3 %copy-start.12 = (s32[4]{0:T(128)S(1)}, s32[4]{0:T(128)}, u32[]{:S(2)}) copy-start(s32[4]{0:T(128)} %constant.130.clone) | copy-start | bytes 52
  187.5 36.2 %collective-permute-start.5 = (bf16[4,512,512]{2,1,0:T(8,128)(2,1)S(1)}, bf16[4,512,512]{2,1,0:T(8,128)(2,1)}, u32[]{:S(2)}, u32[]{:S(2)}) collective-permute-start(bf16[4,512,512]{2,1,0:T(8,128)(2,1)S(1)} %pad_maximum_fusion.mine), channel_id=1, source_target_pairs={{0,1},{1,0},{2,3},{3,2},{4,5},{5,4},{6,7},{7,6},{8,9},{9,8},{10,11... | collective-permute-start | bytes 6291464 | tf_op jit(solution)/shard_map/ppermute | solution.py:239
  203.6 11.1 %all-to-all-start.8 = ((bf16[4,8,8192]{2,1,0:T(8,128)(2,1)}), bf16[4,8,8192]{2,1,0:T(8,128)(2,1)}, u32[]{:S(2)}, u32[]{:S(2)}) async-start(bf16[4,8,8192]{2,1,0:T(8,128)(2,1)} %bitcast.94), calls=%async_computation.8 | async-start | bytes 1048576 | tf_op jit(solution)/shard_map/all_to_all | solution.py:49
  217.0 19.4 %all-to-all-start.9 = ((bf16[128,8,128]{2,1,0:T(8,128)(2,1)}), bf16[128,8,128]{2,1,0:T(8,128)(2,1)S(1)}, u32[]{:S(2)}, u32[]{:S(2)}) async-start(bf16[128,8,128]{2,1,0:T(8,128)(2,1)} %reshape.114), calls=%async_computation.9 | async-start | bytes 524288 | tf_op jit(solution)/shard_map/all_to_all | solution.py:348
  223.7 3.4 %copy-start.3 = (bf16[4096,1024]{1,0:T(8,128)(2,1)S(1)}, bf16[4096,1024]{1,0:T(8,128)(2,1)}, u32[]{:S(2)}) copy-start(bf16[4096,1024]{1,0:T(8,128)(2,1)} %w.3) | copy-start | bytes 25165828
  235.4 1.0 copy-start.5
  236.4 1.2 copy-start.6

commit v3 on v2

--- a/solution.py
+++ b/solution.py
@@ -1,3 +1,4 @@
+import functools
 import math
 
 import jax
@@ -13,6 +14,7 @@
 HD = 128
 TOK = 512
 BLOCKS = 16
+ROOM = 56 << 20
 ALL = ("z", "x", "y", "c")
 SEQ = ("z", "x")
 EXP = ("y", "c")
@@ -54,27 +56,28 @@
 
 
 def pack_heads_kernel(q, k, v, o):
-    for i, ref in enumerate((q, k, v)):
-        o[0, i] = ref[...]
+    for h in range(4):
+        for i, ref in enumerate((q, k, v)):
+            o[h, i] = ref[:, h * HD : (h + 1) * HD]
 
 
 def pack_heads(queries, keys, values):
-    column = pl.BlockSpec((TOK, HD), lambda h: (0, h))
     return pl.pallas_call(
         pack_heads_kernel,
-        grid=(4,),
-        in_specs=[column] * 3,
-        out_specs=pl.BlockSpec((1, 3, TOK, HD), lambda h: (h, 0, 0, 0)),
         out_shape=jax.ShapeDtypeStruct((4, 3, TOK, HD), jnp.bfloat16),
+        compiler_params=pltpu.CompilerParams(vmem_limit_bytes=ROOM),
         name="pack_heads",
     )(queries, keys, values)
 
 
-def pack_parts_kernel(got, q, o):
-    for i in range(4):
-        o[0, i, 0:TOK] = got[i, 1]
-        o[0, i, TOK : 2 * TOK] = got[i, 2]
-        o[0, i, 2 * TOK :] = q[i, 0]
+def pack_parts_kernel(got, q, one, two):
+    for i in range(2):
+        one[0, i, 0:TOK] = got[i, 1]
+        one[0, i, TOK : 2 * TOK] = got[i, 2]
+        one[0, i, 2 * TOK : 2 * TOK + 128] = q[i, 0]
+        one[0, i, 2 * TOK + 128 :] = q[i + 2, 0]
+        two[0, i, 0:TOK] = got[i + 2, 1]
+        two[0, i, TOK:] = got[i + 2, 2]
 
 
 def pack_parts(got):
@@ -85,46 +88,66 @@
             pl.BlockSpec((4, 3, TOK, HD), lambda p: (0, 0, 0, 0)),
             pl.BlockSpec((4, 1, 128, HD), lambda p: (0, 0, p, 0)),
         ],
-        out_specs=pl.BlockSpec((1, 4, 1152, HD), lambda p: (p, 0, 0, 0)),
-        out_shape=jax.ShapeDtypeStruct((4, 4, 1152, HD), jnp.bfloat16),
-        compiler_params=pltpu.CompilerParams(vmem_limit_bytes=16 << 20),
+        out_specs=[
+            pl.BlockSpec((1, 2, 1280, HD), lambda p: (p, 0, 0, 0)),
+            pl.BlockSpec((1, 2, 1024, HD), lambda p: (p, 0, 0, 0)),
+        ],
+        out_shape=[
+            jax.ShapeDtypeStruct((4, 2, 1280, HD), jnp.bfloat16),
+            jax.ShapeDtypeStruct((4, 2, 1024, HD), jnp.bfloat16),
+        ],
+        compiler_params=pltpu.CompilerParams(vmem_limit_bytes=20 << 20),
         name="pack_parts",
     )(got, got)
 
 
 QW = 512
 TILE = QW // 128
-
-
-def attend_kernel(tab, r, o, vt, s0, s1, acc, m, l, qt):
-    bound = tab[32]
-    sub = tab[33]
+TILES = BLOCKS // TILE
+
+
+def attend_kernel(tab, r, *refs, part):
+    if part == 0:
+        mo, lo_, acco, qto, vt, s0, s1, acc, m, l = refs
+    else:
+        mi, li, acci, qti, o, vt, s0, s1, acc, m, l = refs
+    bound, sub, core = tab[48], tab[49], tab[50]
+    start = jnp.where(core == 0, 4 * part, part)
 
     def turn(t, carry):
         vt[t] = r[t, TOK : 2 * TOK, :].T
         return carry
 
-    lax.fori_loop(0, BLOCKS, turn, 0)
+    lax.fori_loop(0, 8, turn, 0)
     col = lax.broadcasted_iota(jnp.int32, (1, QW), 1)
     row = lax.broadcasted_iota(jnp.int32, (TOK, 1), 0)
 
-    def score(t):
-        return jnp.dot(r[tab[t], 0:TOK, :], qt[...], preferred_element_type=jnp.float32)
-
     def tile(index, carry):
         j = TILE * index
-        for i in range(TILE):
-            qt[:, i * 128 : (i + 1) * 128] = r[tab[j + i], 2 * TOK :, :].T
+        if part == 0:
+            qt = qto.at[index]
+            for i in range(TILE):
+                here = r[tab[j + i], pl.ds(2 * TOK + 128 * tab[32 + j + i], 128), :]
+                qt[:, i * 128 : (i + 1) * 128] = here.T
+            m[...] = jnp.full((1, QW), NEG, jnp.float32)
+            l[...] = jnp.zeros((1, QW), jnp.float32)
+            acc[...] = jnp.zeros((HD, QW), jnp.float32)
+        else:
+            qt = qti.at[index]
+            m[...] = mi[index]
+            l[...] = li[index]
+            acc[...] = acci[index]
         first = j * TOK + sub * 128
         last = first + (TILE - 1) * TOK + 127
         qpos = first + (col // 128) * TOK + col % 128
         qlow = jnp.where(qpos >= bound, bound, 0)
         lo = jnp.where(first >= bound, bound // (2 * TOK), 0)
         hi = (j + TILE) // 2
-        m[...] = jnp.full((1, QW), NEG, jnp.float32)
-        l[...] = jnp.zeros((1, QW), jnp.float32)
-        acc[...] = jnp.zeros((HD, QW), jnp.float32)
-        s0[...] = score(2 * lo)
+        lo = (jnp.maximum(lo - start, 0) + core) >> core
+        hi = jnp.minimum((jnp.maximum(hi - start, 0) + core) >> core, 4)
+
+        def score(t):
+            return jnp.dot(r[tab[t], 0:TOK, :], qt[...], preferred_element_type=jnp.float32)
 
         def soft(s, t, masked):
             here = s[...]
@@ -141,13 +164,18 @@
                 vt[tab[t]], p.astype(jnp.bfloat16), preferred_element_type=jnp.float32
             )
 
-        def step(u, inner):
-            t = 2 * u
+        def first_of(i):
+            return 2 * (start + (i << core))
+
+        s0[...] = score(first_of(jnp.minimum(lo, 3)))
+
+        def step(i, inner):
+            t = first_of(i)
 
             def go(masked):
                 s1[...] = score(t + 1)
                 soft(s0, t, masked)
-                s0[...] = score(jnp.minimum(t + 2, j + TILE - 1))
+                s0[...] = score(first_of(jnp.minimum(i + 1, 3)))
                 soft(s1, t + 1, masked)
 
             need = ((t + 2) * TOK - 1 > first) | ((t * TOK < bound) & (last >= bound))
@@ -156,83 +184,152 @@
             return inner
 
         lax.fori_loop(lo, hi, step, 0)
-        out = (acc[...] / l[...]).T.astype(jnp.bfloat16)
-        for i in range(TILE):
-            o[tab[16 + j + i]] = out[i * 128 : (i + 1) * 128]
+        if part == 0:
+            mo[index] = m[...]
+            lo_[index] = l[...]
+            acco[index] = acc[...]
+        else:
+            out = (acc[...] / l[...]).T.astype(jnp.bfloat16)
+            for i in range(TILE):
+                o[tab[16 + j + i]] = out[i * 128 : (i + 1) * 128]
         return carry
 
-    lax.fori_loop(0, BLOCKS // TILE, tile, 0)
-
-
-def attend(tab, received):
+    lax.fori_loop(0, TILES, tile, 0)
+
+
+def attend(part, tab, received, *state):
+    vmem = pl.BlockSpec(memory_space=pltpu.VMEM)
+    if part == 0:
+        out_shape = [
+            jax.ShapeDtypeStruct((TILES, 1, QW), jnp.float32),
+            jax.ShapeDtypeStruct((TILES, 1, QW), jnp.float32),
+            jax.ShapeDtypeStruct((TILES, HD, QW), jnp.float32),
+            jax.ShapeDtypeStruct((TILES, HD, QW), jnp.bfloat16),
+        ]
+    else:
+        out_shape = jax.ShapeDtypeStruct((BLOCKS, 128, HD), jnp.bfloat16)
     return pl.pallas_call(
-        attend_kernel,
-        out_shape=jax.ShapeDtypeStruct((BLOCKS, 128, HD), jnp.bfloat16),
-        in_specs=[
-            pl.BlockSpec(memory_space=pltpu.SMEM),
-            pl.BlockSpec(memory_space=pltpu.VMEM),
-        ],
-        out_specs=pl.BlockSpec(memory_space=pltpu.VMEM),
+        functools.partial(attend_kernel, part=part),
+        out_shape=out_shape,
+        in_specs=[pl.BlockSpec(memory_space=pltpu.SMEM), vmem] + [vmem] * len(state),
+        out_specs=[vmem] * 4 if part == 0 else vmem,
         scratch_shapes=[
-            pltpu.VMEM((BLOCKS, HD, TOK), jnp.bfloat16),
+            pltpu.VMEM((8, HD, TOK), jnp.bfloat16),
             pltpu.VMEM((TOK, QW), jnp.float32),
             pltpu.VMEM((TOK, QW), jnp.float32),
             pltpu.VMEM((HD, QW), jnp.float32),
             pltpu.VMEM((1, QW), jnp.float32),
             pltpu.VMEM((1, QW), jnp.float32),
-            pltpu.VMEM((HD, QW), jnp.bfloat16),
-        ],
-        compiler_params=pltpu.CompilerParams(vmem_limit_bytes=32 << 20),
+        ],
+        compiler_params=pltpu.CompilerParams(vmem_limit_bytes=24 << 20),
         cost_estimate=pl.CostEstimate(
-            flops=10_000_000_000, bytes_accessed=5_000_000, transcendentals=8_000_000
+            flops=6_000_000_000, bytes_accessed=4_000_000, transcendentals=4_000_000
         ),
         name="attend",
-    )(tab, received)
-
-
-def project_kernel(order, mine, theirs, w, base, o, acc):
-    k = pl.program_id(0)
-
-    @pl.when(k == 0)
-    def _():
-        acc[...] = base[...].astype(jnp.float32)
-
-    @pl.when(k < 4)
-    def _():
-        acc[...] += jnp.dot(mine[0], w[...], preferred_element_type=jnp.float32)
-
-    @pl.when(k >= 4)
-    def _():
-        acc[...] += jnp.dot(theirs[0], w[...], preferred_element_type=jnp.float32)
-
-    @pl.when(k == 7)
-    def _():
-        o[...] = acc[...].astype(jnp.bfloat16)
+    )(tab, received, *state)
+
+
+def project_kernel(order, mine, theirs, w, base, o, xs, ws, acc, sem):
+    copies = []
+    for k in range(8):
+        part = (mine if k < 4 else theirs).at[k % 4, pl.ds(0, xs.shape[1])]
+        rows = pl.ds(pl.multiple_of(order[k] * 512, 512), 512)
+        copies.append(
+            (
+                pltpu.make_async_copy(part, xs.at[k], sem.at[0, k]),
+                pltpu.make_async_copy(w.at[rows], ws.at[k], sem.at[1, k]),
+            )
+        )
+        for copy in copies[-1]:
+            copy.start()
+    for k in range(8):
+        for copy in copies[k]:
+            copy.wait()
+        term = jnp.dot(xs[k], ws[k], preferred_element_type=jnp.float32)
+        if k == 0:
+            acc[...] = base[...].astype(jnp.float32) + term
+        elif k < 7:
+            acc[...] += term
+        else:
+            o[...] = (acc[...] + term).astype(jnp.bfloat16)
 
 
 def project(order, mine, theirs, w, base):
     rows = base.shape[0]
+    vmem, anywhere = pl.BlockSpec(memory_space=pltpu.VMEM), pl.BlockSpec(memory_space=pl.ANY)
     return pl.pallas_call(
         project_kernel,
-        grid_spec=pltpu.PrefetchScalarGridSpec(
-            num_scalar_prefetch=1,
-            grid=(8,),
-            in_specs=[
-                pl.BlockSpec((1, rows, 512), lambda k, order: (jnp.minimum(k, 3), 0, 0)),
-                pl.BlockSpec((1, rows, 512), lambda k, order: (jnp.maximum(k - 4, 0), 0, 0)),
-                pl.BlockSpec((512, 1024), lambda k, order: (order[k], 0)),
-                pl.BlockSpec((rows, 1024), lambda k, order: (0, 0)),
-            ],
-            out_specs=pl.BlockSpec((rows, 1024), lambda k, order: (0, 0)),
-            scratch_shapes=[pltpu.VMEM((rows, 1024), jnp.float32)],
-        ),
+        in_specs=[pl.BlockSpec(memory_space=pltpu.SMEM), anywhere, anywhere, anywhere, vmem],
+        out_specs=vmem,
         out_shape=jax.ShapeDtypeStruct((rows, 1024), jnp.bfloat16),
-        compiler_params=pltpu.CompilerParams(vmem_limit_bytes=24 << 20),
+        scratch_shapes=[
+            pltpu.VMEM((8, rows, 512), jnp.bfloat16),
+            pltpu.VMEM((8, 512, 1024), jnp.bfloat16),
+            pltpu.VMEM((rows, 1024), jnp.float32),
+            pltpu.SemaphoreType.DMA((2, 8)),
+        ],
+        compiler_params=pltpu.CompilerParams(vmem_limit_bytes=ROOM),
         cost_estimate=pl.CostEstimate(
             flops=rows * 8_388_608, bytes_accessed=8_388_608 + rows * 12_288, transcendentals=0
         ),
         name="project",
     )(order, mine, theirs, w, base)
+
+
+def experts_kernel(piece, gate, up, down, o, ps, gs, us, ds, sem):
+    wide = D // 4
+    copies = []
+    for k in range(4):
+        span = pl.ds(k * wide, wide)
+        copies.append(
+            (
+                pltpu.make_async_copy(piece.at[:, span], ps.at[k], sem.at[0, k]),
+                pltpu.make_async_copy(gate.at[0, span], gs.at[k], sem.at[1, k]),
+                pltpu.make_async_copy(up.at[0, span], us.at[k], sem.at[2, k]),
+            )
+        )
+    last = [
+        pltpu.make_async_copy(down.at[0, :, pl.ds(k * wide, wide)], ds.at[k], sem.at[3, k])
+        for k in range(4)
+    ]
+    for group in (*copies, last):
+        for copy in group:
+            copy.start()
+    g = u = None
+    for k in range(4):
+        for copy in copies[k]:
+            copy.wait()
+        add_g = jnp.dot(ps[k], gs[k], preferred_element_type=jnp.float32)
+        add_u = jnp.dot(ps[k], us[k], preferred_element_type=jnp.float32)
+        g, u = (add_g, add_u) if k == 0 else (g + add_g, u + add_u)
+    inner = (jax.nn.silu(g) * u).astype(jnp.bfloat16)
+    for k in range(4):
+        last[k].wait()
+        o[:, k * wide : (k + 1) * wide] = jnp.dot(
+            inner, ds[k], preferred_element_type=jnp.float32
+        ).astype(o.dtype)
+
+
+def experts(piece, w_gate, w_up, w_down):
+    anywhere = pl.BlockSpec(memory_space=pl.ANY)
+    return pl.pallas_call(
+        experts_kernel,
+        in_specs=[anywhere] * 4,
+        out_specs=pl.BlockSpec(memory_space=pltpu.VMEM),
+        out_shape=jax.ShapeDtypeStruct((128, D), jnp.bfloat16),
+        scratch_shapes=[
+            pltpu.VMEM((4, 128, D // 4), jnp.bfloat16),
+            pltpu.VMEM((4, D // 4, 256), jnp.bfloat16),
+            pltpu.VMEM((4, D // 4, 256), jnp.bfloat16),
+            pltpu.VMEM((4, 256, D // 4), jnp.bfloat16),
+            pltpu.SemaphoreType.DMA((4, 4)),
+        ],
+        compiler_params=pltpu.CompilerParams(vmem_limit_bytes=ROOM),
+        cost_estimate=pl.CostEstimate(
+            flops=1_610_000_000, bytes_accessed=16_800_000, transcendentals=32_768
+        ),
+        name="experts",
+    )(piece, w_gate, w_up, w_down)
 
 
 def swap(array):
@@ -273,19 +370,27 @@
     b = jnp.where(c == 0, x, z)
 
     got = exchange(pack_heads(queries, keys, values), GROUP_A)
-    received = exchange(pack_parts(got), GROUP_B).reshape(BLOCKS, 1152, HD)
+    one, two = pack_parts(got)
+    one = exchange(one, GROUP_B).reshape(8, 1280, HD)
+    one, two = lax.optimization_barrier((one, two))
+    two = exchange(two, GROUP_B).reshape(8, 1024, HD)
 
     index = jnp.arange(BLOCKS, dtype=jnp.int32)
-    swapped = (index % 4) * 4 + index // 4
+    low, high = index % 4, index // 4
+    from_a = jnp.where(c == 0, high, low)
+    from_b = jnp.where(c == 0, low, high)
     bound = documents.shape[0] - jnp.sum(documents)
     tab = jnp.concatenate(
         [
-            jnp.where(c == 0, swapped, index),
-            jnp.where(c == 0, index, swapped),
-            jnp.stack([bound, b]).astype(jnp.int32),
+            from_b * 2 + from_a % 2,
+            from_a * 4 + from_b,
+            from_a // 2,
+            jnp.stack([bound, b, c]).astype(jnp.int32),
         ]
     ).astype(jnp.int32)
-    attended = exchange(attend(tab, received), GROUP_AB)
+    state = attend(0, tab, one)
+    attended = attend(1, tab, two, *state)
+    attended = exchange(attended, GROUP_AB)
     attended = attended.reshape(4, TOK, HD).transpose(1, 0, 2).reshape(TOK, 4 * HD)
 
     ranked = picks.reshape(8, 8, 16)
@@ -333,11 +438,8 @@
     near = spread(chosen, GROUP_A)
     far = spread(near.reshape(32, D), GROUP_B)
     piece = far.reshape(128, D)
-    gate_part = jnp.dot(piece, w_gate[0], preferred_element_type=jnp.float32)
-    up_part = jnp.dot(piece, w_up[0], preferred_element_type=jnp.float32)
-    inner_act = (jax.nn.silu(gate_part) * up_part).astype(jnp.bfloat16)
-    partial = jnp.dot(inner_act, w_down[0], preferred_element_type=jnp.float32)
-    partial = exchange(partial.astype(jnp.bfloat16).reshape(4, 32, D), GROUP_B)
+    partial = experts(piece, w_gate, w_up, w_down)
+    partial = exchange(partial.reshape(4, 32, D), GROUP_B)
     partial = jnp.sum(partial.astype(jnp.float32), axis=0).astype(jnp.bfloat16)
     partial = exchange(partial.reshape(4, 8, D), GROUP_A)
     summed = jnp.sum(partial.astype(jnp.float32), axis=0)

time: 241 us -> 232 us (0.963)
  blocking collectives: 27.1 us -> 50.1 us
  waiting for transfers between devices: 84.3 us -> 61.6 us
  Pallas kernels: 36.3 us -> 47.4 us
  matrix products: 12.2 us -> 2.79 us
  local copies, waits for them, and re-layouts: 18.4 us -> 13.3 us
  starting transfers between devices: 50.5 us -> 46.4 us
    all_to_all x5, waiting for transfers between devices: 55.6 us -> 31.1 us  [exchange(): lax.all_to_all(array, ALL, 0, 0, tiled=True, axis_index_groups=groups)]
    all_to_all x2 -> x3, blocking collectives: 27.1 us -> 50.1 us  [exchange(): lax.all_to_all(array, ALL, 0, 0, tiled=True, axis_index_groups=groups)]
    pallas_call x4 -> x6, Pallas kernels: 35.9 us -> 47 us  [the longest x2 22.4 us: attend(): pl.pallas_call(functools.partial(attend_kernel, part=part), out_shape=out...]
    dot_general x2 -> x0, matrix products: 10.1 us -> none  [the longest x1 7.17 us: shards(): partial = jnp.dot(inner_act, w_down[0], preferred_element_type=jnp.float32)]
    unnamed x32 -> x34, local copies, waits for them, and re-layouts: 12.5 us -> 6.4 us
    ppermute x2, starting transfers between devices: 7.64 us -> 4.33 us  [swap(): return lax.ppermute(array, 'c', [(0, 1), (1, 0)])]
    all_to_all x1, waiting for transfers between devices: 0.01 us -> 2.51 us  [shards(): returned = lax.all_to_all(back.reshape(128, 8, 128), ALL, 0, 0, tiled=True)]
  transfers between devices with their start and end apart: 14 -> 14, of which waited for: 8 -> 9; matrix products, arithmetic and copies ran while one was open for 10% -> 5% of each run, Pallas kernels for 3% -> 11%
where the time goes in v3:
time: 232 us; the launch traced here: 231 us
  waiting for transfers between devices  61.6 us (27%)
  blocking collectives  50.1 us (22%)
  Pallas kernels  47.4 us (20%)
  starting transfers between devices  46.4 us (20%)
  local copies, waits for them, and re-layouts  13.3 us (6%)
  other arithmetic  8.56 us (4%)
  matrix products  2.79 us (1%)
    all_to_all x3, blocking collectives, exchange(): lax.all_to_all(array, ALL, 0, 0, tiled=True, axis_index_groups=groups)  50.1 us
    all_to_all x5, waiting for transfers between devices, exchange(): lax.all_to_all(array, ALL, 0, 0, tiled=True, axis_index_groups=groups)  31.1 us
    pallas_call x2, Pallas kernels, attend(): pl.pallas_call(functools.partial(attend_kernel, part=part), out_shape=out...  22.4 us
    all_to_all x5, starting transfers between devices, exchange(): lax.all_to_all(array, ALL, 0, 0, tiled=True, axis_index_groups=groups)  21.6 us
    pallas_call x2, Pallas kernels, project(): pl.pallas_call(project_kernel, in_specs=[pl.BlockSpec(memory_space=pltpu....  14.6 us
    all_to_all x1, waiting for transfers between devices, shards(): arrived = lax.all_to_all(rows.reshape(128, 8, 128), ALL, 0, 0, tiled=True)  10.9 us
    ppermute x4, waiting for transfers between devices, ring(): return lax.ppermute(array, 'y', [(i, (i + step) % 4) for i in range(4)])  10.2 us
    pallas_call x1, Pallas kernels, experts(): pl.pallas_call(experts_kernel, in_specs=[anywhere] * 4, out_specs=pl.Bloc...  7.17 us
  transfers between devices with their start and end apart: 14, of which 9 were waited for; matrix products, arithmetic and copies ran while one was open for 5% of the time, Pallas kernels for 11%

profile of v3, /device:TPU:1, one launch (start us, length us, event | category | flops | bytes accessed | tf_op | source)
XLA Modules:
  0.0 231.1 jit_solution(6893962789630966960)
XLA Ops:
  0.0 2.8 %pack_heads.1 = bf16[4,3,512,128]{3,2,1,0:T(8,128)(2,1)} custom-call(bf16[512,512]{1,0:T(8,128)(2,1)} %q.1, bf16[512,512]{1,0:T(8,128)(2,1)} %k.1, bf16[512,512]{1,0:T(8,128)(2,1)} %v.1), custom_call_target="tpu_custom_call" | custom-call | tf_op jit(solution)/shard_map/pack_heads/pallas_call | solution.py:65
  2.8 17.7 %all_to_all.55.got.q = bf16[4,3,512,128]{3,2,1,0:T(8,128)(2,1)S(1)} all-to-all(bf16[4,3,512,128]{3,2,1,0:T(8,128)(2,1)} %pack_heads.1), channel_id=1, replica_groups={{0,32,64,96},{1,9,17,25},{8,40,72,104},{33,41,49,57},{16,48,80,112},{65..., dimensions={0} | all-to-all | bytes 3145728 | tf_op jit(solution)/shard_map/all_to_all | solution.py:51
  21.0 23.0 %all_to_all.56 = bf16[4,2,1280,128]{3,2,1,0:T(8,128)(2,1)S(1)} all-to-all(bf16[4,2,1280,128]{3,2,1,0:T(8,128)(2,1)S(1)} %get-tuple-element.15), channel_id=1, replica_groups={{0,8,16,24},{1,33,65,97},{32,40,48,56},{9,41,73,105},{64,72,80,88},{17,..., dimensions={0} | all-to-all | bytes 5242880 | tf_op jit(solution)/shard_map/all_to_all | solution.py:51
  44.0 4.6 %all-to-all-start.2 = ((bf16[4,2,1024,128]{3,2,1,0:T(8,128)(2,1)}), bf16[4,2,1024,128]{3,2,1,0:T(8,128)(2,1)}, u32[]{:S(2)}, u32[]{:S(2)}) async-start(bf16[4,2,1024,128]{3,2,1,0:T(8,128)(2,1)} %copy-done.1), calls=%async_computation.2 | async-start | bytes 4194304 | tf_op jit(solution)/shard_map/all_to_all | solution.py:51
  48.6 0.6 reduce_sum.48
  50.1 9.1 %attend.2 = (f32[4,1,512]{2,1,0:T(1,128)S(1)}, f32[4,1,512]{2,1,0:T(1,128)S(1)}, f32[4,128,512]{2,1,0:T(8,128)S(1)}, bf16[4,128,512]{2,1,0:T(8,128)(2,1)S(1)}) custom-call(s32[51]{0:T(128)S(1)} %concatenate.17.tab, bf16[8,1280,128]{2,1,0:T(8,128)(2,1)S(1)} %bitcast.71), custom_call_target="tpu_custom_call" | custom-call | flops 6000000000 | bytes 4000000 | tf_op jit(solution)/shard_map/attend/pallas_call | solution.py:211
  59.2 1.0 copy-done.2
  60.2 4.1 %all-to-all-done.2 = bf16[4,2,1024,128]{3,2,1,0:T(8,128)(2,1)} async-done(((bf16[4,2,1024,128]{3,2,1,0:T(8,128)(2,1)}), bf16[4,2,1024,128]{3,2,1,0:T(8,128)(2,1)}, u32[]{:S(2)}, u32[]{:S(2)}) %all-to-all-start.2) | async-done | bytes 2097184 | tf_op jit(solution)/shard_map/all_to_all | solution.py:51
  64.3 1.2 copy-done.3
  65.5 13.3 %attend.3 = bf16[16,128,128]{2,1,0:T(8,128)(2,1)} custom-call(s32[51]{0:T(128)S(1)} %concatenate.17.tab, bf16[8,1024,128]{2,1,0:T(8,128)(2,1)} %bitcast.4.r, f32[4,1,512]{2,1,0:T(1,128)S(1)} %get-tuple-element.19.refs_0_, f32[4,1,512]{2,1,0:T(1,128)S(1)} %get-tuple-element.20.refs_1_, f32[4,128,512]{2,1,0:T(8,128)S(1)} %copy-done.3, ...), custom_call_target="tpu_custom_call" | custom-call | flops 6000000000 | bytes 4000000 | tf_op jit(solution)/shard_map/attend/pallas_call | solution.py:211
  78.8 3.6 %all-to-all-start.3 = ((bf16[16,128,128]{2,1,0:T(8,128)(2,1)}), bf16[16,128,128]{2,1,0:T(8,128)(2,1)S(1)}, u32[]{:S(2)}, u32[]{:S(2)}) async-start(bf16[16,128,128]{2,1,0:T(8,128)(2,1)} %attend.3), calls=%async_computation.3 | async-start | bytes 1048576 | tf_op jit(solution)/shard_map/all_to_all | solution.py:51
  82.9 9.5 %all-to-all-done.3 = bf16[16,128,128]{2,1,0:T(8,128)(2,1)S(1)} async-done(((bf16[16,128,128]{2,1,0:T(8,128)(2,1)}), bf16[16,128,128]{2,1,0:T(8,128)(2,1)S(1)}, u32[]{:S(2)}, u32[]{:S(2)}) %all-to-all-start.3) | async-done | bytes 524320 | tf_op jit(solution)/shard_map/all_to_all | solution.py:51
  93.1 0.9 broadcast_in_dim.10
  94.0 4.2 %all-to-all-start.4 = ((bf16[4,144,512]{2,1,0:T(8,128)(2,1)}), bf16[4,144,512]{2,1,0:T(8,128)(2,1)S(1)}, u32[]{:S(2)}, u32[]{:S(2)}) async-start(bf16[4,144,512]{2,1,0:T(8,128)(2,1)} %broadcast_in_dim.10), calls=%async_computation.4 | async-start | bytes 1179648 | tf_op jit(solution)/shard_map/all_to_all | solution.py:406
  98.3 0.6 pad_add_fusion.1.order
  98.9 6.6 %all-to-all-done.4.mine = bf16[4,144,512]{2,1,0:T(8,128)(2,1)S(1)} async-done(((bf16[4,144,512]{2,1,0:T(8,128)(2,1)}), bf16[4,144,512]{2,1,0:T(8,128)(2,1)S(1)}, u32[]{:S(2)}, u32[]{:S(2)}) %all-to-all-start.4) | async-done | bytes 589856 | tf_op jit(solution)/shard_map/all_to_all | solution.py:406
  105.5 3.8 %collective-permute-start = (bf16[4,144,512]{2,1,0:T(8,128)(2,1)S(1)}, bf16[4,144,512]{2,1,0:T(8,128)(2,1)S(1)}, u32[]{:S(2)}, u32[]{:S(2)}) collective-permute-start(bf16[4,144,512]{2,1,0:T(8,128)(2,1)S(1)} %all-to-all-done.4.mine), channel_id=1, source_target_pairs={{0,1},{1,0},{2,3},{3,2},{4,5},{5,4},{6,7},{7,6},{8,9},{9,8},{10,11... | collective-permute-start | bytes 1769480 | tf_op jit(solution)/shard_map/ppermute | solution.py:336
  109.3 1.1 convolution_convert_fusion.1.base
  110.9 0.9 copy-done.9
  111.8 5.9 %project.2 = bf16[128,1024]{1,0:T(8,128)(2,1)} custom-call(s32[8]{0:T(128)} %pad_add_fusion.1.order, bf16[4,144,512]{2,1,0:T(8,128)(2,1)} %copy-done.5, bf16[4,144,512]{2,1,0:T(8,128)(2,1)} %copy-done.9, bf16[4096,1024]{1,0:T(8,128)(2,1)} %w.3, bf16[128,1024]{1,0:T(8,128)(2,1)} %convolution_convert_fusion.1.base), custom_call_target="tpu_custom_call" | custom-call | flops 1073741824 | bytes 9961472 | tf_op jit(solution)/shard_map/project/pallas_call | solution.py:260
  117.7 0.8 slice.39
  118.6 1.7 copy.36
  120.3 4.1 %all-to-all-start.5 = ((bf16[128,8,128]{2,1,0:T(8,128)(2,1)}), bf16[128,8,128]{2,1,0:T(8,128)(2,1)S(1)}, u32[]{:S(2)}, u32[]{:S(2)}) async-start(bf16[128,8,128]{2,1,0:T(8,128)(2,1)} %bitcast.29), calls=%async_computation.5 | async-start | bytes 524288 | tf_op jit(solution)/shard_map/all_to_all | solution.py:419
  124.6 10.9 %all-to-all-done.5 = bf16[128,8,128]{2,1,0:T(8,128)(2,1)S(1)} async-done(((bf16[128,8,128]{2,1,0:T(8,128)(2,1)}), bf16[128,8,128]{2,1,0:T(8,128)(2,1)S(1)}, u32[]{:S(2)}, u32[]{:S(2)}) %all-to-all-start.5) | async-done | bytes 262176 | tf_op jit(solution)/shard_map/all_to_all | solution.py:419
  136.1 9.4 %all_to_all.57 = bf16[4,8,8192]{2,1,0:T(8,128)(2,1)S(1)} all-to-all(bf16[4,8,8192]{2,1,0:T(8,128)(2,1)S(1)} %broadcast_in_dim.11), channel_id=1, replica_groups={{0,32,64,96},{1,9,17,25},{8,40,72,104},{33,41,49,57},{16,48,80,112},{65..., dimensions={0} | all-to-all | bytes 1048576 | tf_op jit(solution)/shard_map/all_to_all | solution.py:51
  145.5 1.5 broadcast_in_dim.13
  147.0 3.6 %all-to-all-start.7 = ((bf16[4,32,8192]{2,1,0:T(8,128)(2,1)}), bf16[4,32,8192]{2,1,0:T(8,128)(2,1)S(1)}, u32[]{:S(2)}, u32[]{:S(2)}) async-start(bf16[4,32,8192]{2,1,0:T(8,128)(2,1)} %broadcast_in_dim.13), calls=%async_computation.7 | async-start | bytes 4194304 | tf_op jit(solution)/shard_map/all_to_all | solution.py:51
  151.0 2.4 %collective-permute-start.2 = (bf16[512,512]{1,0:T(8,128)(2,1)S(1)}, bf16[512,512]{1,0:T(8,128)(2,1)S(1)}, u32[]{:S(2)}, u32[]{:S(2)}) collective-permute-start(bf16[512,512]{1,0:T(8,128)(2,1)S(1)} %bitcast.79), channel_id=1, source_target_pairs={{0,6},{2,0},{4,2},{6,4},{1,7},{3,1},{5,3},{7,5},{8,14},{10,8},{12,... | collective-permute-start | bytes 1572872 | tf_op jit(solution)/shard_map/ppermute | solution.py:340
  153.4 10.2 %collective-permute-done.1 = bf16[512,512]{1,0:T(8,128)(2,1)S(1)} collective-permute-done((bf16[512,512]{1,0:T(8,128)(2,1)S(1)}, bf16[512,512]{1,0:T(8,128)(2,1)S(1)}, u32[]{:S(2)}, u32[]{:S(2)}) %collective-permute-start.1) | collective-permute-done | bytes 524320 | tf_op jit(solution)/shard_map/ppermute | solution.py:340
  163.6 0.7 slice.36
  164.3 0.8 slice.37
  165.2 2.7 %collective-permute-start.4 = (bf16[256,512]{1,0:T(8,128)(2,1)}, bf16[256,512]{1,0:T(8,128)(2,1)}, u32[]{:S(2)}, u32[]{:S(2)}) collective-permute-start(bf16[256,512]{1,0:T(8,128)(2,1)} %slice.37), channel_id=1, source_target_pairs={{0,6},{2,0},{4,2},{6,4},{1,7},{3,1},{5,3},{7,5},{8,14},{10,8},{12,... | collective-permute-start | bytes 786440 | tf_op jit(solution)/shard_map/ppermute | solution.py:340
  167.8 1.3 copy-done.4
  169.1 7.2 %experts.1 = bf16[128,8192]{1,0:T(8,128)(2,1)} custom-call(bf16[128,8192]{1,0:T(8,128)(2,1)} %bitcast.72, bf16[1,8192,256]{2,1,0:T(8,128)(2,1)} %gate.1, bf16[1,8192,256]{2,1,0:T(8,128)(2,1)} %up.1, bf16[1,256,8192]{2,1,0:T(8,128)(2,1)} %down.1), custom_call_target="tpu_custom_call" | custom-call | flops 1610000000 | bytes 16800000 | tf_op jit(solution)/shard_map/experts/pallas_call | solution.py:315
  176.3 6.4 %all-to-all-start.8 = ((bf16[4,32,8192]{2,1,0:T(8,128)(2,1)}), bf16[4,32,8192]{2,1,0:T(8,128)(2,1)S(1)}, u32[]{:S(2)}, u32[]{:S(2)}) async-start(bf16[4,32,8192]{2,1,0:T(8,128)(2,1)} %bitcast.73), calls=%async_computation.8 | async-start | bytes 4194304 | tf_op jit(solution)/shard_map/all_to_all | solution.py:51
  182.7 1.1 maximum_bitcast_fusion
  183.8 2.6 %pad_maximum_fusion.mine = bf16[4,512,512]{2,1,0:T(8,128)(2,1)} fusion(bf16[1,512,512]{2,1,0:T(8,128)(2,1)S(1)} %maximum_bitcast_fusion, bf16[1,512,512]{2,1,0:T(8,128)(2,1)} %bitcast.82, bf16[1,512,512]{2,1,0:T(8,128)(2,1)S(1)} %bitcast.81, bf16[1,512,512]{2,1,0:T(8,128)(2,1)S(1)} %bitcast.80), kind=kLoop, calls=%fused_computation.1 | loop fusion | flops 3145728 | bytes 4194304 | tf_op jit(solution)/shard_map/stack | solution.py:424
  187.0 11.4 %all-to-all-done.8 = bf16[4,32,8192]{2,1,0:T(8,128)(2,1)S(1)} async-done(((bf16[4,32,8192]{2,1,0:T(8,128)(2,1)}), bf16[4,32,8192]{2,1,0:T(8,128)(2,1)S(1)}, u32[]{:S(2)}, u32[]{:S(2)}) %all-to-all-start.8) | async-done | bytes 2097184 | tf_op jit(solution)/shard_map/all_to_all | solution.py:51
  198.4 1.3 reduce_sum.51
  199.6 3.5 %all-to-all-start.9 = ((bf16[4,8,8192]{2,1,0:T(8,128)(2,1)}), bf16[4,8,8192]{2,1,0:T(8,128)(2,1)S(1)}, u32[]{:S(2)}, u32[]{:S(2)}) async-start(bf16[4,8,8192]{2,1,0:T(8,128)(2,1)} %bitcast.24), calls=%async_computation.9 | async-start | bytes 1048576 | tf_op jit(solution)/shard_map/all_to_all | solution.py:51
  203.1 0.6 pad_add_fusion.order
  203.9 6.1 %all-to-all-done.9 = bf16[4,8,8192]{2,1,0:T(8,128)(2,1)S(1)} async-done(((bf16[4,8,8192]{2,1,0:T(8,128)(2,1)}), bf16[4,8,8192]{2,1,0:T(8,128)(2,1)S(1)}, u32[]{:S(2)}, u32[]{:S(2)}) %all-to-all-start.9) | async-done | bytes 524320 | tf_op jit(solution)/shard_map/all_to_all | solution.py:51
  210.4 0.8 reshape.118
  211.3 6.7 %all-to-all-start.10 = ((bf16[128,8,128]{2,1,0:T(8,128)(2,1)}), bf16[128,8,128]{2,1,0:T(8,128)(2,1)S(1)}, u32[]{:S(2)}, u32[]{:S(2)}) async-start(bf16[128,8,128]{2,1,0:T(8,128)(2,1)} %reshape.118), calls=%async_computation.10 | async-start | bytes 524288 | tf_op jit(solution)/shard_map/all_to_all | solution.py:450
  218.0 8.7 %project.3 = bf16[512,1024]{1,0:T(8,128)(2,1)} custom-call(s32[8]{0:T(128)} %pad_add_fusion.order, bf16[4,512,512]{2,1,0:T(8,128)(2,1)} %pad_maximum_fusion.mine, bf16[4,512,512]{2,1,0:T(8,128)(2,1)} %collective-permute-done.5.theirs, bf16[4096,1024]{1,0:T(8,128)(2,1)} %w.3, bf16[512,1024]{1,0:T(8,128)(2,1)} %base.1), custom_call_target="tpu_custom_call" | custom-call | flops 4294967296 | bytes 14680064 | tf_op jit(solution)/shard_map/project/pallas_call | solution.py:260
  226.7 2.5 %all-to-all-done.10 = bf16[128,8,128]{2,1,0:T(8,128)(2,1)S(1)} async-done(((bf16[128,8,128]{2,1,0:T(8,128)(2,1)}), bf16[128,8,128]{2,1,0:T(8,128)(2,1)S(1)}, u32[]{:S(2)}, u32[]{:S(2)}) %all-to-all-start.10) | async-done | bytes 262176 | tf_op jit(solution)/shard_map/all_to_all | solution.py:450
  229.2 0.6 fusion.5
  229.8 1.4 add_convert_fusion
  (77 shorter events, 5.0 us)
Async XLA Ops:
  0.0 203.7 %copy-start = (bf16[8192,1]{0,1:T(2,128)(2,1)S(1)}, bf16[8192,1]{0,1:T(2,128)(2,1)}, u32[]{:S(2)}) copy-start(bf16[8192,1]{0,1:T(2,128)(2,1)} %param.22) | copy-start | bytes 49156
  21.0 23.0 %copy-start.1 = (bf16[4,2,1024,128]{3,2,1,0:T(8,128)(2,1)}, bf16[4,2,1024,128]{3,2,1,0:T(8,128)(2,1)S(1)}, u32[]{:S(2)}) copy-start(bf16[4,2,1024,128]{3,2,1,0:T(8,128)(2,1)S(1)} %get-tuple-element.17) | copy-start | bytes 6291460
  44.0 4.6 %copy-start.10 = (s32[8192]{0:T(1024)S(1)}, s32[8192]{0:T(1024)}, u32[]{:S(2)}) copy-start(s32[8192]{0:T(1024)} %param.18) | copy-start | bytes 98308
  44.0 5.3 %copy-start.12 = (s32[8,128]{1,0:T(8,128)S(1)}, s32[8,128]{1,0:T(8,128)}, u32[]{:S(2)}) copy-start(s32[8,128]{1,0:T(8,128)} %param.21) | copy-start | bytes 12292
  44.0 20.3 %all-to-all-start.2 = ((bf16[4,2,1024,128]{3,2,1,0:T(8,128)(2,1)}), bf16[4,2,1024,128]{3,2,1,0:T(8,128)(2,1)}, u32[]{:S(2)}, u32[]{:S(2)}) async-start(bf16[4,2,1024,128]{3,2,1,0:T(8,128)(2,1)} %copy-done.1), calls=%async_computation.2 | async-start | bytes 4194304 | tf_op jit(solution)/shard_map/all_to_all | solution.py:51
  59.2 1.0 copy-start.2
  64.3 1.2 copy-start.3
  65.5 17.3 %copy-start.11 = (f32[2,1024]{1,0:T(2,128)S(1)}, f32[2,1024]{1,0:T(2,128)}, u32[]{:S(2)}) copy-start(f32[2,1024]{1,0:T(2,128)} %param.20) | copy-start | bytes 24580
  78.8 13.6 %all-to-all-start.3 = ((bf16[16,128,128]{2,1,0:T(8,128)(2,1)}), bf16[16,128,128]{2,1,0:T(8,128)(2,1)S(1)}, u32[]{:S(2)}, u32[]{:S(2)}) async-start(bf16[16,128,128]{2,1,0:T(8,128)(2,1)} %attend.3), calls=%async_computation.3 | async-start | bytes 1048576 | tf_op jit(solution)/shard_map/all_to_all | solution.py:51
  82.9 26.4 %copy-start.7 = (bf16[512,1024]{1,0:T(8,128)(2,1)S(1)}, bf16[512,1024]{1,0:T(8,128)(2,1)}, u32[]{:S(2)}) copy-start(bf16[512,1024]{1,0:T(8,128)(2,1)} %base.1) | copy-start | bytes 3145732
  94.0 11.5 %all-to-all-start.4 = ((bf16[4,144,512]{2,1,0:T(8,128)(2,1)}), bf16[4,144,512]{2,1,0:T(8,128)(2,1)S(1)}, u32[]{:S(2)}, u32[]{:S(2)}) async-start(bf16[4,144,512]{2,1,0:T(8,128)(2,1)} %broadcast_in_dim.10), calls=%async_computation.4 | async-start | bytes 1179648 | tf_op jit(solution)/shard_map/all_to_all | solution.py:406
  105.5 5.5 %copy-start.5 = (bf16[4,144,512]{2,1,0:T(8,128)(2,1)}, bf16[4,144,512]{2,1,0:T(8,128)(2,1)S(1)}, u32[]{:S(2)}) copy-start(bf16[4,144,512]{2,1,0:T(8,128)(2,1)S(1)} %all-to-all-done.4.mine) | copy-start | bytes 1769476
  105.5 5.4 %collective-permute-start = (bf16[4,144,512]{2,1,0:T(8,128)(2,1)S(1)}, bf16[4,144,512]{2,1,0:T(8,128)(2,1)S(1)}, u32[]{:S(2)}, u32[]{:S(2)}) collective-permute-start(bf16[4,144,512]{2,1,0:T(8,128)(2,1)S(1)} %all-to-all-done.4.mine), channel_id=1, source_target_pairs={{0,1},{1,0},{2,3},{3,2},{4,5},{5,4},{6,7},{7,6},{8,9},{9,8},{10,11... | collective-permute-start | bytes 1769480 | tf_op jit(solution)/shard_map/ppermute | solution.py:336
  110.9 0.9 copy-start.9
  120.3 15.2 %all-to-all-start.5 = ((bf16[128,8,128]{2,1,0:T(8,128)(2,1)}), bf16[128,8,128]{2,1,0:T(8,128)(2,1)S(1)}, u32[]{:S(2)}, u32[]{:S(2)}) async-start(bf16[128,8,128]{2,1,0:T(8,128)(2,1)} %bitcast.29), calls=%async_computation.5 | async-start | bytes 524288 | tf_op jit(solution)/shard_map/all_to_all | solution.py:419
  147.0 20.8 %all-to-all-start.7 = ((bf16[4,32,8192]{2,1,0:T(8,128)(2,1)}), bf16[4,32,8192]{2,1,0:T(8,128)(2,1)S(1)}, u32[]{:S(2)}, u32[]{:S(2)}) async-start(bf16[4,32,8192]{2,1,0:T(8,128)(2,1)} %broadcast_in_dim.13), calls=%async_computation.7 | async-start | bytes 4194304 | tf_op jit(solution)/shard_map/all_to_all | solution.py:51
  150.7 12.9 %collective-permute-start.1 = (bf16[512,512]{1,0:T(8,128)(2,1)S(1)}, bf16[512,512]{1,0:T(8,128)(2,1)S(1)}, u32[]{:S(2)}, u32[]{:S(2)}) collective-permute-start(bf16[512,512]{1,0:T(8,128)(2,1)S(1)} %bitcast.78), channel_id=1, source_target_pairs={{0,2},{2,4},{4,6},{6,0},{1,3},{3,5},{5,7},{7,1},{8,10},{10,12},{12... | collective-permute-start | bytes 1572872 | tf_op jit(solution)/shard_map/ppermute | solution.py:340
  151.0 13.3 %collective-permute-start.2 = (bf16[512,512]{1,0:T(8,128)(2,1)S(1)}, bf16[512,512]{1,0:T(8,128)(2,1)S(1)}, u32[]{:S(2)}, u32[]{:S(2)}) collective-permute-start(bf16[512,512]{1,0:T(8,128)(2,1)S(1)} %bitcast.79), channel_id=1, source_target_pairs={{0,6},{2,0},{4,2},{6,4},{1,7},{3,1},{5,3},{7,5},{8,14},{10,8},{12,... | collective-permute-start | bytes 1572872 | tf_op jit(solution)/shard_map/ppermute | solution.py:340
  164.3 18.5 %collective-permute-start.3 = (bf16[256,512]{1,0:T(8,128)(2,1)}, bf16[256,512]{1,0:T(8,128)(2,1)}, u32[]{:S(2)}, u32[]{:S(2)}) collective-permute-start(bf16[256,512]{1,0:T(8,128)(2,1)} %slice.36), channel_id=1, source_target_pairs={{0,2},{2,4},{4,6},{6,0},{1,3},{3,5},{5,7},{7,1},{8,10},{10,12},{12... | collective-permute-start | bytes 786440 | tf_op jit(solution)/shard_map/ppermute | solution.py:340
  164.3 0.9 copy-start.6
  165.2 17.6 %collective-permute-start.4 = (bf16[256,512]{1,0:T(8,128)(2,1)}, bf16[256,512]{1,0:T(8,128)(2,1)}, u32[]{:S(2)}, u32[]{:S(2)}) collective-permute-start(bf16[256,512]{1,0:T(8,128)(2,1)} %slice.37), channel_id=1, source_target_pairs={{0,6},{2,0},{4,2},{6,4},{1,7},{3,1},{5,3},{7,5},{8,14},{10,8},{12,... | collective-permute-start | bytes 786440 | tf_op jit(solution)/shard_map/ppermute | solution.py:340
  167.8 1.3 copy-start.4
  176.3 22.1 %all-to-all-start.8 = ((bf16[4,32,8192]{2,1,0:T(8,128)(2,1)}), bf16[4,32,8192]{2,1,0:T(8,128)(2,1)S(1)}, u32[]{:S(2)}, u32[]{:S(2)}) async-start(bf16[4,32,8192]{2,1,0:T(8,128)(2,1)} %bitcast.73), calls=%async_computation.8 | async-start | bytes 4194304 | tf_op jit(solution)/shard_map/all_to_all | solution.py:51
  183.8 3.1 %copy-start.13 = (s32[4]{0:T(128)S(1)}, s32[4]{0:T(128)}, u32[]{:S(2)}) copy-start(s32[4]{0:T(128)} %constant.145.clone) | copy-start | bytes 52
  186.4 31.5 %collective-permute-start.5 = (bf16[4,512,512]{2,1,0:T(8,128)(2,1)}, bf16[4,512,512]{2,1,0:T(8,128)(2,1)}, u32[]{:S(2)}, u32[]{:S(2)}) collective-permute-start(bf16[4,512,512]{2,1,0:T(8,128)(2,1)} %pad_maximum_fusion.mine), channel_id=1, source_target_pairs={{0,1},{1,0},{2,3},{3,2},{4,5},{5,4},{6,7},{7,6},{8,9},{9,8},{10,11... | collective-permute-start | bytes 6291464 | tf_op jit(solution)/shard_map/ppermute | solution.py:336
  199.6 10.4 %all-to-all-start.9 = ((bf16[4,8,8192]{2,1,0:T(8,128)(2,1)}), bf16[4,8,8192]{2,1,0:T(8,128)(2,1)S(1)}, u32[]{:S(2)}, u32[]{:S(2)}) async-start(bf16[4,8,8192]{2,1,0:T(8,128)(2,1)} %bitcast.24), calls=%async_computation.9 | async-start | bytes 1048576 | tf_op jit(solution)/shard_map/all_to_all | solution.py:51
  211.3 17.9 %all-to-all-start.10 = ((bf16[128,8,128]{2,1,0:T(8,128)(2,1)}), bf16[128,8,128]{2,1,0:T(8,128)(2,1)S(1)}, u32[]{:S(2)}, u32[]{:S(2)}) async-start(bf16[128,8,128]{2,1,0:T(8,128)(2,1)} %reshape.118), calls=%async_computation.10 | async-start | bytes 524288 | tf_op jit(solution)/shard_map/all_to_all | solution.py:450
  226.7 3.1 %copy-start.8 = (bf16[512,1024]{1,0:T(8,128)(2,1)S(1)}, bf16[512,1024]{1,0:T(8,128)(2,1)}, u32[]{:S(2)}) copy-start(bf16[512,1024]{1,0:T(8,128)(2,1)} %project.3) | copy-start | bytes 3145732

commit v4 on v3

--- a/solution.py
+++ b/solution.py
@@ -14,7 +14,7 @@
 HD = 128
 TOK = 512
 BLOCKS = 16
-ROOM = 56 << 20
+ROOM = 50 << 20
 ALL = ("z", "x", "y", "c")
 SEQ = ("z", "x")
 EXP = ("y", "c")
@@ -229,44 +229,38 @@
     )(tab, received, *state)
 
 
-def project_kernel(order, mine, theirs, w, base, o, xs, ws, acc, sem):
+def project_kernel(order, mine, theirs, w, base, o, ws, acc, sem):
     copies = []
     for k in range(8):
-        part = (mine if k < 4 else theirs).at[k % 4, pl.ds(0, xs.shape[1])]
         rows = pl.ds(pl.multiple_of(order[k] * 512, 512), 512)
-        copies.append(
-            (
-                pltpu.make_async_copy(part, xs.at[k], sem.at[0, k]),
-                pltpu.make_async_copy(w.at[rows], ws.at[k], sem.at[1, k]),
-            )
-        )
-        for copy in copies[-1]:
-            copy.start()
+        copies.append(pltpu.make_async_copy(w.at[rows], ws.at[k], sem.at[k]))
+        copies[-1].start()
     for k in range(8):
-        for copy in copies[k]:
-            copy.wait()
-        term = jnp.dot(xs[k], ws[k], preferred_element_type=jnp.float32)
+        part = (mine if k < 4 else theirs)[k % 4, 0 : acc.shape[0]]
+        copies[k].wait()
+        term = jnp.dot(part, ws[k], preferred_element_type=jnp.float32)
         if k == 0:
             acc[...] = base[...].astype(jnp.float32) + term
         elif k < 7:
             acc[...] += term
         else:
-            o[...] = (acc[...] + term).astype(jnp.bfloat16)
-
-
-def project(order, mine, theirs, w, base):
+            total = (acc[...] + term).astype(jnp.bfloat16)
+            o[...] = total.reshape(o.shape)
+
+
+def project(order, mine, theirs, w, base, shape):
     rows = base.shape[0]
-    vmem, anywhere = pl.BlockSpec(memory_space=pltpu.VMEM), pl.BlockSpec(memory_space=pl.ANY)
+    vmem = pl.BlockSpec(memory_space=pltpu.VMEM)
+    hbm = pl.BlockSpec(memory_space=pltpu.HBM)
     return pl.pallas_call(
         project_kernel,
-        in_specs=[pl.BlockSpec(memory_space=pltpu.SMEM), anywhere, anywhere, anywhere, vmem],
+        in_specs=[pl.BlockSpec(memory_space=pltpu.SMEM), vmem, vmem, hbm, vmem],
         out_specs=vmem,
-        out_shape=jax.ShapeDtypeStruct((rows, 1024), jnp.bfloat16),
+        out_shape=jax.ShapeDtypeStruct(shape, jnp.bfloat16),
         scratch_shapes=[
-            pltpu.VMEM((8, rows, 512), jnp.bfloat16),
             pltpu.VMEM((8, 512, 1024), jnp.bfloat16),
             pltpu.VMEM((rows, 1024), jnp.float32),
-            pltpu.SemaphoreType.DMA((2, 8)),
+            pltpu.SemaphoreType.DMA((8,)),
         ],
         compiler_params=pltpu.CompilerParams(vmem_limit_bytes=ROOM),
         cost_estimate=pl.CostEstimate(
@@ -276,20 +270,19 @@
     )(order, mine, theirs, w, base)
 
 
-def experts_kernel(piece, gate, up, down, o, ps, gs, us, ds, sem):
+def experts_kernel(piece, gate, up, down, o, gs, us, ds, sem):
     wide = D // 4
     copies = []
     for k in range(4):
         span = pl.ds(k * wide, wide)
         copies.append(
             (
-                pltpu.make_async_copy(piece.at[:, span], ps.at[k], sem.at[0, k]),
-                pltpu.make_async_copy(gate.at[0, span], gs.at[k], sem.at[1, k]),
-                pltpu.make_async_copy(up.at[0, span], us.at[k], sem.at[2, k]),
+                pltpu.make_async_copy(gate.at[0, span], gs.at[k], sem.at[0, k]),
+                pltpu.make_async_copy(up.at[0, span], us.at[k], sem.at[1, k]),
             )
         )
     last = [
-        pltpu.make_async_copy(down.at[0, :, pl.ds(k * wide, wide)], ds.at[k], sem.at[3, k])
+        pltpu.make_async_copy(down.at[0, :, pl.ds(k * wide, wide)], ds.at[k], sem.at[2, k])
         for k in range(4)
     ]
     for group in (*copies, last):
@@ -299,8 +292,9 @@
     for k in range(4):
         for copy in copies[k]:
             copy.wait()
-        add_g = jnp.dot(ps[k], gs[k], preferred_element_type=jnp.float32)
-        add_u = jnp.dot(ps[k], us[k], preferred_element_type=jnp.float32)
+        rows = piece[:, k * wide : (k + 1) * wide]
+        add_g = jnp.dot(rows, gs[k], preferred_element_type=jnp.float32)
+        add_u = jnp.dot(rows, us[k], preferred_element_type=jnp.float32)
         g, u = (add_g, add_u) if k == 0 else (g + add_g, u + add_u)
     inner = (jax.nn.silu(g) * u).astype(jnp.bfloat16)
     for k in range(4):
@@ -311,18 +305,17 @@
 
 
 def experts(piece, w_gate, w_up, w_down):
-    anywhere = pl.BlockSpec(memory_space=pl.ANY)
+    hbm = pl.BlockSpec(memory_space=pltpu.HBM)
     return pl.pallas_call(
         experts_kernel,
-        in_specs=[anywhere] * 4,
+        in_specs=[pl.BlockSpec(memory_space=pltpu.VMEM)] + [hbm] * 3,
         out_specs=pl.BlockSpec(memory_space=pltpu.VMEM),
         out_shape=jax.ShapeDtypeStruct((128, D), jnp.bfloat16),
         scratch_shapes=[
-            pltpu.VMEM((4, 128, D // 4), jnp.bfloat16),
             pltpu.VMEM((4, D // 4, 256), jnp.bfloat16),
             pltpu.VMEM((4, D // 4, 256), jnp.bfloat16),
             pltpu.VMEM((4, 256, D // 4), jnp.bfloat16),
-            pltpu.SemaphoreType.DMA((4, 4)),
+            pltpu.SemaphoreType.DMA((3, 4)),
         ],
         compiler_params=pltpu.CompilerParams(vmem_limit_bytes=ROOM),
         cost_estimate=pl.CostEstimate(
@@ -388,27 +381,29 @@
             jnp.stack([bound, b, c]).astype(jnp.int32),
         ]
     ).astype(jnp.int32)
-    state = attend(0, tab, one)
-    attended = attend(1, tab, two, *state)
-    attended = exchange(attended, GROUP_AB)
-    attended = attended.reshape(4, TOK, HD).transpose(1, 0, 2).reshape(TOK, 4 * HD)
-
     ranked = picks.reshape(8, 8, 16)
     inside = (ranked // TOK) == seq
     local = jnp.sum(jnp.where(inside, ranked - seq * TOK, 0), axis=1).T.reshape(128, 1)
     filled = jnp.any(inside, axis=1).T.reshape(128, 1)
     hot = ((jnp.arange(TOK, dtype=jnp.int32)[None, :] == local) & filled).astype(jnp.bfloat16)
 
-    early = jnp.dot(hot, attended, preferred_element_type=jnp.float32).astype(jnp.bfloat16)
+    base = jnp.dot(hot, residual, preferred_element_type=jnp.float32).astype(jnp.bfloat16)
     gain_sent = jnp.stack(in_three(norm_gain), axis=1).reshape(12, 512)
     gain_sent = jnp.pad(gain_sent, ((0, 4), (0, 0)))
+
+    state = attend(0, tab, one)
+    attended = attend(1, tab, two, *state)
+    attended = exchange(attended, GROUP_AB)
+    attended, hot, base, gain_sent = lax.optimization_barrier((attended, hot, base, gain_sent))
+    attended = attended.reshape(4, TOK, HD).transpose(1, 0, 2).reshape(TOK, 4 * HD)
+
+    early = jnp.dot(hot, attended, preferred_element_type=jnp.float32).astype(jnp.bfloat16)
     early = jnp.concatenate([early, gain_sent], axis=0)
     mine = lax.all_to_all(jnp.broadcast_to(early[None], (4, 144, 512)), "y", 0, 0, tiled=True)
     theirs = swap(mine)
     chip = jnp.arange(4, dtype=jnp.int32)
     order = jnp.concatenate([2 * chip + c, 2 * chip + 1 - c]).astype(jnp.int32)
-    base = jnp.dot(hot, residual, preferred_element_type=jnp.float32).astype(jnp.bfloat16)
-    rows = project(order, mine, theirs, out_proj, base)
+    rows = project(order, mine, theirs, out_proj, base, (128, 8, 128))
     gains = jnp.stack([mine[:, 128:140], theirs[:, 128:140]]).reshape(2, 4, 2, 3, 1024)
     gains = jnp.where(expert < 4, gains[:, :, 0], gains[:, :, 1]).astype(jnp.float32)
     gains = gains[:, :, 0] + (gains[:, :, 1] + gains[:, :, 2])
@@ -416,7 +411,7 @@
     gain = gains.transpose(1, 0, 2).reshape(1, D)
 
     held, rows = lax.optimization_barrier((attended, rows))
-    arrived = lax.all_to_all(rows.reshape(128, 8, 128), ALL, 0, 0, tiled=True)
+    arrived = lax.all_to_all(rows, ALL, 0, 0, tiled=True)
     before = ring(held, 1)
     after = ring(held, -1)
     half = TOK // 2
@@ -425,8 +420,6 @@
     theirs = swap(mine)
     chip = jnp.remainder(y + jnp.array([0, 3, 1, 2], jnp.int32), 4)
     order = jnp.concatenate([2 * chip + c, 2 * chip + 1 - c]).astype(jnp.int32)
-    hidden = project(order, mine, theirs, out_proj, residual)
-
     own = lax.dynamic_index_in_dim(ranked, expert, 0, keepdims=False)
     own = lax.dynamic_index_in_dim(own, seq, 1, keepdims=False)
     source = (own // TOK)[:, None] == jnp.arange(16, dtype=jnp.int32)[None, :]
@@ -447,6 +440,8 @@
     back = lax.dot_general(
         source, weighted, (((0,), (0,)), ((), ())), preferred_element_type=jnp.float32
     ).astype(jnp.bfloat16)
+    back, mine, theirs = lax.optimization_barrier((back, mine, theirs))
+    hidden = project(order, mine, theirs, out_proj, residual, (TOK, 1024))
     returned = lax.all_to_all(back.reshape(128, 8, 128), ALL, 0, 0, tiled=True)
     expert_add = lax.dot_general(
         hot, returned.reshape(128, 1024), (((0,), (0,)), ((), ())), preferred_element_type=jnp.float32

time: 232 us -> 231 us (level)
  starting transfers between devices: 46.4 us -> 50.9 us
    ppermute x2, starting transfers between devices: 4.33 us -> 7.53 us  [swap(): return lax.ppermute(array, 'c', [(0, 1), (1, 0)])]
    all_to_all x5, waiting for transfers between devices: 31.1 us -> 28.1 us  [exchange(): lax.all_to_all(array, ALL, 0, 0, tiled=True, axis_index_groups=groups)]
    pallas_call x1, Pallas kernels: 2.82 us -> 0.27 us  [pack_heads(): pl.pallas_call(pack_heads_kernel, out_shape=jax.ShapeDtypeStruct((4, 3, T...]
    unnamed x34 -> x31, local copies, waits for them, and re-layouts: 6.4 us -> 6.35 us
  transfers between devices with their start and end apart: 14 -> 14, of which waited for: 9 -> 9; matrix products, arithmetic and copies ran while one was open for 5% -> 4% of each run, Pallas kernels for 11% -> 12%
where the time goes in v4:
time: 231 us; the launch traced here: 230 us
  waiting for transfers between devices  59.3 us (26%)
  starting transfers between devices  50.9 us (22%)
  blocking collectives  49.9 us (22%)
  Pallas kernels  46.7 us (20%)
  local copies, waits for them, and re-layouts  11.7 us (5%)
  other arithmetic  8.24 us (4%)
    all_to_all x3, blocking collectives, exchange(): lax.all_to_all(array, ALL, 0, 0, tiled=True, axis_index_groups=groups)  49.9 us
    all_to_all x5, waiting for transfers between devices, exchange(): lax.all_to_all(array, ALL, 0, 0, tiled=True, axis_index_groups=groups)  28.1 us
    pallas_call x2, Pallas kernels, attend(): pl.pallas_call(functools.partial(attend_kernel, part=part), out_shape=out...  24 us
    all_to_all x5, starting transfers between devices, exchange(): lax.all_to_all(array, ALL, 0, 0, tiled=True, axis_index_groups=groups)  21.7 us
    pallas_call x2, Pallas kernels, project(): pl.pallas_call(project_kernel, in_specs=[pl.BlockSpec(memory_space=pltpu....  13.8 us
    all_to_all x1, waiting for transfers between devices, shards(): arrived = lax.all_to_all(rows, ALL, 0, 0, tiled=True)  10.9 us
    ppermute x4, waiting for transfers between devices, ring(): return lax.ppermute(array, 'y', [(i, (i + step) % 4) for i in range(4)])  10.3 us
    all_to_all x1, starting transfers between devices, shards(): returned = lax.all_to_all(back.reshape(128, 8, 128), ALL, 0, 0, tiled=True)  9 us
  transfers between devices with their start and end apart: 14, of which 9 were waited for; matrix products, arithmetic and copies ran while one was open for 4% of the time, Pallas kernels for 12%

profile of v4, /device:TPU:1, one launch (start us, length us, event | category | flops | bytes accessed | tf_op | source)
XLA Modules:
  0.0 229.7 jit_solution(8370021331736243924)
XLA Ops:
  0.0 1.0 copy-done.3
  1.1 1.0 copy-done.4
  2.1 1.0 copy-done.5
  3.4 17.5 %all_to_all.55.got.q = bf16[4,3,512,128]{3,2,1,0:T(8,128)(2,1)S(1)} all-to-all(bf16[4,3,512,128]{3,2,1,0:T(8,128)(2,1)S(1)} %pack_heads.1), channel_id=1, replica_groups={{0,32,64,96},{1,9,17,25},{8,40,72,104},{33,41,49,57},{16,48,80,112},{65..., dimensions={0} | all-to-all | bytes 3145728 | tf_op jit(solution)/shard_map/all_to_all | solution.py:51
  20.9 0.4 pack_parts.1
  21.4 23.0 %all_to_all.56 = bf16[4,2,1280,128]{3,2,1,0:T(8,128)(2,1)S(1)} all-to-all(bf16[4,2,1280,128]{3,2,1,0:T(8,128)(2,1)S(1)} %get-tuple-element.22), channel_id=1, replica_groups={{0,8,16,24},{1,33,65,97},{32,40,48,56},{9,41,73,105},{64,72,80,88},{17,..., dimensions={0} | all-to-all | bytes 5242880 | tf_op jit(solution)/shard_map/all_to_all | solution.py:51
  44.4 4.6 %all-to-all-start.2 = ((bf16[4,2,1024,128]{3,2,1,0:T(8,128)(2,1)}), bf16[4,2,1024,128]{3,2,1,0:T(8,128)(2,1)}, u32[]{:S(2)}, u32[]{:S(2)}) async-start(bf16[4,2,1024,128]{3,2,1,0:T(8,128)(2,1)} %copy-done.1), calls=%async_computation.2 | async-start | bytes 4194304 | tf_op jit(solution)/shard_map/all_to_all | solution.py:51
  49.0 0.6 reduce_sum.48
  50.6 11.3 %attend.2 = (f32[4,1,512]{2,1,0:T(1,128)S(1)}, f32[4,1,512]{2,1,0:T(1,128)S(1)}, f32[4,128,512]{2,1,0:T(8,128)S(1)}, bf16[4,128,512]{2,1,0:T(8,128)(2,1)S(1)}) custom-call(s32[51]{0:T(128)S(1)} %concatenate.17.tab, bf16[8,1280,128]{2,1,0:T(8,128)(2,1)S(1)} %bitcast.71), custom_call_target="tpu_custom_call" | custom-call | flops 6000000000 | bytes 4000000 | tf_op jit(solution)/shard_map/attend/pallas_call | solution.py:211
  61.9 1.0 copy-done.6
  62.9 1.8 all-to-all-done.2
  64.7 1.2 copy-done.7
  65.9 12.7 %attend.3 = bf16[16,128,128]{2,1,0:T(8,128)(2,1)} custom-call(s32[51]{0:T(128)S(1)} %concatenate.17.tab, bf16[8,1024,128]{2,1,0:T(8,128)(2,1)} %bitcast.5.r, f32[4,1,512]{2,1,0:T(1,128)S(1)} %get-tuple-element.26.refs_0_, f32[4,1,512]{2,1,0:T(1,128)S(1)} %get-tuple-element.27.refs_1_, f32[4,128,512]{2,1,0:T(8,128)S(1)} %copy-done.7, ...), custom_call_target="tpu_custom_call" | custom-call | flops 6000000000 | bytes 4000000 | tf_op jit(solution)/shard_map/attend/pallas_call | solution.py:211
  78.6 3.6 %all-to-all-start.3 = ((bf16[16,128,128]{2,1,0:T(8,128)(2,1)}), bf16[16,128,128]{2,1,0:T(8,128)(2,1)S(1)}, u32[]{:S(2)}, u32[]{:S(2)}) async-start(bf16[16,128,128]{2,1,0:T(8,128)(2,1)} %attend.3), calls=%async_computation.3 | async-start | bytes 1048576 | tf_op jit(solution)/shard_map/all_to_all | solution.py:51
  83.1 8.0 %all-to-all-done.3 = bf16[16,128,128]{2,1,0:T(8,128)(2,1)S(1)} async-done(((bf16[16,128,128]{2,1,0:T(8,128)(2,1)}), bf16[16,128,128]{2,1,0:T(8,128)(2,1)S(1)}, u32[]{:S(2)}, u32[]{:S(2)}) %all-to-all-start.3) | async-done | bytes 524320 | tf_op jit(solution)/shard_map/all_to_all | solution.py:51
  91.2 0.4 copy.31
  91.8 0.9 broadcast_in_dim.10
  92.7 4.2 %all-to-all-start.4 = ((bf16[4,144,512]{2,1,0:T(8,128)(2,1)}), bf16[4,144,512]{2,1,0:T(8,128)(2,1)S(1)}, u32[]{:S(2)}, u32[]{:S(2)}) async-start(bf16[4,144,512]{2,1,0:T(8,128)(2,1)} %broadcast_in_dim.10), calls=%async_computation.4 | async-start | bytes 1179648 | tf_op jit(solution)/shard_map/all_to_all | solution.py:402
  96.9 7.3 %all-to-all-done.4.mine = bf16[4,144,512]{2,1,0:T(8,128)(2,1)S(1)} async-done(((bf16[4,144,512]{2,1,0:T(8,128)(2,1)}), bf16[4,144,512]{2,1,0:T(8,128)(2,1)S(1)}, u32[]{:S(2)}, u32[]{:S(2)}) %all-to-all-start.4) | async-done | bytes 589856 | tf_op jit(solution)/shard_map/all_to_all | solution.py:402
  104.2 5.9 %collective-permute-start = (bf16[4,144,512]{2,1,0:T(8,128)(2,1)S(1)}, bf16[4,144,512]{2,1,0:T(8,128)(2,1)S(1)}, u32[]{:S(2)}, u32[]{:S(2)}) collective-permute-start(bf16[4,144,512]{2,1,0:T(8,128)(2,1)S(1)} %all-to-all-done.4.mine), channel_id=1, source_target_pairs={{0,1},{1,0},{2,3},{3,2},{4,5},{5,4},{6,7},{7,6},{8,9},{9,8},{10,11... | collective-permute-start | bytes 1769480 | tf_op jit(solution)/shard_map/ppermute | solution.py:329
  110.3 0.9 copy.46
  111.3 0.4 collective-permute-done.theirs
  111.7 5.0 %project.2 = bf16[128,8,128]{2,1,0:T(8,128)(2,1)} custom-call(s32[8]{0:T(128)S(1)} %pad_add_fusion.1.order, bf16[4,144,512]{2,1,0:T(8,128)(2,1)S(1)} %all-to-all-done.4.mine, bf16[4,144,512]{2,1,0:T(8,128)(2,1)S(1)} %collective-permute-done.theirs, bf16[4096,1024]{1,0:T(8,128)(2,1)} %w.3, bf16[128,1024]{1,0:T(8,128)(2,1)S(1)} %convolution_convert_fusion.1.base), custom_call_target="tpu_custom_call" | custom-call | flops 1073741824 | bytes 9961472 | tf_op jit(solution)/shard_map/project/pallas_call | solution.py:255
  116.8 3.8 %all-to-all-start.5 = ((bf16[128,8,128]{2,1,0:T(8,128)(2,1)}), bf16[128,8,128]{2,1,0:T(8,128)(2,1)S(1)}, u32[]{:S(2)}, u32[]{:S(2)}) async-start(bf16[128,8,128]{2,1,0:T(8,128)(2,1)} %project.2), calls=%async_computation.5 | async-start | bytes 524288 | tf_op jit(solution)/shard_map/all_to_all | solution.py:414
  120.9 10.9 %all-to-all-done.5 = bf16[128,8,128]{2,1,0:T(8,128)(2,1)S(1)} async-done(((bf16[128,8,128]{2,1,0:T(8,128)(2,1)}), bf16[128,8,128]{2,1,0:T(8,128)(2,1)S(1)}, u32[]{:S(2)}, u32[]{:S(2)}) %all-to-all-start.5) | async-done | bytes 262176 | tf_op jit(solution)/shard_map/all_to_all | solution.py:414
  131.9 0.4 multiply_reduce_fusion
  132.5 9.4 %all_to_all.57 = bf16[4,8,8192]{2,1,0:T(8,128)(2,1)S(1)} all-to-all(bf16[4,8,8192]{2,1,0:T(8,128)(2,1)S(1)} %broadcast_in_dim.11), channel_id=1, replica_groups={{0,32,64,96},{1,9,17,25},{8,40,72,104},{33,41,49,57},{16,48,80,112},{65..., dimensions={0} | all-to-all | bytes 1048576 | tf_op jit(solution)/shard_map/all_to_all | solution.py:51
  141.8 1.5 broadcast_in_dim.13
  143.4 4.6 %all-to-all-start.7 = ((bf16[4,32,8192]{2,1,0:T(8,128)(2,1)}), bf16[4,32,8192]{2,1,0:T(8,128)(2,1)}, u32[]{:S(2)}, u32[]{:S(2)}) async-start(bf16[4,32,8192]{2,1,0:T(8,128)(2,1)} %broadcast_in_dim.13), calls=%async_computation.7 | async-start | bytes 4194304 | tf_op jit(solution)/shard_map/all_to_all | solution.py:51
  148.0 1.4 collective-permute-start.2
  149.5 10.3 %collective-permute-done.2 = bf16[512,512]{1,0:T(8,128)(2,1)S(1)} collective-permute-done((bf16[512,512]{1,0:T(8,128)(2,1)S(1)}, bf16[512,512]{1,0:T(8,128)(2,1)S(1)}, u32[]{:S(2)}, u32[]{:S(2)}) %collective-permute-start.2) | collective-permute-done | bytes 524320 | tf_op jit(solution)/shard_map/ppermute | solution.py:333
  159.8 3.1 %collective-permute-start.4 = (bf16[256,512]{1,0:T(8,128)(2,1)S(1)}, bf16[256,512]{1,0:T(8,128)(2,1)}, u32[]{:S(2)}, u32[]{:S(2)}) collective-permute-start(bf16[256,512]{1,0:T(8,128)(2,1)S(1)} %slice.44), channel_id=1, source_target_pairs={{0,6},{2,0},{4,2},{6,4},{1,7},{3,1},{5,3},{7,5},{8,14},{10,8},{12,... | collective-permute-start | bytes 786440 | tf_op jit(solution)/shard_map/ppermute | solution.py:333
  162.9 0.7 slice.43
  163.7 8.1 %experts.1 = bf16[128,8192]{1,0:T(8,128)(2,1)} custom-call(bf16[128,8192]{1,0:T(8,128)(2,1)} %bitcast.18.piece, bf16[1,8192,256]{2,1,0:T(8,128)(2,1)} %gate.1, bf16[1,8192,256]{2,1,0:T(8,128)(2,1)} %up.1, bf16[1,256,8192]{2,1,0:T(8,128)(2,1)} %down.1), custom_call_target="tpu_custom_call" | custom-call | flops 1610000000 | bytes 16800000 | tf_op jit(solution)/shard_map/experts/pallas_call | solution.py:309
  171.8 5.5 %all-to-all-start.8 = ((bf16[4,32,8192]{2,1,0:T(8,128)(2,1)}), bf16[4,32,8192]{2,1,0:T(8,128)(2,1)}, u32[]{:S(2)}, u32[]{:S(2)}) async-start(bf16[4,32,8192]{2,1,0:T(8,128)(2,1)} %bitcast.19), calls=%async_computation.8 | async-start | bytes 4194304 | tf_op jit(solution)/shard_map/all_to_all | solution.py:51
  177.4 1.1 maximum_bitcast_fusion
  178.4 1.6 pad_maximum_fusion.mine
  180.1 1.6 collective-permute-start.5
  181.7 11.6 %all-to-all-done.8 = bf16[4,32,8192]{2,1,0:T(8,128)(2,1)} async-done(((bf16[4,32,8192]{2,1,0:T(8,128)(2,1)}), bf16[4,32,8192]{2,1,0:T(8,128)(2,1)}, u32[]{:S(2)}, u32[]{:S(2)}) %all-to-all-start.8) | async-done | bytes 2097184 | tf_op jit(solution)/shard_map/all_to_all | solution.py:51
  193.3 2.8 %reduce_sum.51 = bf16[32,8192]{1,0:T(8,128)(2,1)} reduce(bf16[4,32,8192]{2,1,0:T(8,128)(2,1)} %all-to-all-done.8, bf16[]{:T(256)} %constant.141.clone.1), dimensions={0}, to_apply=%region_4.5 | reduce | flops 786432 | bytes 2621442 | tf_op jit(solution)/shard_map/reduce_sum | solution.py:436
  196.1 3.5 %all-to-all-start.9 = ((bf16[4,8,8192]{2,1,0:T(8,128)(2,1)}), bf16[4,8,8192]{2,1,0:T(8,128)(2,1)S(1)}, u32[]{:S(2)}, u32[]{:S(2)}) async-start(bf16[4,8,8192]{2,1,0:T(8,128)(2,1)} %bitcast.20), calls=%async_computation.9 | async-start | bytes 1048576 | tf_op jit(solution)/shard_map/all_to_all | solution.py:51
  199.9 6.6 %all-to-all-done.9 = bf16[4,8,8192]{2,1,0:T(8,128)(2,1)S(1)} async-done(((bf16[4,8,8192]{2,1,0:T(8,128)(2,1)}), bf16[4,8,8192]{2,1,0:T(8,128)(2,1)S(1)}, u32[]{:S(2)}, u32[]{:S(2)}) %all-to-all-start.9) | async-done | bytes 524320 | tf_op jit(solution)/shard_map/all_to_all | solution.py:51
  206.9 0.8 reshape.114
  207.8 9.0 %all-to-all-start.10 = ((bf16[128,8,128]{2,1,0:T(8,128)(2,1)}), bf16[128,8,128]{2,1,0:T(8,128)(2,1)S(1)}, u32[]{:S(2)}, u32[]{:S(2)}) async-start(bf16[128,8,128]{2,1,0:T(8,128)(2,1)} %reshape.114), calls=%async_computation.10 | async-start | bytes 524288 | tf_op jit(solution)/shard_map/all_to_all | solution.py:445
  216.8 8.8 %project.3 = bf16[512,1024]{1,0:T(8,128)(2,1)S(1)} custom-call(s32[8]{0:T(128)S(1)} %pad_add_fusion.order, bf16[4,512,512]{2,1,0:T(8,128)(2,1)} %pad_maximum_fusion.mine, bf16[4,512,512]{2,1,0:T(8,128)(2,1)} %collective-permute-done.5.theirs, bf16[4096,1024]{1,0:T(8,128)(2,1)} %w.3, bf16[512,1024]{1,0:T(8,128)(2,1)S(1)} %copy-done.2), custom_call_target="tpu_custom_call" | custom-call | flops 4294967296 | bytes 14680064 | tf_op jit(solution)/shard_map/project/pallas_call | solution.py:255
  225.5 2.3 %all-to-all-done.10 = bf16[128,8,128]{2,1,0:T(8,128)(2,1)S(1)} async-done(((bf16[128,8,128]{2,1,0:T(8,128)(2,1)}), bf16[128,8,128]{2,1,0:T(8,128)(2,1)S(1)}, u32[]{:S(2)}, u32[]{:S(2)}) %all-to-all-start.10) | async-done | bytes 262176 | tf_op jit(solution)/shard_map/all_to_all | solution.py:445
  227.8 0.5 fusion.4
  228.3 1.4 add_convert_fusion
  (76 shorter events, 3.4 us)
Async XLA Ops:
  0.0 199.7 %copy-start = (bf16[8192,1]{0,1:T(2,128)(2,1)S(1)}, bf16[8192,1]{0,1:T(2,128)(2,1)}, u32[]{:S(2)}) copy-start(bf16[8192,1]{0,1:T(2,128)(2,1)} %param.22) | copy-start | bytes 49156
  0.0 1.0 copy-start.3
  1.1 1.0 copy-start.4
  2.1 1.0 copy-start.5
  21.3 23.0 %copy-start.1 = (bf16[4,2,1024,128]{3,2,1,0:T(8,128)(2,1)}, bf16[4,2,1024,128]{3,2,1,0:T(8,128)(2,1)S(1)}, u32[]{:S(2)}) copy-start(bf16[4,2,1024,128]{3,2,1,0:T(8,128)(2,1)S(1)} %get-tuple-element.24) | copy-start | bytes 6291460
  44.4 4.6 %copy-start.9 = (s32[8192]{0:T(1024)S(1)}, s32[8192]{0:T(1024)}, u32[]{:S(2)}) copy-start(s32[8192]{0:T(1024)} %param.18) | copy-start | bytes 98308
  44.4 5.3 %copy-start.11 = (s32[8,128]{1,0:T(8,128)S(1)}, s32[8,128]{1,0:T(8,128)}, u32[]{:S(2)}) copy-start(s32[8,128]{1,0:T(8,128)} %param.21) | copy-start | bytes 12292
  44.4 6.2 %copy-start.10 = (f32[2,1024]{1,0:T(2,128)S(1)}, f32[2,1024]{1,0:T(2,128)}, u32[]{:S(2)}) copy-start(f32[2,1024]{1,0:T(2,128)} %param.20) | copy-start | bytes 24580
  44.4 20.3 %all-to-all-start.2 = ((bf16[4,2,1024,128]{3,2,1,0:T(8,128)(2,1)}), bf16[4,2,1024,128]{3,2,1,0:T(8,128)(2,1)}, u32[]{:S(2)}, u32[]{:S(2)}) async-start(bf16[4,2,1024,128]{3,2,1,0:T(8,128)(2,1)} %copy-done.1), calls=%async_computation.2 | async-start | bytes 4194304 | tf_op jit(solution)/shard_map/all_to_all | solution.py:51
  61.9 1.0 copy-start.6
  64.7 1.2 copy-start.7
  65.9 16.9 %copy-start.2 = (bf16[512,1024]{1,0:T(8,128)(2,1)S(1)}, bf16[512,1024]{1,0:T(8,128)(2,1)}, u32[]{:S(2)}) copy-start(bf16[512,1024]{1,0:T(8,128)(2,1)} %base.1) | copy-start | bytes 3145732
  78.6 12.5 %all-to-all-start.3 = ((bf16[16,128,128]{2,1,0:T(8,128)(2,1)}), bf16[16,128,128]{2,1,0:T(8,128)(2,1)S(1)}, u32[]{:S(2)}, u32[]{:S(2)}) async-start(bf16[16,128,128]{2,1,0:T(8,128)(2,1)} %attend.3), calls=%async_computation.3 | async-start | bytes 1048576 | tf_op jit(solution)/shard_map/all_to_all | solution.py:51
  92.7 11.5 %all-to-all-start.4 = ((bf16[4,144,512]{2,1,0:T(8,128)(2,1)}), bf16[4,144,512]{2,1,0:T(8,128)(2,1)S(1)}, u32[]{:S(2)}, u32[]{:S(2)}) async-start(bf16[4,144,512]{2,1,0:T(8,128)(2,1)} %broadcast_in_dim.10), calls=%async_computation.4 | async-start | bytes 1179648 | tf_op jit(solution)/shard_map/all_to_all | solution.py:402
  104.2 7.6 %collective-permute-start = (bf16[4,144,512]{2,1,0:T(8,128)(2,1)S(1)}, bf16[4,144,512]{2,1,0:T(8,128)(2,1)S(1)}, u32[]{:S(2)}, u32[]{:S(2)}) collective-permute-start(bf16[4,144,512]{2,1,0:T(8,128)(2,1)S(1)} %all-to-all-done.4.mine), channel_id=1, source_target_pairs={{0,1},{1,0},{2,3},{3,2},{4,5},{5,4},{6,7},{7,6},{8,9},{9,8},{10,11... | collective-permute-start | bytes 1769480 | tf_op jit(solution)/shard_map/ppermute | solution.py:329
  116.8 15.0 %all-to-all-start.5 = ((bf16[128,8,128]{2,1,0:T(8,128)(2,1)}), bf16[128,8,128]{2,1,0:T(8,128)(2,1)S(1)}, u32[]{:S(2)}, u32[]{:S(2)}) async-start(bf16[128,8,128]{2,1,0:T(8,128)(2,1)} %project.2), calls=%async_computation.5 | async-start | bytes 524288 | tf_op jit(solution)/shard_map/all_to_all | solution.py:414
  143.4 4.6 %copy-start.8 = (bf16[64,8,4,128]{3,1,2,0:T(8,128)(2,1)S(1)}, bf16[64,8,4,128]{3,1,2,0:T(8,128)(2,1)}, u32[]{:S(2)}) copy-start(bf16[64,8,4,128]{3,1,2,0:T(8,128)(2,1)} %copy.46) | copy-start | bytes 1572868
  143.4 20.3 %all-to-all-start.7 = ((bf16[4,32,8192]{2,1,0:T(8,128)(2,1)}), bf16[4,32,8192]{2,1,0:T(8,128)(2,1)}, u32[]{:S(2)}, u32[]{:S(2)}) async-start(bf16[4,32,8192]{2,1,0:T(8,128)(2,1)} %broadcast_in_dim.13), calls=%async_computation.7 | async-start | bytes 4194304 | tf_op jit(solution)/shard_map/all_to_all | solution.py:51
  148.0 11.8 %collective-permute-start.2 = (bf16[512,512]{1,0:T(8,128)(2,1)S(1)}, bf16[512,512]{1,0:T(8,128)(2,1)S(1)}, u32[]{:S(2)}, u32[]{:S(2)}) collective-permute-start(bf16[512,512]{1,0:T(8,128)(2,1)S(1)} %bitcast.76), channel_id=1, source_target_pairs={{0,6},{2,0},{4,2},{6,4},{1,7},{3,1},{5,3},{7,5},{8,14},{10,8},{12,... | collective-permute-start | bytes 1572872 | tf_op jit(solution)/shard_map/ppermute | solution.py:333
  149.3 13.6 %collective-permute-start.1 = (bf16[512,512]{1,0:T(8,128)(2,1)S(1)}, bf16[512,512]{1,0:T(8,128)(2,1)S(1)}, u32[]{:S(2)}, u32[]{:S(2)}) collective-permute-start(bf16[512,512]{1,0:T(8,128)(2,1)S(1)} %bitcast.77), channel_id=1, source_target_pairs={{0,2},{2,4},{4,6},{6,0},{1,3},{3,5},{5,7},{7,1},{8,10},{10,12},{12... | collective-permute-start | bytes 1572872 | tf_op jit(solution)/shard_map/ppermute | solution.py:333
  159.8 17.6 %collective-permute-start.4 = (bf16[256,512]{1,0:T(8,128)(2,1)S(1)}, bf16[256,512]{1,0:T(8,128)(2,1)}, u32[]{:S(2)}, u32[]{:S(2)}) collective-permute-start(bf16[256,512]{1,0:T(8,128)(2,1)S(1)} %slice.44), channel_id=1, source_target_pairs={{0,6},{2,0},{4,2},{6,4},{1,7},{3,1},{5,3},{7,5},{8,14},{10,8},{12,... | collective-permute-start | bytes 786440 | tf_op jit(solution)/shard_map/ppermute | solution.py:333
  163.6 13.7 %collective-permute-start.3 = (bf16[256,512]{1,0:T(8,128)(2,1)}, bf16[256,512]{1,0:T(8,128)(2,1)}, u32[]{:S(2)}, u32[]{:S(2)}) collective-permute-start(bf16[256,512]{1,0:T(8,128)(2,1)} %slice.43), channel_id=1, source_target_pairs={{0,2},{2,4},{4,6},{6,0},{1,3},{3,5},{5,7},{7,1},{8,10},{10,12},{12... | collective-permute-start | bytes 786440 | tf_op jit(solution)/shard_map/ppermute | solution.py:333
  171.8 21.5 %all-to-all-start.8 = ((bf16[4,32,8192]{2,1,0:T(8,128)(2,1)}), bf16[4,32,8192]{2,1,0:T(8,128)(2,1)}, u32[]{:S(2)}, u32[]{:S(2)}) async-start(bf16[4,32,8192]{2,1,0:T(8,128)(2,1)} %bitcast.19), calls=%async_computation.8 | async-start | bytes 4194304 | tf_op jit(solution)/shard_map/all_to_all | solution.py:51
  178.4 3.2 %copy-start.12 = (s32[4]{0:T(128)S(1)}, s32[4]{0:T(128)}, u32[]{:S(2)}) copy-start(s32[4]{0:T(128)} %constant.145.clone) | copy-start | bytes 52
  180.1 26.9 %collective-permute-start.5 = (bf16[4,512,512]{2,1,0:T(8,128)(2,1)}, bf16[4,512,512]{2,1,0:T(8,128)(2,1)}, u32[]{:S(2)}, u32[]{:S(2)}) collective-permute-start(bf16[4,512,512]{2,1,0:T(8,128)(2,1)} %pad_maximum_fusion.mine), channel_id=1, source_target_pairs={{0,1},{1,0},{2,3},{3,2},{4,5},{5,4},{6,7},{7,6},{8,9},{9,8},{10,11... | collective-permute-start | bytes 6291464 | tf_op jit(solution)/shard_map/ppermute | solution.py:329
  196.1 10.4 %all-to-all-start.9 = ((bf16[4,8,8192]{2,1,0:T(8,128)(2,1)}), bf16[4,8,8192]{2,1,0:T(8,128)(2,1)S(1)}, u32[]{:S(2)}, u32[]{:S(2)}) async-start(bf16[4,8,8192]{2,1,0:T(8,128)(2,1)} %bitcast.20), calls=%async_computation.9 | async-start | bytes 1048576 | tf_op jit(solution)/shard_map/all_to_all | solution.py:51
  207.8 20.1 %all-to-all-start.10 = ((bf16[128,8,128]{2,1,0:T(8,128)(2,1)}), bf16[128,8,128]{2,1,0:T(8,128)(2,1)S(1)}, u32[]{:S(2)}, u32[]{:S(2)}) async-start(bf16[128,8,128]{2,1,0:T(8,128)(2,1)} %reshape.114), calls=%async_computation.10 | async-start | bytes 524288 | tf_op jit(solution)/shard_map/all_to_all | solution.py:445

commit v5 on v4

--- a/solution.py
+++ b/solution.py
@@ -108,9 +108,17 @@
 
 def attend_kernel(tab, r, *refs, part):
     if part == 0:
-        mo, lo_, acco, qto, vt, s0, s1, acc, m, l = refs
+        mo, lo_, acco, qto, vt, s0, s1, sums, m, l, sem = refs
+        moves = [
+            pltpu.make_async_copy(sums.at[n], acco.at[n], sem.at[n]) for n in range(TILES)
+        ]
     else:
-        mi, li, acci, qti, o, vt, s0, s1, acc, m, l = refs
+        mi, li, acci, qti, o, vt, s0, s1, sums, m, l, sem = refs
+        moves = [
+            pltpu.make_async_copy(acci.at[n], sums.at[n], sem.at[n]) for n in range(TILES)
+        ]
+        for move in moves:
+            move.start()
     bound, sub, core = tab[48], tab[49], tab[50]
     start = jnp.where(core == 0, 4 * part, part)
 
@@ -122,8 +130,9 @@
     col = lax.broadcasted_iota(jnp.int32, (1, QW), 1)
     row = lax.broadcasted_iota(jnp.int32, (TOK, 1), 0)
 
-    def tile(index, carry):
+    def tile(index):
         j = TILE * index
+        acc = sums.at[index]
         if part == 0:
             qt = qto.at[index]
             for i in range(TILE):
@@ -136,7 +145,7 @@
             qt = qti.at[index]
             m[...] = mi[index]
             l[...] = li[index]
-            acc[...] = acci[index]
+            moves[index].wait()
         first = j * TOK + sub * 128
         last = first + (TILE - 1) * TOK + 127
         qpos = first + (col // 128) * TOK + col % 128
@@ -146,21 +155,23 @@
         lo = (jnp.maximum(lo - start, 0) + core) >> core
         hi = jnp.minimum((jnp.maximum(hi - start, 0) + core) >> core, 4)
 
-        def score(t):
-            return jnp.dot(r[tab[t], 0:TOK, :], qt[...], preferred_element_type=jnp.float32)
-
-        def soft(s, t, masked):
-            here = s[...]
+        def score(t, c0=0):
+            return jnp.dot(
+                r[tab[t], 0:TOK, :], qt[:, c0:], preferred_element_type=jnp.float32
+            )
+
+        def soft(s, t, masked, c0=0):
+            here = s[:, c0:]
             if masked:
                 kpos = t * TOK + row
-                here = jnp.where((kpos <= qpos) & (kpos >= qlow), here, NEG)
-            old = m[...]
+                here = jnp.where((kpos <= qpos[:, c0:]) & (kpos >= qlow[:, c0:]), here, NEG)
+            old = m[:, c0:]
             new = jnp.maximum(old, jnp.max(here, axis=0, keepdims=True))
             p = jnp.exp2(here * SCALE - new * SCALE)
             f = jnp.exp2((old - new) * SCALE)
-            m[...] = new
-            l[...] = l[...] * f + jnp.sum(p, axis=0, keepdims=True)
-            acc[...] = acc[...] * f + jnp.dot(
+            m[:, c0:] = new
+            l[:, c0:] = l[:, c0:] * f + jnp.sum(p, axis=0, keepdims=True)
+            acc[:, c0:] = acc[:, c0:] * f + jnp.dot(
                 vt[tab[t]], p.astype(jnp.bfloat16), preferred_element_type=jnp.float32
             )
 
@@ -178,27 +189,40 @@
                 s0[...] = score(first_of(jnp.minimum(i + 1, 3)))
                 soft(s1, t + 1, masked)
 
+            def go_half():
+                half = QW // 2
+                s1[:, half:] = score(t + 1, half)
+                soft(s0, t, True, half)
+                soft(s1, t + 1, True, half)
+
             need = ((t + 2) * TOK - 1 > first) | ((t * TOK < bound) & (last >= bound))
-            pl.when(need)(lambda: go(True))
-            pl.when(jnp.logical_not(need))(lambda: go(False))
+            final = t == j + 2
+            pl.when(final)(go_half)
+            pl.when(need & jnp.logical_not(final))(lambda: go(True))
+            pl.when(jnp.logical_not(need | final))(lambda: go(False))
             return inner
 
         lax.fori_loop(lo, hi, step, 0)
         if part == 0:
             mo[index] = m[...]
             lo_[index] = l[...]
-            acco[index] = acc[...]
+            moves[index].start()
         else:
             out = (acc[...] / l[...]).T.astype(jnp.bfloat16)
             for i in range(TILE):
                 o[tab[16 + j + i]] = out[i * 128 : (i + 1) * 128]
-        return carry
-
-    lax.fori_loop(0, TILES, tile, 0)
+
+    for n in range(TILES):
+        tile(n)
+    if part == 0:
+        for move in moves:
+            move.wait()
 
 
 def attend(part, tab, received, *state):
     vmem = pl.BlockSpec(memory_space=pltpu.VMEM)
+    anywhere = pl.BlockSpec(memory_space=pl.ANY)
+    state_specs = [vmem, vmem, anywhere, vmem]
     if part == 0:
         out_shape = [
             jax.ShapeDtypeStruct((TILES, 1, QW), jnp.float32),
@@ -211,15 +235,16 @@
     return pl.pallas_call(
         functools.partial(attend_kernel, part=part),
         out_shape=out_shape,
-        in_specs=[pl.BlockSpec(memory_space=pltpu.SMEM), vmem] + [vmem] * len(state),
-        out_specs=[vmem] * 4 if part == 0 else vmem,
+        in_specs=[pl.BlockSpec(memory_space=pltpu.SMEM), vmem] + state_specs[: len(state)],
+        out_specs=state_specs if part == 0 else vmem,
         scratch_shapes=[
             pltpu.VMEM((8, HD, TOK), jnp.bfloat16),
             pltpu.VMEM((TOK, QW), jnp.float32),
             pltpu.VMEM((TOK, QW), jnp.float32),
-            pltpu.VMEM((HD, QW), jnp.float32),
+            pltpu.VMEM((TILES, HD, QW), jnp.float32),
             pltpu.VMEM((1, QW), jnp.float32),
             pltpu.VMEM((1, QW), jnp.float32),
+            pltpu.SemaphoreType.DMA((TILES,)),
         ],
         compiler_params=pltpu.CompilerParams(vmem_limit_bytes=24 << 20),
         cost_estimate=pl.CostEstimate(
@@ -317,12 +342,32 @@
             pltpu.VMEM((4, 256, D // 4), jnp.bfloat16),
             pltpu.SemaphoreType.DMA((3, 4)),
         ],
-        compiler_params=pltpu.CompilerParams(vmem_limit_bytes=ROOM),
+        compiler_params=pltpu.CompilerParams(vmem_limit_bytes=46 << 20),
         cost_estimate=pl.CostEstimate(
             flops=1_610_000_000, bytes_accessed=16_800_000, transcendentals=32_768
         ),
         name="experts",
     )(piece, w_gate, w_up, w_down)
+
+
+def add_kernel(parts, o):
+    total = parts[0].astype(jnp.float32)
+    for n in range(1, 4):
+        total += parts[n].astype(jnp.float32)
+    o[...] = total.astype(o.dtype)
+
+
+def add(parts):
+    rows, width = parts.shape[1] // 4, parts.shape[2]
+    return pl.pallas_call(
+        add_kernel,
+        grid=(4,),
+        in_specs=[pl.BlockSpec((4, rows, width), lambda k: (0, k, 0))],
+        out_specs=pl.BlockSpec((rows, width), lambda k: (k, 0)),
+        out_shape=jax.ShapeDtypeStruct(parts.shape[1:], jnp.bfloat16),
+        compiler_params=pltpu.CompilerParams(vmem_limit_bytes=8 << 20),
+        name="add",
+    )(parts)
 
 
 def swap(array):
@@ -433,7 +478,7 @@
     piece = far.reshape(128, D)
     partial = experts(piece, w_gate, w_up, w_down)
     partial = exchange(partial.reshape(4, 32, D), GROUP_B)
-    partial = jnp.sum(partial.astype(jnp.float32), axis=0).astype(jnp.bfloat16)
+    partial = add(partial)
     partial = exchange(partial.reshape(4, 8, D), GROUP_A)
     summed = jnp.sum(partial.astype(jnp.float32), axis=0)
     weighted = (jax.nn.sigmoid(logits) * summed).astype(jnp.bfloat16)

time: 231 us -> 226 us (0.978)
  Pallas kernels: 46.7 us -> 42 us
  local copies, waits for them, and re-layouts: 11.7 us -> 15.8 us
  starting transfers between devices: 50.9 us -> 47.2 us
    unnamed x31 -> x39, local copies, waits for them, and re-layouts: 6.35 us -> 9.71 us
    pallas_call x2, Pallas kernels: 24 us -> 20.7 us  [attend(): pl.pallas_call(functools.partial(attend_kernel, part=part), out_shape=out...]
    pallas_call x1, Pallas kernels: 8.13 us -> 5.21 us  [experts(): pl.pallas_call(experts_kernel, in_specs=[pl.BlockSpec(memory_space=pltpu....]
    reduce_sum x1 -> x0, other arithmetic: 2.85 us -> none  [shards(): partial = jnp.sum(partial.astype(jnp.float32), axis=0).astype(jnp.bfloat16)]
  transfers between devices with their start and end apart: 14 -> 14, of which waited for: 9 -> 9; matrix products, arithmetic and copies ran while one was open for 4% -> 4% of each run, Pallas kernels for 12% -> 11%
where the time goes in v5:
time: 226 us; the launch traced here: 225 us
  waiting for transfers between devices  60.6 us (27%)
  blocking collectives  49.9 us (22%)
  starting transfers between devices  47.2 us (21%)
  Pallas kernels  42 us (19%)
  local copies, waits for them, and re-layouts  15.8 us (7%)
  other arithmetic  6.73 us (3%)
    all_to_all x3, blocking collectives, exchange(): lax.all_to_all(array, ALL, 0, 0, tiled=True, axis_index_groups=groups)  49.9 us
    all_to_all x5, waiting for transfers between devices, exchange(): lax.all_to_all(array, ALL, 0, 0, tiled=True, axis_index_groups=groups)  29.3 us
    all_to_all x5, starting transfers between devices, exchange(): lax.all_to_all(array, ALL, 0, 0, tiled=True, axis_index_groups=groups)  20.9 us
    pallas_call x2, Pallas kernels, attend(): pl.pallas_call(functools.partial(attend_kernel, part=part), out_shape=out...  20.7 us
    pallas_call x2, Pallas kernels, project(): pl.pallas_call(project_kernel, in_specs=[pl.BlockSpec(memory_space=pltpu....  13.8 us
    all_to_all x1, waiting for transfers between devices, shards(): arrived = lax.all_to_all(rows, ALL, 0, 0, tiled=True)  10.9 us
    ppermute x4, waiting for transfers between devices, ring(): return lax.ppermute(array, 'y', [(i, (i + step) % 4) for i in range(4)])  10.4 us
    unnamed x39, local copies, waits for them, and re-layouts  9.71 us
  transfers between devices with their start and end apart: 14, of which 9 were waited for; matrix products, arithmetic and copies ran while one was open for 4% of the time, Pallas kernels for 11%

profile of v5, /device:TPU:1, one launch (start us, length us, event | category | flops | bytes accessed | tf_op | source)
XLA Modules:
  0.0 225.2 jit_solution(16177334792622338343)
XLA Ops:
  0.0 1.0 copy-done.4
  1.1 1.0 copy-done.5
  2.1 1.0 copy-done.6
  3.4 17.5 %all_to_all.55.got.q = bf16[4,3,512,128]{3,2,1,0:T(8,128)(2,1)S(1)} all-to-all(bf16[4,3,512,128]{3,2,1,0:T(8,128)(2,1)S(1)} %pack_heads.1), channel_id=1, replica_groups={{0,32,64,96},{1,9,17,25},{8,40,72,104},{33,41,49,57},{16,48,80,112},{65..., dimensions={0} | all-to-all | bytes 3145728 | tf_op jit(solution)/shard_map/all_to_all | solution.py:51
  21.4 23.0 %all_to_all.56 = bf16[4,2,1280,128]{3,2,1,0:T(8,128)(2,1)S(1)} all-to-all(bf16[4,2,1280,128]{3,2,1,0:T(8,128)(2,1)S(1)} %get-tuple-element.22), channel_id=1, replica_groups={{0,8,16,24},{1,33,65,97},{32,40,48,56},{9,41,73,105},{64,72,80,88},{17,..., dimensions={0} | all-to-all | bytes 5242880 | tf_op jit(solution)/shard_map/all_to_all | solution.py:51
  44.4 4.6 %all-to-all-start.2 = ((bf16[4,2,1024,128]{3,2,1,0:T(8,128)(2,1)}), bf16[4,2,1024,128]{3,2,1,0:T(8,128)(2,1)}, u32[]{:S(2)}, u32[]{:S(2)}) async-start(bf16[4,2,1024,128]{3,2,1,0:T(8,128)(2,1)} %copy-done.2), calls=%async_computation.2 | async-start | bytes 4194304 | tf_op jit(solution)/shard_map/all_to_all | solution.py:51
  49.0 0.6 reduce_sum.36
  50.6 9.0 %attend.2 = (f32[4,1,512]{2,1,0:T(1,128)S(1)}, f32[4,1,512]{2,1,0:T(1,128)S(1)}, f32[4,128,512]{2,1,0:T(8,128)S(1)}, bf16[4,128,512]{2,1,0:T(8,128)(2,1)S(1)}) custom-call(s32[51]{0:T(128)S(1)} %concatenate.17.tab, bf16[8,1280,128]{2,1,0:T(8,128)(2,1)S(1)} %bitcast.73), custom_call_target="tpu_custom_call" | custom-call | flops 6000000000 | bytes 4000000 | tf_op jit(solution)/shard_map/attend/pallas_call | solution.py:235
  59.6 1.0 copy-done.7
  60.6 0.8 copy-done.9
  61.4 3.3 %all-to-all-done.2 = bf16[4,2,1024,128]{3,2,1,0:T(8,128)(2,1)} async-done(((bf16[4,2,1024,128]{3,2,1,0:T(8,128)(2,1)}), bf16[4,2,1024,128]{3,2,1,0:T(8,128)(2,1)}, u32[]{:S(2)}, u32[]{:S(2)}) %all-to-all-start.2) | async-done | bytes 2097184 | tf_op jit(solution)/shard_map/all_to_all | solution.py:51
  64.7 1.2 copy-done.8
  65.9 1.0 copy-done.10
  67.0 11.7 %attend.3 = bf16[16,128,128]{2,1,0:T(8,128)(2,1)} custom-call(s32[51]{0:T(128)S(1)} %concatenate.17.tab, bf16[8,1024,128]{2,1,0:T(8,128)(2,1)} %bitcast.5.r, f32[4,1,512]{2,1,0:T(1,128)S(1)} %get-tuple-element.26.refs_0_, f32[4,1,512]{2,1,0:T(1,128)S(1)} %get-tuple-element.27.refs_1_, f32[4,128,512]{2,1,0:T(8,128)S(1)} %copy-done.8, ...), custom_call_target="tpu_custom_call" | custom-call | flops 6000000000 | bytes 4000000 | tf_op jit(solution)/shard_map/attend/pallas_call | solution.py:235
  78.6 3.6 %all-to-all-start.3 = ((bf16[16,128,128]{2,1,0:T(8,128)(2,1)}), bf16[16,128,128]{2,1,0:T(8,128)(2,1)S(1)}, u32[]{:S(2)}, u32[]{:S(2)}) async-start(bf16[16,128,128]{2,1,0:T(8,128)(2,1)} %attend.3), calls=%async_computation.3 | async-start | bytes 1048576 | tf_op jit(solution)/shard_map/all_to_all | solution.py:51
  83.1 8.2 %all-to-all-done.3 = bf16[16,128,128]{2,1,0:T(8,128)(2,1)S(1)} async-done(((bf16[16,128,128]{2,1,0:T(8,128)(2,1)}), bf16[16,128,128]{2,1,0:T(8,128)(2,1)S(1)}, u32[]{:S(2)}, u32[]{:S(2)}) %all-to-all-start.3) | async-done | bytes 524320 | tf_op jit(solution)/shard_map/all_to_all | solution.py:51
  92.0 0.9 broadcast_in_dim.10
  92.9 4.2 %all-to-all-start.4 = ((bf16[4,144,512]{2,1,0:T(8,128)(2,1)}), bf16[4,144,512]{2,1,0:T(8,128)(2,1)S(1)}, u32[]{:S(2)}, u32[]{:S(2)}) async-start(bf16[4,144,512]{2,1,0:T(8,128)(2,1)} %broadcast_in_dim.10), calls=%async_computation.4 | async-start | bytes 1179648 | tf_op jit(solution)/shard_map/all_to_all | solution.py:447
  97.1 7.3 %all-to-all-done.4.mine = bf16[4,144,512]{2,1,0:T(8,128)(2,1)S(1)} async-done(((bf16[4,144,512]{2,1,0:T(8,128)(2,1)}), bf16[4,144,512]{2,1,0:T(8,128)(2,1)S(1)}, u32[]{:S(2)}, u32[]{:S(2)}) %all-to-all-start.4) | async-done | bytes 589856 | tf_op jit(solution)/shard_map/all_to_all | solution.py:447
  104.4 4.8 %collective-permute-start = (bf16[4,144,512]{2,1,0:T(8,128)(2,1)S(1)}, bf16[4,144,512]{2,1,0:T(8,128)(2,1)S(1)}, u32[]{:S(2)}, u32[]{:S(2)}) collective-permute-start(bf16[4,144,512]{2,1,0:T(8,128)(2,1)S(1)} %all-to-all-done.4.mine), channel_id=1, source_target_pairs={{0,1},{1,0},{2,3},{3,2},{4,5},{5,4},{6,7},{7,6},{8,9},{9,8},{10,11... | collective-permute-start | bytes 1769480 | tf_op jit(solution)/shard_map/ppermute | solution.py:374
  109.5 0.9 copy.40
  110.9 5.0 %project.2 = bf16[128,8,128]{2,1,0:T(8,128)(2,1)} custom-call(s32[8]{0:T(128)S(1)} %pad_add_fusion.1.order, bf16[4,144,512]{2,1,0:T(8,128)(2,1)S(1)} %all-to-all-done.4.mine, bf16[4,144,512]{2,1,0:T(8,128)(2,1)S(1)} %collective-permute-done.theirs, bf16[4096,1024]{1,0:T(8,128)(2,1)} %w.3, bf16[128,1024]{1,0:T(8,128)(2,1)S(1)} %convolution_convert_fusion.1.base), custom_call_target="tpu_custom_call" | custom-call | flops 1073741824 | bytes 9961472 | tf_op jit(solution)/shard_map/project/pallas_call | solution.py:280
  115.9 3.8 %all-to-all-start.5 = ((bf16[128,8,128]{2,1,0:T(8,128)(2,1)}), bf16[128,8,128]{2,1,0:T(8,128)(2,1)S(1)}, u32[]{:S(2)}, u32[]{:S(2)}) async-start(bf16[128,8,128]{2,1,0:T(8,128)(2,1)} %project.2), calls=%async_computation.5 | async-start | bytes 524288 | tf_op jit(solution)/shard_map/all_to_all | solution.py:459
  120.0 10.9 %all-to-all-done.5 = bf16[128,8,128]{2,1,0:T(8,128)(2,1)S(1)} async-done(((bf16[128,8,128]{2,1,0:T(8,128)(2,1)}), bf16[128,8,128]{2,1,0:T(8,128)(2,1)S(1)}, u32[]{:S(2)}, u32[]{:S(2)}) %all-to-all-start.5) | async-done | bytes 262176 | tf_op jit(solution)/shard_map/all_to_all | solution.py:459
  131.6 9.4 %all_to_all.57 = bf16[4,8,8192]{2,1,0:T(8,128)(2,1)S(1)} all-to-all(bf16[4,8,8192]{2,1,0:T(8,128)(2,1)S(1)} %broadcast_in_dim.11), channel_id=1, replica_groups={{0,32,64,96},{1,9,17,25},{8,40,72,104},{33,41,49,57},{16,48,80,112},{65..., dimensions={0} | all-to-all | bytes 1048576 | tf_op jit(solution)/shard_map/all_to_all | solution.py:51
  141.0 1.6 broadcast_in_dim.13
  142.5 3.6 %all-to-all-start.7 = ((bf16[4,32,8192]{2,1,0:T(8,128)(2,1)}), bf16[4,32,8192]{2,1,0:T(8,128)(2,1)S(1)}, u32[]{:S(2)}, u32[]{:S(2)}) async-start(bf16[4,32,8192]{2,1,0:T(8,128)(2,1)} %broadcast_in_dim.13), calls=%async_computation.7 | async-start | bytes 4194304 | tf_op jit(solution)/shard_map/all_to_all | solution.py:51
  146.2 1.4 collective-permute-start.2
  147.7 10.4 %collective-permute-done.2 = bf16[512,512]{1,0:T(8,128)(2,1)S(1)} collective-permute-done((bf16[512,512]{1,0:T(8,128)(2,1)}, bf16[512,512]{1,0:T(8,128)(2,1)S(1)}, u32[]{:S(2)}, u32[]{:S(2)}) %collective-permute-start.2) | collective-permute-done | bytes 524320 | tf_op jit(solution)/shard_map/ppermute | solution.py:378
  158.1 0.8 slice.44
  158.8 3.0 %collective-permute-start.4 = (bf16[256,512]{1,0:T(8,128)(2,1)}, bf16[256,512]{1,0:T(8,128)(2,1)}, u32[]{:S(2)}, u32[]{:S(2)}) collective-permute-start(bf16[256,512]{1,0:T(8,128)(2,1)} %slice.44), channel_id=1, source_target_pairs={{0,6},{2,0},{4,2},{6,4},{1,7},{3,1},{5,3},{7,5},{8,14},{10,8},{12,... | collective-permute-start | bytes 786440 | tf_op jit(solution)/shard_map/ppermute | solution.py:378
  161.9 0.8 slice.43
  162.8 5.2 %experts.1 = bf16[128,8192]{1,0:T(8,128)(2,1)S(1)} custom-call(bf16[128,8192]{1,0:T(8,128)(2,1)S(1)} %bitcast.71, bf16[1,8192,256]{2,1,0:T(8,128)(2,1)} %gate.1, bf16[1,8192,256]{2,1,0:T(8,128)(2,1)} %up.1, bf16[1,256,8192]{2,1,0:T(8,128)(2,1)} %down.1), custom_call_target="tpu_custom_call" | custom-call | flops 1610000000 | bytes 16800000 | tf_op jit(solution)/shard_map/experts/pallas_call | solution.py:334
  168.0 1.4 copy-done.1
  169.4 5.6 %all-to-all-start.8 = ((bf16[4,32,8192]{2,1,0:T(8,128)(2,1)}), bf16[4,32,8192]{2,1,0:T(8,128)(2,1)S(1)}, u32[]{:S(2)}, u32[]{:S(2)}) async-start(bf16[4,32,8192]{2,1,0:T(8,128)(2,1)} %bitcast.72), calls=%async_computation.8 | async-start | bytes 4194304 | tf_op jit(solution)/shard_map/all_to_all | solution.py:51
  175.0 1.1 maximum_bitcast_fusion
  176.1 2.9 %pad_maximum_fusion.mine = bf16[4,512,512]{2,1,0:T(8,128)(2,1)} fusion(bf16[1,512,512]{2,1,0:T(8,128)(2,1)S(1)} %maximum_bitcast_fusion, bf16[1,512,512]{2,1,0:T(8,128)(2,1)} %bitcast.81, bf16[1,512,512]{2,1,0:T(8,128)(2,1)} %bitcast.82, bf16[1,512,512]{2,1,0:T(8,128)(2,1)} %bitcast.80), kind=kLoop, calls=%fused_computation.1 | loop fusion | flops 3145728 | bytes 4194304 | tf_op jit(solution)/shard_map/stack | solution.py:464
  179.0 0.5 collective-permute-start.5
  179.5 11.1 %all-to-all-done.8.parts = bf16[4,32,8192]{2,1,0:T(8,128)(2,1)S(1)} async-done(((bf16[4,32,8192]{2,1,0:T(8,128)(2,1)}), bf16[4,32,8192]{2,1,0:T(8,128)(2,1)S(1)}, u32[]{:S(2)}, u32[]{:S(2)}) %all-to-all-start.8) | async-done | bytes 2097184 | tf_op jit(solution)/shard_map/all_to_all | solution.py:51
  190.6 1.6 add.183
  192.3 3.5 %all-to-all-start.9 = ((bf16[4,8,8192]{2,1,0:T(8,128)(2,1)}), bf16[4,8,8192]{2,1,0:T(8,128)(2,1)S(1)}, u32[]{:S(2)}, u32[]{:S(2)}) async-start(bf16[4,8,8192]{2,1,0:T(8,128)(2,1)} %bitcast.20), calls=%async_computation.9 | async-start | bytes 1048576 | tf_op jit(solution)/shard_map/all_to_all | solution.py:51
  196.0 6.6 %all-to-all-done.9 = bf16[4,8,8192]{2,1,0:T(8,128)(2,1)S(1)} async-done(((bf16[4,8,8192]{2,1,0:T(8,128)(2,1)}), bf16[4,8,8192]{2,1,0:T(8,128)(2,1)S(1)}, u32[]{:S(2)}, u32[]{:S(2)}) %all-to-all-start.9) | async-done | bytes 524320 | tf_op jit(solution)/shard_map/all_to_all | solution.py:51
  203.1 0.8 reshape.114
  203.9 8.4 %all-to-all-start.10 = ((bf16[128,8,128]{2,1,0:T(8,128)(2,1)}), bf16[128,8,128]{2,1,0:T(8,128)(2,1)S(1)}, u32[]{:S(2)}, u32[]{:S(2)}) async-start(bf16[128,8,128]{2,1,0:T(8,128)(2,1)} %reshape.114), calls=%async_computation.10 | async-start | bytes 524288 | tf_op jit(solution)/shard_map/all_to_all | solution.py:490
  212.3 8.8 %project.3 = bf16[512,1024]{1,0:T(8,128)(2,1)S(1)} custom-call(s32[8]{0:T(128)S(1)} %pad_add_fusion.order, bf16[4,512,512]{2,1,0:T(8,128)(2,1)} %pad_maximum_fusion.mine, bf16[4,512,512]{2,1,0:T(8,128)(2,1)} %collective-permute-done.5.theirs, bf16[4096,1024]{1,0:T(8,128)(2,1)} %w.3, bf16[512,1024]{1,0:T(8,128)(2,1)S(1)} %copy-done.3), custom_call_target="tpu_custom_call" | custom-call | flops 4294967296 | bytes 14680064 | tf_op jit(solution)/shard_map/project/pallas_call | solution.py:280
  221.1 2.3 %all-to-all-done.10 = bf16[128,8,128]{2,1,0:T(8,128)(2,1)S(1)} async-done(((bf16[128,8,128]{2,1,0:T(8,128)(2,1)}), bf16[128,8,128]{2,1,0:T(8,128)(2,1)S(1)}, u32[]{:S(2)}, u32[]{:S(2)}) %all-to-all-start.10) | async-done | bytes 262176 | tf_op jit(solution)/shard_map/all_to_all | solution.py:490
  223.4 0.5 fusion.4
  223.9 1.4 add_convert_fusion
  (84 shorter events, 5.2 us)
Async XLA Ops:
  0.0 195.8 %copy-start = (bf16[8192,1]{0,1:T(2,128)(2,1)S(1)}, bf16[8192,1]{0,1:T(2,128)(2,1)}, u32[]{:S(2)}) copy-start(bf16[8192,1]{0,1:T(2,128)(2,1)} %param.22) | copy-start | bytes 49156
  0.0 1.0 copy-start.4
  1.1 1.0 copy-start.5
  2.1 1.0 copy-start.6
  21.3 23.0 %copy-start.2 = (bf16[4,2,1024,128]{3,2,1,0:T(8,128)(2,1)}, bf16[4,2,1024,128]{3,2,1,0:T(8,128)(2,1)S(1)}, u32[]{:S(2)}) copy-start(bf16[4,2,1024,128]{3,2,1,0:T(8,128)(2,1)S(1)} %get-tuple-element.24) | copy-start | bytes 6291460
  44.4 4.6 %copy-start.13 = (s32[8192]{0:T(1024)S(1)}, s32[8192]{0:T(1024)}, u32[]{:S(2)}) copy-start(s32[8192]{0:T(1024)} %param.18) | copy-start | bytes 98308
  44.4 5.3 %copy-start.15 = (s32[8,128]{1,0:T(8,128)S(1)}, s32[8,128]{1,0:T(8,128)}, u32[]{:S(2)}) copy-start(s32[8,128]{1,0:T(8,128)} %param.21) | copy-start | bytes 12292
  44.4 6.2 %copy-start.14 = (f32[2,1024]{1,0:T(2,128)S(1)}, f32[2,1024]{1,0:T(2,128)}, u32[]{:S(2)}) copy-start(f32[2,1024]{1,0:T(2,128)} %param.20) | copy-start | bytes 24580
  44.4 20.3 %all-to-all-start.2 = ((bf16[4,2,1024,128]{3,2,1,0:T(8,128)(2,1)}), bf16[4,2,1024,128]{3,2,1,0:T(8,128)(2,1)}, u32[]{:S(2)}, u32[]{:S(2)}) async-start(bf16[4,2,1024,128]{3,2,1,0:T(8,128)(2,1)} %copy-done.2), calls=%async_computation.2 | async-start | bytes 4194304 | tf_op jit(solution)/shard_map/all_to_all | solution.py:51
  59.6 1.0 copy-start.7
  60.6 0.8 copy-start.9
  64.7 1.2 copy-start.8
  65.9 1.0 copy-start.10
  67.0 15.8 %copy-start.3 = (bf16[512,1024]{1,0:T(8,128)(2,1)S(1)}, bf16[512,1024]{1,0:T(8,128)(2,1)}, u32[]{:S(2)}) copy-start(bf16[512,1024]{1,0:T(8,128)(2,1)} %base.1) | copy-start | bytes 3145732
  78.6 12.7 %all-to-all-start.3 = ((bf16[16,128,128]{2,1,0:T(8,128)(2,1)}), bf16[16,128,128]{2,1,0:T(8,128)(2,1)S(1)}, u32[]{:S(2)}, u32[]{:S(2)}) async-start(bf16[16,128,128]{2,1,0:T(8,128)(2,1)} %attend.3), calls=%async_computation.3 | async-start | bytes 1048576 | tf_op jit(solution)/shard_map/all_to_all | solution.py:51
  92.9 11.5 %all-to-all-start.4 = ((bf16[4,144,512]{2,1,0:T(8,128)(2,1)}), bf16[4,144,512]{2,1,0:T(8,128)(2,1)S(1)}, u32[]{:S(2)}, u32[]{:S(2)}) async-start(bf16[4,144,512]{2,1,0:T(8,128)(2,1)} %broadcast_in_dim.10), calls=%async_computation.4 | async-start | bytes 1179648 | tf_op jit(solution)/shard_map/all_to_all | solution.py:447
  104.4 6.5 %collective-permute-start = (bf16[4,144,512]{2,1,0:T(8,128)(2,1)S(1)}, bf16[4,144,512]{2,1,0:T(8,128)(2,1)S(1)}, u32[]{:S(2)}, u32[]{:S(2)}) collective-permute-start(bf16[4,144,512]{2,1,0:T(8,128)(2,1)S(1)} %all-to-all-done.4.mine), channel_id=1, source_target_pairs={{0,1},{1,0},{2,3},{3,2},{4,5},{5,4},{6,7},{7,6},{8,9},{9,8},{10,11... | collective-permute-start | bytes 1769480 | tf_op jit(solution)/shard_map/ppermute | solution.py:374
  115.9 15.0 %all-to-all-start.5 = ((bf16[128,8,128]{2,1,0:T(8,128)(2,1)}), bf16[128,8,128]{2,1,0:T(8,128)(2,1)S(1)}, u32[]{:S(2)}, u32[]{:S(2)}) async-start(bf16[128,8,128]{2,1,0:T(8,128)(2,1)} %project.2), calls=%async_computation.5 | async-start | bytes 524288 | tf_op jit(solution)/shard_map/all_to_all | solution.py:459
  142.5 20.3 %all-to-all-start.7 = ((bf16[4,32,8192]{2,1,0:T(8,128)(2,1)}), bf16[4,32,8192]{2,1,0:T(8,128)(2,1)S(1)}, u32[]{:S(2)}, u32[]{:S(2)}) async-start(bf16[4,32,8192]{2,1,0:T(8,128)(2,1)} %broadcast_in_dim.13), calls=%async_computation.7 | async-start | bytes 4194304 | tf_op jit(solution)/shard_map/all_to_all | solution.py:51
  146.2 11.9 %collective-permute-start.2 = (bf16[512,512]{1,0:T(8,128)(2,1)}, bf16[512,512]{1,0:T(8,128)(2,1)S(1)}, u32[]{:S(2)}, u32[]{:S(2)}) collective-permute-start(bf16[512,512]{1,0:T(8,128)(2,1)} %bitcast.78), channel_id=1, source_target_pairs={{0,6},{2,0},{4,2},{6,4},{1,7},{3,1},{5,3},{7,5},{8,14},{10,8},{12,... | collective-permute-start | bytes 1572872 | tf_op jit(solution)/shard_map/ppermute | solution.py:378
  147.5 14.4 %collective-permute-start.1 = (bf16[512,512]{1,0:T(8,128)(2,1)}, bf16[512,512]{1,0:T(8,128)(2,1)S(1)}, u32[]{:S(2)}, u32[]{:S(2)}) collective-permute-start(bf16[512,512]{1,0:T(8,128)(2,1)} %bitcast.79), channel_id=1, source_target_pairs={{0,2},{2,4},{4,6},{6,0},{1,3},{3,5},{5,7},{7,1},{8,10},{10,12},{12... | collective-permute-start | bytes 1572872 | tf_op jit(solution)/shard_map/ppermute | solution.py:378
  158.0 4.6 %copy-start.11 = (bf16[512,512]{1,0:T(8,128)(2,1)}, bf16[512,512]{1,0:T(8,128)(2,1)S(1)}, u32[]{:S(2)}) copy-start(bf16[512,512]{1,0:T(8,128)(2,1)S(1)} %collective-permute-done.2) | copy-start | bytes 1572868
  158.8 16.1 %collective-permute-start.4 = (bf16[256,512]{1,0:T(8,128)(2,1)}, bf16[256,512]{1,0:T(8,128)(2,1)}, u32[]{:S(2)}, u32[]{:S(2)}) collective-permute-start(bf16[256,512]{1,0:T(8,128)(2,1)} %slice.44), channel_id=1, source_target_pairs={{0,6},{2,0},{4,2},{6,4},{1,7},{3,1},{5,3},{7,5},{8,14},{10,8},{12,... | collective-permute-start | bytes 786440 | tf_op jit(solution)/shard_map/ppermute | solution.py:378
  161.9 0.9 copy-start.12
  162.8 12.2 %collective-permute-start.3 = (bf16[256,512]{1,0:T(8,128)(2,1)}, bf16[256,512]{1,0:T(8,128)(2,1)}, u32[]{:S(2)}, u32[]{:S(2)}) collective-permute-start(bf16[256,512]{1,0:T(8,128)(2,1)} %slice.43), channel_id=1, source_target_pairs={{0,2},{2,4},{4,6},{6,0},{1,3},{3,5},{5,7},{7,1},{8,10},{10,12},{12... | collective-permute-start | bytes 786440 | tf_op jit(solution)/shard_map/ppermute | solution.py:378
  168.0 1.4 copy-start.1
  169.4 21.2 %all-to-all-start.8 = ((bf16[4,32,8192]{2,1,0:T(8,128)(2,1)}), bf16[4,32,8192]{2,1,0:T(8,128)(2,1)S(1)}, u32[]{:S(2)}, u32[]{:S(2)}) async-start(bf16[4,32,8192]{2,1,0:T(8,128)(2,1)} %bitcast.72), calls=%async_computation.8 | async-start | bytes 4194304 | tf_op jit(solution)/shard_map/all_to_all | solution.py:51
  176.1 3.5 %copy-start.16 = (s32[4]{0:T(128)S(1)}, s32[4]{0:T(128)}, u32[]{:S(2)}) copy-start(s32[4]{0:T(128)} %constant.144.clone) | copy-start | bytes 52
  179.0 24.1 %collective-permute-start.5 = (bf16[4,512,512]{2,1,0:T(8,128)(2,1)}, bf16[4,512,512]{2,1,0:T(8,128)(2,1)}, u32[]{:S(2)}, u32[]{:S(2)}) collective-permute-start(bf16[4,512,512]{2,1,0:T(8,128)(2,1)} %pad_maximum_fusion.mine), channel_id=1, source_target_pairs={{0,1},{1,0},{2,3},{3,2},{4,5},{5,4},{6,7},{7,6},{8,9},{9,8},{10,11... | collective-permute-start | bytes 6291464 | tf_op jit(solution)/shard_map/ppermute | solution.py:374
  192.3 10.4 %all-to-all-start.9 = ((bf16[4,8,8192]{2,1,0:T(8,128)(2,1)}), bf16[4,8,8192]{2,1,0:T(8,128)(2,1)S(1)}, u32[]{:S(2)}, u32[]{:S(2)}) async-start(bf16[4,8,8192]{2,1,0:T(8,128)(2,1)} %bitcast.20), calls=%async_computation.9 | async-start | bytes 1048576 | tf_op jit(solution)/shard_map/all_to_all | solution.py:51
  203.9 19.5 %all-to-all-start.10 = ((bf16[128,8,128]{2,1,0:T(8,128)(2,1)}), bf16[128,8,128]{2,1,0:T(8,128)(2,1)S(1)}, u32[]{:S(2)}, u32[]{:S(2)}) async-start(bf16[128,8,128]{2,1,0:T(8,128)(2,1)} %reshape.114), calls=%async_computation.10 | async-start | bytes 524288 | tf_op jit(solution)/shard_map/all_to_all | solution.py:490

commit v6 on v5

--- a/solution.py
+++ b/solution.py
@@ -14,7 +14,6 @@
 HD = 128
 TOK = 512
 BLOCKS = 16
-ROOM = 50 << 20
 ALL = ("z", "x", "y", "c")
 SEQ = ("z", "x")
 EXP = ("y", "c")
@@ -55,19 +54,40 @@
     return exchange(jnp.broadcast_to(array[None], (4, *array.shape)), groups)
 
 
-def pack_heads_kernel(q, k, v, o):
+def in_hbm(array):
+    return pltpu.with_memory_space_constraint(array, pltpu.HBM)
+
+
+def pack_heads_kernel(q, k, v, o, held, sem):
+    reads = []
     for h in range(4):
         for i, ref in enumerate((q, k, v)):
-            o[h, i] = ref[:, h * HD : (h + 1) * HD]
+            part = ref.at[:, pl.ds(h * HD, HD)]
+            reads.append(pltpu.make_async_copy(part, held.at[h, i], sem.at[0, h, i]))
+            reads[-1].start()
+    writes = []
+    for n, read in enumerate(reads):
+        read.wait()
+        h, i = n // 3, n % 3
+        writes.append(pltpu.make_async_copy(held.at[h, i], o.at[h, i], sem.at[1, h, i]))
+        writes[-1].start()
+    for write in writes:
+        write.wait()
 
 
 def pack_heads(queries, keys, values):
+    hbm = pl.BlockSpec(memory_space=pltpu.HBM)
     return pl.pallas_call(
         pack_heads_kernel,
-        out_shape=jax.ShapeDtypeStruct((4, 3, TOK, HD), jnp.bfloat16),
-        compiler_params=pltpu.CompilerParams(vmem_limit_bytes=ROOM),
+        in_specs=[hbm] * 3,
+        out_specs=hbm,
+        out_shape=pltpu.HBM((4, 3, TOK, HD), jnp.bfloat16),
+        scratch_shapes=[
+            pltpu.VMEM((4, 3, TOK, HD), jnp.bfloat16),
+            pltpu.SemaphoreType.DMA((2, 4, 3)),
+        ],
         name="pack_heads",
-    )(queries, keys, values)
+    )(in_hbm(queries), in_hbm(keys), in_hbm(values))
 
 
 def pack_parts_kernel(got, q, one, two):
@@ -108,17 +128,26 @@
 
 def attend_kernel(tab, r, *refs, part):
     if part == 0:
-        mo, lo_, acco, qto, vt, s0, s1, sums, m, l, sem = refs
+        mo, lo_, acco, qto, vt, s0, s1, sums, turned, m, l, sem = refs
         moves = [
-            pltpu.make_async_copy(sums.at[n], acco.at[n], sem.at[n]) for n in range(TILES)
+            (
+                pltpu.make_async_copy(turned.at[n], qto.at[n], sem.at[0, n]),
+                pltpu.make_async_copy(sums.at[n], acco.at[n], sem.at[1, n]),
+            )
+            for n in range(TILES)
         ]
     else:
-        mi, li, acci, qti, o, vt, s0, s1, sums, m, l, sem = refs
+        mi, li, acci, qti, o, vt, s0, s1, sums, turned, m, l, sem = refs
         moves = [
-            pltpu.make_async_copy(acci.at[n], sums.at[n], sem.at[n]) for n in range(TILES)
+            (
+                pltpu.make_async_copy(qti.at[n], turned.at[n], sem.at[0, n]),
+                pltpu.make_async_copy(acci.at[n], sums.at[n], sem.at[1, n]),
+            )
+            for n in range(TILES)
         ]
         for move in moves:
-            move.start()
+            move[0].start()
+            move[1].start()
     bound, sub, core = tab[48], tab[49], tab[50]
     start = jnp.where(core == 0, 4 * part, part)
 
@@ -133,8 +162,8 @@
     def tile(index):
         j = TILE * index
         acc = sums.at[index]
+        qt = turned.at[index]
         if part == 0:
-            qt = qto.at[index]
             for i in range(TILE):
                 here = r[tab[j + i], pl.ds(2 * TOK + 128 * tab[32 + j + i], 128), :]
                 qt[:, i * 128 : (i + 1) * 128] = here.T
@@ -142,10 +171,10 @@
             l[...] = jnp.zeros((1, QW), jnp.float32)
             acc[...] = jnp.zeros((HD, QW), jnp.float32)
         else:
-            qt = qti.at[index]
             m[...] = mi[index]
             l[...] = li[index]
-            moves[index].wait()
+            moves[index][0].wait()
+            moves[index][1].wait()
         first = j * TOK + sub * 128
         last = first + (TILE - 1) * TOK + 127
         qpos = first + (col // 128) * TOK + col % 128
@@ -206,7 +235,8 @@
         if part == 0:
             mo[index] = m[...]
             lo_[index] = l[...]
-            moves[index].start()
+            moves[index][0].start()
+            moves[index][1].start()
         else:
             out = (acc[...] / l[...]).T.astype(jnp.bfloat16)
             for i in range(TILE):
@@ -216,19 +246,21 @@
         tile(n)
     if part == 0:
         for move in moves:
-            move.wait()
+            move[0].wait()
+            move[1].wait()
 
 
 def attend(part, tab, received, *state):
     vmem = pl.BlockSpec(memory_space=pltpu.VMEM)
-    anywhere = pl.BlockSpec(memory_space=pl.ANY)
-    state_specs = [vmem, vmem, anywhere, vmem]
+    anywhere = pl.BlockSpec(memory_space=pltpu.HBM)
+    state_specs = [vmem, vmem, anywhere, anywhere]
+    state = [*state[:2], *(in_hbm(a) for a in state[2:])]
     if part == 0:
         out_shape = [
             jax.ShapeDtypeStruct((TILES, 1, QW), jnp.float32),
             jax.ShapeDtypeStruct((TILES, 1, QW), jnp.float32),
-            jax.ShapeDtypeStruct((TILES, HD, QW), jnp.float32),
-            jax.ShapeDtypeStruct((TILES, HD, QW), jnp.bfloat16),
+            pltpu.HBM((TILES, HD, QW), jnp.float32),
+            pltpu.HBM((TILES, HD, QW), jnp.bfloat16),
         ]
     else:
         out_shape = jax.ShapeDtypeStruct((BLOCKS, 128, HD), jnp.bfloat16)
@@ -242,9 +274,10 @@
             pltpu.VMEM((TOK, QW), jnp.float32),
             pltpu.VMEM((TOK, QW), jnp.float32),
             pltpu.VMEM((TILES, HD, QW), jnp.float32),
+            pltpu.VMEM((TILES, HD, QW), jnp.bfloat16),
             pltpu.VMEM((1, QW), jnp.float32),
             pltpu.VMEM((1, QW), jnp.float32),
-            pltpu.SemaphoreType.DMA((TILES,)),
+            pltpu.SemaphoreType.DMA((2, TILES)),
         ],
         compiler_params=pltpu.CompilerParams(vmem_limit_bytes=24 << 20),
         cost_estimate=pl.CostEstimate(
@@ -287,15 +320,15 @@
             pltpu.VMEM((rows, 1024), jnp.float32),
             pltpu.SemaphoreType.DMA((8,)),
         ],
-        compiler_params=pltpu.CompilerParams(vmem_limit_bytes=ROOM),
+        compiler_params=pltpu.CompilerParams(vmem_limit_bytes=24 << 20),
         cost_estimate=pl.CostEstimate(
             flops=rows * 8_388_608, bytes_accessed=8_388_608 + rows * 12_288, transcendentals=0
         ),
         name="project",
-    )(order, mine, theirs, w, base)
-
-
-def experts_kernel(piece, gate, up, down, o, gs, us, ds, sem):
+    )(order, mine, theirs, in_hbm(w), base)
+
+
+def experts_kernel(piece, gate, up, down, o, gs, us, ds, out, sem):
     wide = D // 4
     copies = []
     for k in range(4):
@@ -324,9 +357,14 @@
     inner = (jax.nn.silu(g) * u).astype(jnp.bfloat16)
     for k in range(4):
         last[k].wait()
-        o[:, k * wide : (k + 1) * wide] = jnp.dot(
-            inner, ds[k], preferred_element_type=jnp.float32
-        ).astype(o.dtype)
+        out[k] = jnp.dot(inner, ds[k], preferred_element_type=jnp.float32).astype(o.dtype)
+        written = pltpu.make_async_copy(
+            out.at[k], o.at[:, pl.ds(k * wide, wide)], sem.at[3, k]
+        )
+        written.start()
+        last[k] = written
+    for written in last:
+        written.wait()
 
 
 def experts(piece, w_gate, w_up, w_down):
@@ -334,20 +372,21 @@
     return pl.pallas_call(
         experts_kernel,
         in_specs=[pl.BlockSpec(memory_space=pltpu.VMEM)] + [hbm] * 3,
-        out_specs=pl.BlockSpec(memory_space=pltpu.VMEM),
-        out_shape=jax.ShapeDtypeStruct((128, D), jnp.bfloat16),
+        out_specs=hbm,
+        out_shape=pltpu.HBM((128, D), jnp.bfloat16),
         scratch_shapes=[
             pltpu.VMEM((4, D // 4, 256), jnp.bfloat16),
             pltpu.VMEM((4, D // 4, 256), jnp.bfloat16),
             pltpu.VMEM((4, 256, D // 4), jnp.bfloat16),
-            pltpu.SemaphoreType.DMA((3, 4)),
-        ],
-        compiler_params=pltpu.CompilerParams(vmem_limit_bytes=46 << 20),
+            pltpu.VMEM((4, 128, D // 4), jnp.bfloat16),
+            pltpu.SemaphoreType.DMA((4, 4)),
+        ],
+        compiler_params=pltpu.CompilerParams(vmem_limit_bytes=24 << 20),
         cost_estimate=pl.CostEstimate(
             flops=1_610_000_000, bytes_accessed=16_800_000, transcendentals=32_768
         ),
         name="experts",
-    )(piece, w_gate, w_up, w_down)
+    )(piece, in_hbm(w_gate), in_hbm(w_up), in_hbm(w_down))
 
 
 def add_kernel(parts, o):

time: 226 us -> 223 us (0.987)
  local copies, waits for them, and re-layouts: 15.8 us -> 7.27 us
  Pallas kernels: 42 us -> 47.1 us
    unnamed x39 -> x23, local copies, waits for them, and re-layouts: 9.71 us -> 1.16 us
  transfers between devices with their start and end apart: 14 -> 14, of which waited for: 9 -> 9; matrix products, arithmetic and copies ran while one was open for 4% -> 4% of each run, Pallas kernels for 11% -> 12%
where the time goes in v6:
time: 223 us; the launch traced here: 222 us
  waiting for transfers between devices  60.7 us (27%)
  blocking collectives  50.1 us (22%)
  Pallas kernels  47.1 us (21%)
  starting transfers between devices  46.9 us (21%)
  local copies, waits for them, and re-layouts  7.27 us (3%)
  other arithmetic  6.72 us (3%)
    all_to_all x3, blocking collectives, exchange(): lax.all_to_all(array, ALL, 0, 0, tiled=True, axis_index_groups=groups)  50.1 us
    all_to_all x5, waiting for transfers between devices, exchange(): lax.all_to_all(array, ALL, 0, 0, tiled=True, axis_index_groups=groups)  29.4 us
    pallas_call x2, Pallas kernels, attend(): pl.pallas_call(functools.partial(attend_kernel, part=part), out_shape=out...  22.7 us
    all_to_all x5, starting transfers between devices, exchange(): lax.all_to_all(array, ALL, 0, 0, tiled=True, axis_index_groups=groups)  20.9 us
    pallas_call x2, Pallas kernels, project(): pl.pallas_call(project_kernel, in_specs=[pl.BlockSpec(memory_space=pltpu....  13.8 us
    all_to_all x1, waiting for transfers between devices, shards(): arrived = lax.all_to_all(rows, ALL, 0, 0, tiled=True)  10.9 us
    ppermute x4, waiting for transfers between devices, ring(): return lax.ppermute(array, 'y', [(i, (i + step) % 4) for i in range(4)])  10.4 us
    all_to_all x1, starting transfers between devices, shards(): returned = lax.all_to_all(back.reshape(128, 8, 128), ALL, 0, 0, tiled=True)  8.44 us
  transfers between devices with their start and end apart: 14, of which 9 were waited for; matrix products, arithmetic and copies ran while one was open for 4% of the time, Pallas kernels for 12%

profile of v6, /device:TPU:1, one launch (start us, length us, event | category | flops | bytes accessed | tf_op | source)
XLA Modules:
  0.0 221.8 jit_solution(1230906716620478526)
XLA Ops:
  0.0 2.4 %pack_heads.1 = bf16[4,3,512,128]{3,2,1,0:T(8,128)(2,1)} custom-call(bf16[512,512]{1,0:T(8,128)(2,1)} %q.1, bf16[512,512]{1,0:T(8,128)(2,1)} %k.1, bf16[512,512]{1,0:T(8,128)(2,1)} %v.1), custom_call_target="tpu_custom_call" | custom-call | tf_op jit(solution)/shard_map/pack_heads/pallas_call | solution.py:80
  2.4 17.7 %all_to_all.55.got.q = bf16[4,3,512,128]{3,2,1,0:T(8,128)(2,1)S(1)} all-to-all(bf16[4,3,512,128]{3,2,1,0:T(8,128)(2,1)} %pack_heads.1), channel_id=1, replica_groups={{0,32,64,96},{1,9,17,25},{8,40,72,104},{33,41,49,57},{16,48,80,112},{65..., dimensions={0} | all-to-all | bytes 3145728 | tf_op jit(solution)/shard_map/all_to_all | solution.py:50
  20.1 0.4 pack_parts.1
  20.6 23.0 %all_to_all.56 = bf16[4,2,1280,128]{3,2,1,0:T(8,128)(2,1)S(1)} all-to-all(bf16[4,2,1280,128]{3,2,1,0:T(8,128)(2,1)S(1)} %get-tuple-element.22), channel_id=1, replica_groups={{0,8,16,24},{1,33,65,97},{32,40,48,56},{9,41,73,105},{64,72,80,88},{17,..., dimensions={0} | all-to-all | bytes 5242880 | tf_op jit(solution)/shard_map/all_to_all | solution.py:50
  43.6 4.6 %all-to-all-start.2 = ((bf16[4,2,1024,128]{3,2,1,0:T(8,128)(2,1)}), bf16[4,2,1024,128]{3,2,1,0:T(8,128)(2,1)}, u32[]{:S(2)}, u32[]{:S(2)}) async-start(bf16[4,2,1024,128]{3,2,1,0:T(8,128)(2,1)} %copy-done.1), calls=%async_computation.2 | async-start | bytes 4194304 | tf_op jit(solution)/shard_map/all_to_all | solution.py:50
  48.2 0.6 reduce_sum.36
  49.8 10.8 %attend.2 = (f32[4,1,512]{2,1,0:T(1,128)S(1)}, f32[4,1,512]{2,1,0:T(1,128)S(1)}, f32[4,128,512]{2,1,0:T(8,128)}, bf16[4,128,512]{2,1,0:T(8,128)(2,1)}) custom-call(s32[51]{0:T(128)S(1)} %concatenate.17.tab, bf16[8,1280,128]{2,1,0:T(8,128)(2,1)S(1)} %bitcast.72), custom_call_target="tpu_custom_call" | custom-call | flops 6000000000 | bytes 4000000 | tf_op jit(solution)/shard_map/attend/pallas_call | solution.py:267
  60.6 3.3 %all-to-all-done.2 = bf16[4,2,1024,128]{3,2,1,0:T(8,128)(2,1)} async-done(((bf16[4,2,1024,128]{3,2,1,0:T(8,128)(2,1)}), bf16[4,2,1024,128]{3,2,1,0:T(8,128)(2,1)}, u32[]{:S(2)}, u32[]{:S(2)}) %all-to-all-start.2) | async-done | bytes 2097184 | tf_op jit(solution)/shard_map/all_to_all | solution.py:50
  63.9 12.0 %attend.3 = bf16[16,128,128]{2,1,0:T(8,128)(2,1)} custom-call(s32[51]{0:T(128)S(1)} %concatenate.17.tab, bf16[8,1024,128]{2,1,0:T(8,128)(2,1)} %bitcast.5.r, f32[4,1,512]{2,1,0:T(1,128)S(1)} %get-tuple-element.26.refs_0_, f32[4,1,512]{2,1,0:T(1,128)S(1)} %get-tuple-element.27.refs_1_, f32[4,128,512]{2,1,0:T(8,128)} %get-tuple-element.28.refs_2_, ...), custom_call_target="tpu_custom_call" | custom-call | flops 6000000000 | bytes 4000000 | tf_op jit(solution)/shard_map/attend/pallas_call | solution.py:267
  75.9 3.6 %all-to-all-start.3 = ((bf16[16,128,128]{2,1,0:T(8,128)(2,1)}), bf16[16,128,128]{2,1,0:T(8,128)(2,1)S(1)}, u32[]{:S(2)}, u32[]{:S(2)}) async-start(bf16[16,128,128]{2,1,0:T(8,128)(2,1)} %attend.3), calls=%async_computation.3 | async-start | bytes 1048576 | tf_op jit(solution)/shard_map/all_to_all | solution.py:50
  80.0 0.4 convolution_convert_fusion.1.base
  80.4 8.4 %all-to-all-done.3 = bf16[16,128,128]{2,1,0:T(8,128)(2,1)S(1)} async-done(((bf16[16,128,128]{2,1,0:T(8,128)(2,1)}), bf16[16,128,128]{2,1,0:T(8,128)(2,1)S(1)}, u32[]{:S(2)}, u32[]{:S(2)}) %all-to-all-start.3) | async-done | bytes 524320 | tf_op jit(solution)/shard_map/all_to_all | solution.py:50
  88.7 0.4 copy.25
  89.2 0.2 convolution_convert_fusion.2
  89.4 0.9 broadcast_in_dim.10
  90.3 4.2 %all-to-all-start.4 = ((bf16[4,144,512]{2,1,0:T(8,128)(2,1)}), bf16[4,144,512]{2,1,0:T(8,128)(2,1)S(1)}, u32[]{:S(2)}, u32[]{:S(2)}) async-start(bf16[4,144,512]{2,1,0:T(8,128)(2,1)} %broadcast_in_dim.10), calls=%async_computation.4 | async-start | bytes 1179648 | tf_op jit(solution)/shard_map/all_to_all | solution.py:486
  94.5 7.3 %all-to-all-done.4.mine = bf16[4,144,512]{2,1,0:T(8,128)(2,1)S(1)} async-done(((bf16[4,144,512]{2,1,0:T(8,128)(2,1)}), bf16[4,144,512]{2,1,0:T(8,128)(2,1)S(1)}, u32[]{:S(2)}, u32[]{:S(2)}) %all-to-all-start.4) | async-done | bytes 589856 | tf_op jit(solution)/shard_map/all_to_all | solution.py:486
  101.8 4.5 %collective-permute-start = (bf16[4,144,512]{2,1,0:T(8,128)(2,1)S(1)}, bf16[4,144,512]{2,1,0:T(8,128)(2,1)S(1)}, u32[]{:S(2)}, u32[]{:S(2)}) collective-permute-start(bf16[4,144,512]{2,1,0:T(8,128)(2,1)S(1)} %all-to-all-done.4.mine), channel_id=1, source_target_pairs={{0,1},{1,0},{2,3},{3,2},{4,5},{5,4},{6,7},{7,6},{8,9},{9,8},{10,11... | collective-permute-start | bytes 1769480 | tf_op jit(solution)/shard_map/ppermute | solution.py:413
  106.5 0.9 copy.40
  107.5 0.4 collective-permute-done.theirs
  107.9 5.0 %project.2 = bf16[128,8,128]{2,1,0:T(8,128)(2,1)} custom-call(s32[8]{0:T(128)S(1)} %pad_add_fusion.1.order, bf16[4,144,512]{2,1,0:T(8,128)(2,1)S(1)} %all-to-all-done.4.mine, bf16[4,144,512]{2,1,0:T(8,128)(2,1)S(1)} %collective-permute-done.theirs, bf16[4096,1024]{1,0:T(8,128)(2,1)} %w.3, bf16[128,1024]{1,0:T(8,128)(2,1)S(1)} %convolution_convert_fusion.1.base), custom_call_target="tpu_custom_call" | custom-call | flops 1073741824 | bytes 9961472 | tf_op jit(solution)/shard_map/project/pallas_call | solution.py:313
  113.0 3.8 %all-to-all-start.5 = ((bf16[128,8,128]{2,1,0:T(8,128)(2,1)}), bf16[128,8,128]{2,1,0:T(8,128)(2,1)S(1)}, u32[]{:S(2)}, u32[]{:S(2)}) async-start(bf16[128,8,128]{2,1,0:T(8,128)(2,1)} %project.2), calls=%async_computation.5 | async-start | bytes 524288 | tf_op jit(solution)/shard_map/all_to_all | solution.py:498
  117.0 10.9 %all-to-all-done.5 = bf16[128,8,128]{2,1,0:T(8,128)(2,1)S(1)} async-done(((bf16[128,8,128]{2,1,0:T(8,128)(2,1)}), bf16[128,8,128]{2,1,0:T(8,128)(2,1)S(1)}, u32[]{:S(2)}, u32[]{:S(2)}) %all-to-all-start.5) | async-done | bytes 262176 | tf_op jit(solution)/shard_map/all_to_all | solution.py:498
  128.1 0.4 multiply_reduce_fusion
  128.6 9.4 %all_to_all.57 = bf16[4,8,8192]{2,1,0:T(8,128)(2,1)S(1)} all-to-all(bf16[4,8,8192]{2,1,0:T(8,128)(2,1)S(1)} %broadcast_in_dim.11), channel_id=1, replica_groups={{0,32,64,96},{1,9,17,25},{8,40,72,104},{33,41,49,57},{16,48,80,112},{65..., dimensions={0} | all-to-all | bytes 1048576 | tf_op jit(solution)/shard_map/all_to_all | solution.py:50
  138.0 1.5 broadcast_in_dim.13
  139.6 3.6 %all-to-all-start.7 = ((bf16[4,32,8192]{2,1,0:T(8,128)(2,1)}), bf16[4,32,8192]{2,1,0:T(8,128)(2,1)S(1)}, u32[]{:S(2)}, u32[]{:S(2)}) async-start(bf16[4,32,8192]{2,1,0:T(8,128)(2,1)} %broadcast_in_dim.13), calls=%async_computation.7 | async-start | bytes 4194304 | tf_op jit(solution)/shard_map/all_to_all | solution.py:50
  143.2 1.4 collective-permute-start.2
  144.7 10.4 %collective-permute-done.2 = bf16[512,512]{1,0:T(8,128)(2,1)S(1)} collective-permute-done((bf16[512,512]{1,0:T(8,128)(2,1)}, bf16[512,512]{1,0:T(8,128)(2,1)S(1)}, u32[]{:S(2)}, u32[]{:S(2)}) %collective-permute-start.2) | collective-permute-done | bytes 524320 | tf_op jit(solution)/shard_map/ppermute | solution.py:417
  155.1 0.8 slice.44
  155.9 3.0 %collective-permute-start.4 = (bf16[256,512]{1,0:T(8,128)(2,1)}, bf16[256,512]{1,0:T(8,128)(2,1)}, u32[]{:S(2)}, u32[]{:S(2)}) collective-permute-start(bf16[256,512]{1,0:T(8,128)(2,1)} %slice.44), channel_id=1, source_target_pairs={{0,6},{2,0},{4,2},{6,4},{1,7},{3,1},{5,3},{7,5},{8,14},{10,8},{12,... | collective-permute-start | bytes 786440 | tf_op jit(solution)/shard_map/ppermute | solution.py:417
  158.9 0.8 slice.43
  159.8 6.1 %experts.1 = bf16[128,8192]{1,0:T(8,128)(2,1)} custom-call(bf16[128,8192]{1,0:T(8,128)(2,1)S(1)} %bitcast.71, bf16[1,8192,256]{2,1,0:T(8,128)(2,1)} %gate.1, bf16[1,8192,256]{2,1,0:T(8,128)(2,1)} %up.1, bf16[1,256,8192]{2,1,0:T(8,128)(2,1)} %down.1), custom_call_target="tpu_custom_call" | custom-call | flops 1610000000 | bytes 16800000 | tf_op jit(solution)/shard_map/experts/pallas_call | solution.py:372
  165.9 5.6 %all-to-all-start.8 = ((bf16[4,32,8192]{2,1,0:T(8,128)(2,1)}), bf16[4,32,8192]{2,1,0:T(8,128)(2,1)S(1)}, u32[]{:S(2)}, u32[]{:S(2)}) async-start(bf16[4,32,8192]{2,1,0:T(8,128)(2,1)} %bitcast.73), calls=%async_computation.8 | async-start | bytes 4194304 | tf_op jit(solution)/shard_map/all_to_all | solution.py:50
  171.5 1.1 maximum_bitcast_fusion
  172.6 2.9 %pad_maximum_fusion.mine = bf16[4,512,512]{2,1,0:T(8,128)(2,1)} fusion(bf16[1,512,512]{2,1,0:T(8,128)(2,1)S(1)} %maximum_bitcast_fusion, bf16[1,512,512]{2,1,0:T(8,128)(2,1)} %bitcast.81, bf16[1,512,512]{2,1,0:T(8,128)(2,1)} %bitcast.82, bf16[1,512,512]{2,1,0:T(8,128)(2,1)} %bitcast.80), kind=kLoop, calls=%fused_computation.1 | loop fusion | flops 3145728 | bytes 4194304 | tf_op jit(solution)/shard_map/stack | solution.py:503
  175.5 0.5 collective-permute-start.5
  176.0 11.1 %all-to-all-done.8.parts = bf16[4,32,8192]{2,1,0:T(8,128)(2,1)S(1)} async-done(((bf16[4,32,8192]{2,1,0:T(8,128)(2,1)}), bf16[4,32,8192]{2,1,0:T(8,128)(2,1)S(1)}, u32[]{:S(2)}, u32[]{:S(2)}) %all-to-all-start.8) | async-done | bytes 2097184 | tf_op jit(solution)/shard_map/all_to_all | solution.py:50
  187.2 1.6 add.183
  188.8 3.5 %all-to-all-start.9 = ((bf16[4,8,8192]{2,1,0:T(8,128)(2,1)}), bf16[4,8,8192]{2,1,0:T(8,128)(2,1)S(1)}, u32[]{:S(2)}, u32[]{:S(2)}) async-start(bf16[4,8,8192]{2,1,0:T(8,128)(2,1)} %bitcast.20), calls=%async_computation.9 | async-start | bytes 1048576 | tf_op jit(solution)/shard_map/all_to_all | solution.py:50
  192.6 6.6 %all-to-all-done.9 = bf16[4,8,8192]{2,1,0:T(8,128)(2,1)S(1)} async-done(((bf16[4,8,8192]{2,1,0:T(8,128)(2,1)}), bf16[4,8,8192]{2,1,0:T(8,128)(2,1)S(1)}, u32[]{:S(2)}, u32[]{:S(2)}) %all-to-all-start.9) | async-done | bytes 524320 | tf_op jit(solution)/shard_map/all_to_all | solution.py:50
  199.3 0.3 convolution_convert_fusion
  199.6 0.8 reshape.114
  200.4 8.4 %all-to-all-start.10 = ((bf16[128,8,128]{2,1,0:T(8,128)(2,1)}), bf16[128,8,128]{2,1,0:T(8,128)(2,1)S(1)}, u32[]{:S(2)}, u32[]{:S(2)}) async-start(bf16[128,8,128]{2,1,0:T(8,128)(2,1)} %reshape.114), calls=%async_computation.10 | async-start | bytes 524288 | tf_op jit(solution)/shard_map/all_to_all | solution.py:529
  208.9 8.8 %project.3 = bf16[512,1024]{1,0:T(8,128)(2,1)S(1)} custom-call(s32[8]{0:T(128)S(1)} %pad_add_fusion.order, bf16[4,512,512]{2,1,0:T(8,128)(2,1)} %pad_maximum_fusion.mine, bf16[4,512,512]{2,1,0:T(8,128)(2,1)} %collective-permute-done.5.theirs, bf16[4096,1024]{1,0:T(8,128)(2,1)} %w.3, bf16[512,1024]{1,0:T(8,128)(2,1)S(1)} %copy-done.2), custom_call_target="tpu_custom_call" | custom-call | flops 4294967296 | bytes 14680064 | tf_op jit(solution)/shard_map/project/pallas_call | solution.py:313
  217.7 2.3 %all-to-all-done.10 = bf16[128,8,128]{2,1,0:T(8,128)(2,1)S(1)} async-done(((bf16[128,8,128]{2,1,0:T(8,128)(2,1)}), bf16[128,8,128]{2,1,0:T(8,128)(2,1)S(1)}, u32[]{:S(2)}, u32[]{:S(2)}) %all-to-all-start.10) | async-done | bytes 262176 | tf_op jit(solution)/shard_map/all_to_all | solution.py:529
  220.0 0.5 fusion.4
  220.4 1.4 add_convert_fusion
  (68 shorter events, 2.3 us)
Async XLA Ops:
  0.0 192.4 %copy-start = (bf16[8192,1]{0,1:T(2,128)(2,1)S(1)}, bf16[8192,1]{0,1:T(2,128)(2,1)}, u32[]{:S(2)}) copy-start(bf16[8192,1]{0,1:T(2,128)(2,1)} %param.22) | copy-start | bytes 49156
  20.5 23.0 %copy-start.1 = (bf16[4,2,1024,128]{3,2,1,0:T(8,128)(2,1)}, bf16[4,2,1024,128]{3,2,1,0:T(8,128)(2,1)S(1)}, u32[]{:S(2)}) copy-start(bf16[4,2,1024,128]{3,2,1,0:T(8,128)(2,1)S(1)} %get-tuple-element.24) | copy-start | bytes 6291460
  43.6 4.6 %copy-start.5 = (s32[8192]{0:T(1024)S(1)}, s32[8192]{0:T(1024)}, u32[]{:S(2)}) copy-start(s32[8192]{0:T(1024)} %param.18) | copy-start | bytes 98308
  43.6 5.3 %copy-start.7 = (s32[8,128]{1,0:T(8,128)S(1)}, s32[8,128]{1,0:T(8,128)}, u32[]{:S(2)}) copy-start(s32[8,128]{1,0:T(8,128)} %param.21) | copy-start | bytes 12292
  43.6 6.2 %copy-start.6 = (f32[2,1024]{1,0:T(2,128)S(1)}, f32[2,1024]{1,0:T(2,128)}, u32[]{:S(2)}) copy-start(f32[2,1024]{1,0:T(2,128)} %param.20) | copy-start | bytes 24580
  43.6 20.3 %all-to-all-start.2 = ((bf16[4,2,1024,128]{3,2,1,0:T(8,128)(2,1)}), bf16[4,2,1024,128]{3,2,1,0:T(8,128)(2,1)}, u32[]{:S(2)}, u32[]{:S(2)}) async-start(bf16[4,2,1024,128]{3,2,1,0:T(8,128)(2,1)} %copy-done.1), calls=%async_computation.2 | async-start | bytes 4194304 | tf_op jit(solution)/shard_map/all_to_all | solution.py:50
  63.9 16.1 %copy-start.2 = (bf16[512,1024]{1,0:T(8,128)(2,1)S(1)}, bf16[512,1024]{1,0:T(8,128)(2,1)}, u32[]{:S(2)}) copy-start(bf16[512,1024]{1,0:T(8,128)(2,1)} %base.1) | copy-start | bytes 3145732
  75.9 12.9 %all-to-all-start.3 = ((bf16[16,128,128]{2,1,0:T(8,128)(2,1)}), bf16[16,128,128]{2,1,0:T(8,128)(2,1)S(1)}, u32[]{:S(2)}, u32[]{:S(2)}) async-start(bf16[16,128,128]{2,1,0:T(8,128)(2,1)} %attend.3), calls=%async_computation.3 | async-start | bytes 1048576 | tf_op jit(solution)/shard_map/all_to_all | solution.py:50
  90.3 11.5 %all-to-all-start.4 = ((bf16[4,144,512]{2,1,0:T(8,128)(2,1)}), bf16[4,144,512]{2,1,0:T(8,128)(2,1)S(1)}, u32[]{:S(2)}, u32[]{:S(2)}) async-start(bf16[4,144,512]{2,1,0:T(8,128)(2,1)} %broadcast_in_dim.10), calls=%async_computation.4 | async-start | bytes 1179648 | tf_op jit(solution)/shard_map/all_to_all | solution.py:486
  101.8 6.1 %collective-permute-start = (bf16[4,144,512]{2,1,0:T(8,128)(2,1)S(1)}, bf16[4,144,512]{2,1,0:T(8,128)(2,1)S(1)}, u32[]{:S(2)}, u32[]{:S(2)}) collective-permute-start(bf16[4,144,512]{2,1,0:T(8,128)(2,1)S(1)} %all-to-all-done.4.mine), channel_id=1, source_target_pairs={{0,1},{1,0},{2,3},{3,2},{4,5},{5,4},{6,7},{7,6},{8,9},{9,8},{10,11... | collective-permute-start | bytes 1769480 | tf_op jit(solution)/shard_map/ppermute | solution.py:413
  113.0 15.0 %all-to-all-start.5 = ((bf16[128,8,128]{2,1,0:T(8,128)(2,1)}), bf16[128,8,128]{2,1,0:T(8,128)(2,1)S(1)}, u32[]{:S(2)}, u32[]{:S(2)}) async-start(bf16[128,8,128]{2,1,0:T(8,128)(2,1)} %project.2), calls=%async_computation.5 | async-start | bytes 524288 | tf_op jit(solution)/shard_map/all_to_all | solution.py:498
  139.6 20.2 %all-to-all-start.7 = ((bf16[4,32,8192]{2,1,0:T(8,128)(2,1)}), bf16[4,32,8192]{2,1,0:T(8,128)(2,1)S(1)}, u32[]{:S(2)}, u32[]{:S(2)}) async-start(bf16[4,32,8192]{2,1,0:T(8,128)(2,1)} %broadcast_in_dim.13), calls=%async_computation.7 | async-start | bytes 4194304 | tf_op jit(solution)/shard_map/all_to_all | solution.py:50
  143.2 11.9 %collective-permute-start.2 = (bf16[512,512]{1,0:T(8,128)(2,1)}, bf16[512,512]{1,0:T(8,128)(2,1)S(1)}, u32[]{:S(2)}, u32[]{:S(2)}) collective-permute-start(bf16[512,512]{1,0:T(8,128)(2,1)} %bitcast.78), channel_id=1, source_target_pairs={{0,6},{2,0},{4,2},{6,4},{1,7},{3,1},{5,3},{7,5},{8,14},{10,8},{12,... | collective-permute-start | bytes 1572872 | tf_op jit(solution)/shard_map/ppermute | solution.py:417
  144.5 14.4 %collective-permute-start.1 = (bf16[512,512]{1,0:T(8,128)(2,1)}, bf16[512,512]{1,0:T(8,128)(2,1)S(1)}, u32[]{:S(2)}, u32[]{:S(2)}) collective-permute-start(bf16[512,512]{1,0:T(8,128)(2,1)} %bitcast.79), channel_id=1, source_target_pairs={{0,2},{2,4},{4,6},{6,0},{1,3},{3,5},{5,7},{7,1},{8,10},{10,12},{12... | collective-permute-start | bytes 1572872 | tf_op jit(solution)/shard_map/ppermute | solution.py:417
  155.1 4.6 %copy-start.3 = (bf16[512,512]{1,0:T(8,128)(2,1)}, bf16[512,512]{1,0:T(8,128)(2,1)S(1)}, u32[]{:S(2)}) copy-start(bf16[512,512]{1,0:T(8,128)(2,1)S(1)} %collective-permute-done.2) | copy-start | bytes 1572868
  155.9 15.7 %collective-permute-start.4 = (bf16[256,512]{1,0:T(8,128)(2,1)}, bf16[256,512]{1,0:T(8,128)(2,1)}, u32[]{:S(2)}, u32[]{:S(2)}) collective-permute-start(bf16[256,512]{1,0:T(8,128)(2,1)} %slice.44), channel_id=1, source_target_pairs={{0,6},{2,0},{4,2},{6,4},{1,7},{3,1},{5,3},{7,5},{8,14},{10,8},{12,... | collective-permute-start | bytes 786440 | tf_op jit(solution)/shard_map/ppermute | solution.py:417
  158.9 0.9 copy-start.4
  159.8 11.7 %collective-permute-start.3 = (bf16[256,512]{1,0:T(8,128)(2,1)}, bf16[256,512]{1,0:T(8,128)(2,1)}, u32[]{:S(2)}, u32[]{:S(2)}) collective-permute-start(bf16[256,512]{1,0:T(8,128)(2,1)} %slice.43), channel_id=1, source_target_pairs={{0,2},{2,4},{4,6},{6,0},{1,3},{3,5},{5,7},{7,1},{8,10},{10,12},{12... | collective-permute-start | bytes 786440 | tf_op jit(solution)/shard_map/ppermute | solution.py:417
  165.9 21.3 %all-to-all-start.8 = ((bf16[4,32,8192]{2,1,0:T(8,128)(2,1)}), bf16[4,32,8192]{2,1,0:T(8,128)(2,1)S(1)}, u32[]{:S(2)}, u32[]{:S(2)}) async-start(bf16[4,32,8192]{2,1,0:T(8,128)(2,1)} %bitcast.73), calls=%async_computation.8 | async-start | bytes 4194304 | tf_op jit(solution)/shard_map/all_to_all | solution.py:50
  172.6 3.4 %copy-start.8 = (s32[4]{0:T(128)S(1)}, s32[4]{0:T(128)}, u32[]{:S(2)}) copy-start(s32[4]{0:T(128)} %constant.144.clone) | copy-start | bytes 52
  175.5 24.1 %collective-permute-start.5 = (bf16[4,512,512]{2,1,0:T(8,128)(2,1)}, bf16[4,512,512]{2,1,0:T(8,128)(2,1)}, u32[]{:S(2)}, u32[]{:S(2)}) collective-permute-start(bf16[4,512,512]{2,1,0:T(8,128)(2,1)} %pad_maximum_fusion.mine), channel_id=1, source_target_pairs={{0,1},{1,0},{2,3},{3,2},{4,5},{5,4},{6,7},{7,6},{8,9},{9,8},{10,11... | collective-permute-start | bytes 6291464 | tf_op jit(solution)/shard_map/ppermute | solution.py:413
  188.8 10.4 %all-to-all-start.9 = ((bf16[4,8,8192]{2,1,0:T(8,128)(2,1)}), bf16[4,8,8192]{2,1,0:T(8,128)(2,1)S(1)}, u32[]{:S(2)}, u32[]{:S(2)}) async-start(bf16[4,8,8192]{2,1,0:T(8,128)(2,1)} %bitcast.20), calls=%async_computation.9 | async-start | bytes 1048576 | tf_op jit(solution)/shard_map/all_to_all | solution.py:50
  200.4 19.5 %all-to-all-start.10 = ((bf16[128,8,128]{2,1,0:T(8,128)(2,1)}), bf16[128,8,128]{2,1,0:T(8,128)(2,1)S(1)}, u32[]{:S(2)}, u32[]{:S(2)}) async-start(bf16[128,8,128]{2,1,0:T(8,128)(2,1)} %reshape.114), calls=%async_computation.10 | async-start | bytes 524288 | tf_op jit(solution)/shard_map/all_to_all | solution.py:529

commit v7 on v6

--- a/solution.py
+++ b/solution.py
@@ -137,7 +137,11 @@
             for n in range(TILES)
         ]
     else:
-        mi, li, acci, qti, o, vt, s0, s1, sums, turned, m, l, sem = refs
+        mi, li, acci, qti, o, vt, s0, s1, sums, turned, m, l, sem, held, got = refs
+        parts = [pltpu.make_async_copy(r.at[n], held.at[n], got.at[n]) for n in range(8)]
+        for part_copy in parts:
+            part_copy.start()
+        r = held
         moves = [
             (
                 pltpu.make_async_copy(qti.at[n], turned.at[n], sem.at[0, n]),
@@ -151,11 +155,10 @@
     bound, sub, core = tab[48], tab[49], tab[50]
     start = jnp.where(core == 0, 4 * part, part)
 
-    def turn(t, carry):
+    for t in range(8):
+        if part == 1:
+            parts[t].wait()
         vt[t] = r[t, TOK : 2 * TOK, :].T
-        return carry
-
-    lax.fori_loop(0, 8, turn, 0)
     col = lax.broadcasted_iota(jnp.int32, (1, QW), 1)
     row = lax.broadcasted_iota(jnp.int32, (TOK, 1), 0)
 
@@ -264,10 +267,12 @@
         ]
     else:
         out_shape = jax.ShapeDtypeStruct((BLOCKS, 128, HD), jnp.bfloat16)
+    second = [pltpu.VMEM((8, 1024, HD), jnp.bfloat16), pltpu.SemaphoreType.DMA((8,))] * part
     return pl.pallas_call(
         functools.partial(attend_kernel, part=part),
         out_shape=out_shape,
-        in_specs=[pl.BlockSpec(memory_space=pltpu.SMEM), vmem] + state_specs[: len(state)],
+        in_specs=[pl.BlockSpec(memory_space=pltpu.SMEM), anywhere if part else vmem]
+        + state_specs[: len(state)],
         out_specs=state_specs if part == 0 else vmem,
         scratch_shapes=[
             pltpu.VMEM((8, HD, TOK), jnp.bfloat16),
@@ -278,13 +283,14 @@
             pltpu.VMEM((1, QW), jnp.float32),
             pltpu.VMEM((1, QW), jnp.float32),
             pltpu.SemaphoreType.DMA((2, TILES)),
-        ],
+        ]
+        + second,
         compiler_params=pltpu.CompilerParams(vmem_limit_bytes=24 << 20),
         cost_estimate=pl.CostEstimate(
             flops=6_000_000_000, bytes_accessed=4_000_000, transcendentals=4_000_000
         ),
         name="attend",
-    )(tab, received, *state)
+    )(tab, in_hbm(received) if part else received, *state)
 
 
 def project_kernel(order, mine, theirs, w, base, o, ws, acc, sem):

time: 223 us -> 223 us (level)
  no operation moved by 1% of the time
where the time goes in v7:
time: 223 us; the launch traced here: 222 us
  waiting for transfers between devices  60 us (27%)
  blocking collectives  50.1 us (22%)
  starting transfers between devices  48.1 us (22%)
  Pallas kernels  46.8 us (21%)
  local copies, waits for them, and re-layouts  7.27 us (3%)
  other arithmetic  6.72 us (3%)
    all_to_all x3, blocking collectives, exchange(): lax.all_to_all(array, ALL, 0, 0, tiled=True, axis_index_groups=groups)  50.1 us
    all_to_all x5, waiting for transfers between devices, exchange(): lax.all_to_all(array, ALL, 0, 0, tiled=True, axis_index_groups=groups)  28.7 us
    pallas_call x2, Pallas kernels, attend(): pl.pallas_call(functools.partial(attend_kernel, part=part), out_shape=out...  22.4 us
    all_to_all x5, starting transfers between devices, exchange(): lax.all_to_all(array, ALL, 0, 0, tiled=True, axis_index_groups=groups)  20.9 us
    pallas_call x2, Pallas kernels, project(): pl.pallas_call(project_kernel, in_specs=[pl.BlockSpec(memory_space=pltpu....  13.8 us
    all_to_all x1, waiting for transfers between devices, shards(): arrived = lax.all_to_all(rows, ALL, 0, 0, tiled=True)  10.9 us
    ppermute x4, waiting for transfers between devices, ring(): return lax.ppermute(array, 'y', [(i, (i + step) % 4) for i in range(4)])  10.4 us
    all_to_all x1, starting transfers between devices, shards(): returned = lax.all_to_all(back.reshape(128, 8, 128), ALL, 0, 0, tiled=True)  8.43 us
  transfers between devices with their start and end apart: 14, of which 9 were waited for; matrix products, arithmetic and copies ran while one was open for 4% of the time, Pallas kernels for 12%

profile of v7, /device:TPU:1, one launch (start us, length us, event | category | flops | bytes accessed | tf_op | source)
XLA Modules:
  0.0 221.9 jit_solution(17671404807545977180)
XLA Ops:
  0.0 2.4 %pack_heads.1 = bf16[4,3,512,128]{3,2,1,0:T(8,128)(2,1)} custom-call(bf16[512,512]{1,0:T(8,128)(2,1)} %q.1, bf16[512,512]{1,0:T(8,128)(2,1)} %k.1, bf16[512,512]{1,0:T(8,128)(2,1)} %v.1), custom_call_target="tpu_custom_call" | custom-call | tf_op jit(solution)/shard_map/pack_heads/pallas_call | solution.py:80
  2.4 17.7 %all_to_all.55.got.q = bf16[4,3,512,128]{3,2,1,0:T(8,128)(2,1)S(1)} all-to-all(bf16[4,3,512,128]{3,2,1,0:T(8,128)(2,1)} %pack_heads.1), channel_id=1, replica_groups={{0,32,64,96},{1,9,17,25},{8,40,72,104},{33,41,49,57},{16,48,80,112},{65..., dimensions={0} | all-to-all | bytes 3145728 | tf_op jit(solution)/shard_map/all_to_all | solution.py:50
  20.1 0.4 pack_parts.1
  20.6 23.0 %all_to_all.56 = bf16[4,2,1280,128]{3,2,1,0:T(8,128)(2,1)S(1)} all-to-all(bf16[4,2,1280,128]{3,2,1,0:T(8,128)(2,1)S(1)} %get-tuple-element.22), channel_id=1, replica_groups={{0,8,16,24},{1,33,65,97},{32,40,48,56},{9,41,73,105},{64,72,80,88},{17,..., dimensions={0} | all-to-all | bytes 5242880 | tf_op jit(solution)/shard_map/all_to_all | solution.py:50
  43.6 4.6 %all-to-all-start.2 = ((bf16[4,2,1024,128]{3,2,1,0:T(8,128)(2,1)}), bf16[4,2,1024,128]{3,2,1,0:T(8,128)(2,1)}, u32[]{:S(2)}, u32[]{:S(2)}) async-start(bf16[4,2,1024,128]{3,2,1,0:T(8,128)(2,1)} %copy-done.1), calls=%async_computation.2 | async-start | bytes 4194304 | tf_op jit(solution)/shard_map/all_to_all | solution.py:50
  48.2 0.6 reduce_sum.36
  49.8 11.2 %attend.2 = (f32[4,1,512]{2,1,0:T(1,128)S(1)}, f32[4,1,512]{2,1,0:T(1,128)S(1)}, f32[4,128,512]{2,1,0:T(8,128)}, bf16[4,128,512]{2,1,0:T(8,128)(2,1)}) custom-call(s32[51]{0:T(128)S(1)} %concatenate.17.tab, bf16[8,1280,128]{2,1,0:T(8,128)(2,1)S(1)} %bitcast.72), custom_call_target="tpu_custom_call" | custom-call | flops 6000000000 | bytes 4000000 | tf_op jit(solution)/shard_map/attend/pallas_call | solution.py:271
  61.0 2.9 %all-to-all-done.2 = bf16[4,2,1024,128]{3,2,1,0:T(8,128)(2,1)} async-done(((bf16[4,2,1024,128]{3,2,1,0:T(8,128)(2,1)}), bf16[4,2,1024,128]{3,2,1,0:T(8,128)(2,1)}, u32[]{:S(2)}, u32[]{:S(2)}) %all-to-all-start.2) | async-done | bytes 2097184 | tf_op jit(solution)/shard_map/all_to_all | solution.py:50
  63.9 11.2 %attend.3 = bf16[16,128,128]{2,1,0:T(8,128)(2,1)} custom-call(s32[51]{0:T(128)S(1)} %concatenate.17.tab, bf16[8,1024,128]{2,1,0:T(8,128)(2,1)} %bitcast.5.r, f32[4,1,512]{2,1,0:T(1,128)S(1)} %get-tuple-element.26.refs_0_, f32[4,1,512]{2,1,0:T(1,128)S(1)} %get-tuple-element.27.refs_1_, f32[4,128,512]{2,1,0:T(8,128)} %get-tuple-element.28.refs_2_, ...), custom_call_target="tpu_custom_call" | custom-call | flops 6000000000 | bytes 4000000 | tf_op jit(solution)/shard_map/attend/pallas_call | solution.py:271
  75.1 3.6 %all-to-all-start.3 = ((bf16[16,128,128]{2,1,0:T(8,128)(2,1)}), bf16[16,128,128]{2,1,0:T(8,128)(2,1)S(1)}, u32[]{:S(2)}, u32[]{:S(2)}) async-start(bf16[16,128,128]{2,1,0:T(8,128)(2,1)} %attend.3), calls=%async_computation.3 | async-start | bytes 1048576 | tf_op jit(solution)/shard_map/all_to_all | solution.py:50
  79.2 0.3 convolution_convert_fusion.1.base
  79.6 8.0 %all-to-all-done.3 = bf16[16,128,128]{2,1,0:T(8,128)(2,1)S(1)} async-done(((bf16[16,128,128]{2,1,0:T(8,128)(2,1)}), bf16[16,128,128]{2,1,0:T(8,128)(2,1)S(1)}, u32[]{:S(2)}, u32[]{:S(2)}) %all-to-all-start.3) | async-done | bytes 524320 | tf_op jit(solution)/shard_map/all_to_all | solution.py:50
  87.6 0.4 copy.25
  88.0 0.2 convolution_convert_fusion.2
  88.3 0.9 broadcast_in_dim.10
  89.2 4.2 %all-to-all-start.4 = ((bf16[4,144,512]{2,1,0:T(8,128)(2,1)}), bf16[4,144,512]{2,1,0:T(8,128)(2,1)S(1)}, u32[]{:S(2)}, u32[]{:S(2)}) async-start(bf16[4,144,512]{2,1,0:T(8,128)(2,1)} %broadcast_in_dim.10), calls=%async_computation.4 | async-start | bytes 1179648 | tf_op jit(solution)/shard_map/all_to_all | solution.py:492
  93.4 7.3 %all-to-all-done.4.mine = bf16[4,144,512]{2,1,0:T(8,128)(2,1)S(1)} async-done(((bf16[4,144,512]{2,1,0:T(8,128)(2,1)}), bf16[4,144,512]{2,1,0:T(8,128)(2,1)S(1)}, u32[]{:S(2)}, u32[]{:S(2)}) %all-to-all-start.4) | async-done | bytes 589856 | tf_op jit(solution)/shard_map/all_to_all | solution.py:492
  100.6 5.7 %collective-permute-start = (bf16[4,144,512]{2,1,0:T(8,128)(2,1)S(1)}, bf16[4,144,512]{2,1,0:T(8,128)(2,1)S(1)}, u32[]{:S(2)}, u32[]{:S(2)}) collective-permute-start(bf16[4,144,512]{2,1,0:T(8,128)(2,1)S(1)} %all-to-all-done.4.mine), channel_id=1, source_target_pairs={{0,1},{1,0},{2,3},{3,2},{4,5},{5,4},{6,7},{7,6},{8,9},{9,8},{10,11... | collective-permute-start | bytes 1769480 | tf_op jit(solution)/shard_map/ppermute | solution.py:419
  106.6 0.9 copy.40
  107.6 0.4 collective-permute-done.theirs
  108.0 5.1 %project.2 = bf16[128,8,128]{2,1,0:T(8,128)(2,1)} custom-call(s32[8]{0:T(128)S(1)} %pad_add_fusion.1.order, bf16[4,144,512]{2,1,0:T(8,128)(2,1)S(1)} %all-to-all-done.4.mine, bf16[4,144,512]{2,1,0:T(8,128)(2,1)S(1)} %collective-permute-done.theirs, bf16[4096,1024]{1,0:T(8,128)(2,1)} %w.3, bf16[128,1024]{1,0:T(8,128)(2,1)S(1)} %convolution_convert_fusion.1.base), custom_call_target="tpu_custom_call" | custom-call | flops 1073741824 | bytes 9961472 | tf_op jit(solution)/shard_map/project/pallas_call | solution.py:319
  113.1 3.8 %all-to-all-start.5 = ((bf16[128,8,128]{2,1,0:T(8,128)(2,1)}), bf16[128,8,128]{2,1,0:T(8,128)(2,1)S(1)}, u32[]{:S(2)}, u32[]{:S(2)}) async-start(bf16[128,8,128]{2,1,0:T(8,128)(2,1)} %project.2), calls=%async_computation.5 | async-start | bytes 524288 | tf_op jit(solution)/shard_map/all_to_all | solution.py:504
  117.1 10.9 %all-to-all-done.5 = bf16[128,8,128]{2,1,0:T(8,128)(2,1)S(1)} async-done(((bf16[128,8,128]{2,1,0:T(8,128)(2,1)}), bf16[128,8,128]{2,1,0:T(8,128)(2,1)S(1)}, u32[]{:S(2)}, u32[]{:S(2)}) %all-to-all-start.5) | async-done | bytes 262176 | tf_op jit(solution)/shard_map/all_to_all | solution.py:504
  128.2 0.4 multiply_reduce_fusion
  128.7 9.4 %all_to_all.57 = bf16[4,8,8192]{2,1,0:T(8,128)(2,1)S(1)} all-to-all(bf16[4,8,8192]{2,1,0:T(8,128)(2,1)S(1)} %broadcast_in_dim.11), channel_id=1, replica_groups={{0,32,64,96},{1,9,17,25},{8,40,72,104},{33,41,49,57},{16,48,80,112},{65..., dimensions={0} | all-to-all | bytes 1048576 | tf_op jit(solution)/shard_map/all_to_all | solution.py:50
  138.1 1.5 broadcast_in_dim.13
  139.7 3.6 %all-to-all-start.7 = ((bf16[4,32,8192]{2,1,0:T(8,128)(2,1)}), bf16[4,32,8192]{2,1,0:T(8,128)(2,1)S(1)}, u32[]{:S(2)}, u32[]{:S(2)}) async-start(bf16[4,32,8192]{2,1,0:T(8,128)(2,1)} %broadcast_in_dim.13), calls=%async_computation.7 | async-start | bytes 4194304 | tf_op jit(solution)/shard_map/all_to_all | solution.py:50
  143.3 1.4 collective-permute-start.2
  144.8 10.4 %collective-permute-done.2 = bf16[512,512]{1,0:T(8,128)(2,1)S(1)} collective-permute-done((bf16[512,512]{1,0:T(8,128)(2,1)}, bf16[512,512]{1,0:T(8,128)(2,1)S(1)}, u32[]{:S(2)}, u32[]{:S(2)}) %collective-permute-start.2) | collective-permute-done | bytes 524320 | tf_op jit(solution)/shard_map/ppermute | solution.py:423
  155.2 0.8 slice.44
  156.0 3.0 %collective-permute-start.4 = (bf16[256,512]{1,0:T(8,128)(2,1)}, bf16[256,512]{1,0:T(8,128)(2,1)}, u32[]{:S(2)}, u32[]{:S(2)}) collective-permute-start(bf16[256,512]{1,0:T(8,128)(2,1)} %slice.44), channel_id=1, source_target_pairs={{0,6},{2,0},{4,2},{6,4},{1,7},{3,1},{5,3},{7,5},{8,14},{10,8},{12,... | collective-permute-start | bytes 786440 | tf_op jit(solution)/shard_map/ppermute | solution.py:423
  159.0 0.8 slice.43
  159.9 6.1 %experts.1 = bf16[128,8192]{1,0:T(8,128)(2,1)} custom-call(bf16[128,8192]{1,0:T(8,128)(2,1)S(1)} %bitcast.71, bf16[1,8192,256]{2,1,0:T(8,128)(2,1)} %gate.1, bf16[1,8192,256]{2,1,0:T(8,128)(2,1)} %up.1, bf16[1,256,8192]{2,1,0:T(8,128)(2,1)} %down.1), custom_call_target="tpu_custom_call" | custom-call | flops 1610000000 | bytes 16800000 | tf_op jit(solution)/shard_map/experts/pallas_call | solution.py:378
  166.0 5.6 %all-to-all-start.8 = ((bf16[4,32,8192]{2,1,0:T(8,128)(2,1)}), bf16[4,32,8192]{2,1,0:T(8,128)(2,1)S(1)}, u32[]{:S(2)}, u32[]{:S(2)}) async-start(bf16[4,32,8192]{2,1,0:T(8,128)(2,1)} %bitcast.73), calls=%async_computation.8 | async-start | bytes 4194304 | tf_op jit(solution)/shard_map/all_to_all | solution.py:50
  171.6 1.1 maximum_bitcast_fusion
  172.7 2.9 %pad_maximum_fusion.mine = bf16[4,512,512]{2,1,0:T(8,128)(2,1)} fusion(bf16[1,512,512]{2,1,0:T(8,128)(2,1)S(1)} %maximum_bitcast_fusion, bf16[1,512,512]{2,1,0:T(8,128)(2,1)} %bitcast.81, bf16[1,512,512]{2,1,0:T(8,128)(2,1)} %bitcast.82, bf16[1,512,512]{2,1,0:T(8,128)(2,1)} %bitcast.80), kind=kLoop, calls=%fused_computation.1 | loop fusion | flops 3145728 | bytes 4194304 | tf_op jit(solution)/shard_map/stack | solution.py:509
  175.6 0.5 collective-permute-start.5
  176.1 11.1 %all-to-all-done.8.parts = bf16[4,32,8192]{2,1,0:T(8,128)(2,1)S(1)} async-done(((bf16[4,32,8192]{2,1,0:T(8,128)(2,1)}), bf16[4,32,8192]{2,1,0:T(8,128)(2,1)S(1)}, u32[]{:S(2)}, u32[]{:S(2)}) %all-to-all-start.8) | async-done | bytes 2097184 | tf_op jit(solution)/shard_map/all_to_all | solution.py:50
  187.3 1.6 add.183
  188.9 3.5 %all-to-all-start.9 = ((bf16[4,8,8192]{2,1,0:T(8,128)(2,1)}), bf16[4,8,8192]{2,1,0:T(8,128)(2,1)S(1)}, u32[]{:S(2)}, u32[]{:S(2)}) async-start(bf16[4,8,8192]{2,1,0:T(8,128)(2,1)} %bitcast.20), calls=%async_computation.9 | async-start | bytes 1048576 | tf_op jit(solution)/shard_map/all_to_all | solution.py:50
  192.7 6.6 %all-to-all-done.9 = bf16[4,8,8192]{2,1,0:T(8,128)(2,1)S(1)} async-done(((bf16[4,8,8192]{2,1,0:T(8,128)(2,1)}), bf16[4,8,8192]{2,1,0:T(8,128)(2,1)S(1)}, u32[]{:S(2)}, u32[]{:S(2)}) %all-to-all-start.9) | async-done | bytes 524320 | tf_op jit(solution)/shard_map/all_to_all | solution.py:50
  199.4 0.3 convolution_convert_fusion
  199.7 0.8 reshape.114
  200.5 8.4 %all-to-all-start.10 = ((bf16[128,8,128]{2,1,0:T(8,128)(2,1)}), bf16[128,8,128]{2,1,0:T(8,128)(2,1)S(1)}, u32[]{:S(2)}, u32[]{:S(2)}) async-start(bf16[128,8,128]{2,1,0:T(8,128)(2,1)} %reshape.114), calls=%async_computation.10 | async-start | bytes 524288 | tf_op jit(solution)/shard_map/all_to_all | solution.py:535
  209.0 8.8 %project.3 = bf16[512,1024]{1,0:T(8,128)(2,1)S(1)} custom-call(s32[8]{0:T(128)S(1)} %pad_add_fusion.order, bf16[4,512,512]{2,1,0:T(8,128)(2,1)} %pad_maximum_fusion.mine, bf16[4,512,512]{2,1,0:T(8,128)(2,1)} %collective-permute-done.5.theirs, bf16[4096,1024]{1,0:T(8,128)(2,1)} %w.3, bf16[512,1024]{1,0:T(8,128)(2,1)S(1)} %copy-done.2), custom_call_target="tpu_custom_call" | custom-call | flops 4294967296 | bytes 14680064 | tf_op jit(solution)/shard_map/project/pallas_call | solution.py:319
  217.8 2.3 %all-to-all-done.10 = bf16[128,8,128]{2,1,0:T(8,128)(2,1)S(1)} async-done(((bf16[128,8,128]{2,1,0:T(8,128)(2,1)}), bf16[128,8,128]{2,1,0:T(8,128)(2,1)S(1)}, u32[]{:S(2)}, u32[]{:S(2)}) %all-to-all-start.10) | async-done | bytes 262176 | tf_op jit(solution)/shard_map/all_to_all | solution.py:535
  220.1 0.5 fusion.4
  220.5 1.4 add_convert_fusion
  (68 shorter events, 2.3 us)
Async XLA Ops:
  0.0 192.5 %copy-start = (bf16[8192,1]{0,1:T(2,128)(2,1)S(1)}, bf16[8192,1]{0,1:T(2,128)(2,1)}, u32[]{:S(2)}) copy-start(bf16[8192,1]{0,1:T(2,128)(2,1)} %param.22) | copy-start | bytes 49156
  20.5 23.0 %copy-start.1 = (bf16[4,2,1024,128]{3,2,1,0:T(8,128)(2,1)}, bf16[4,2,1024,128]{3,2,1,0:T(8,128)(2,1)S(1)}, u32[]{:S(2)}) copy-start(bf16[4,2,1024,128]{3,2,1,0:T(8,128)(2,1)S(1)} %get-tuple-element.24) | copy-start | bytes 6291460
  43.6 4.6 %copy-start.5 = (s32[8192]{0:T(1024)S(1)}, s32[8192]{0:T(1024)}, u32[]{:S(2)}) copy-start(s32[8192]{0:T(1024)} %param.18) | copy-start | bytes 98308
  43.6 5.3 %copy-start.7 = (s32[8,128]{1,0:T(8,128)S(1)}, s32[8,128]{1,0:T(8,128)}, u32[]{:S(2)}) copy-start(s32[8,128]{1,0:T(8,128)} %param.21) | copy-start | bytes 12292
  43.6 6.2 %copy-start.6 = (f32[2,1024]{1,0:T(2,128)S(1)}, f32[2,1024]{1,0:T(2,128)}, u32[]{:S(2)}) copy-start(f32[2,1024]{1,0:T(2,128)} %param.20) | copy-start | bytes 24580
  43.6 20.3 %all-to-all-start.2 = ((bf16[4,2,1024,128]{3,2,1,0:T(8,128)(2,1)}), bf16[4,2,1024,128]{3,2,1,0:T(8,128)(2,1)}, u32[]{:S(2)}, u32[]{:S(2)}) async-start(bf16[4,2,1024,128]{3,2,1,0:T(8,128)(2,1)} %copy-done.1), calls=%async_computation.2 | async-start | bytes 4194304 | tf_op jit(solution)/shard_map/all_to_all | solution.py:50
  63.9 15.3 %copy-start.2 = (bf16[512,1024]{1,0:T(8,128)(2,1)S(1)}, bf16[512,1024]{1,0:T(8,128)(2,1)}, u32[]{:S(2)}) copy-start(bf16[512,1024]{1,0:T(8,128)(2,1)} %base.1) | copy-start | bytes 3145732
  75.1 12.5 %all-to-all-start.3 = ((bf16[16,128,128]{2,1,0:T(8,128)(2,1)}), bf16[16,128,128]{2,1,0:T(8,128)(2,1)S(1)}, u32[]{:S(2)}, u32[]{:S(2)}) async-start(bf16[16,128,128]{2,1,0:T(8,128)(2,1)} %attend.3), calls=%async_computation.3 | async-start | bytes 1048576 | tf_op jit(solution)/shard_map/all_to_all | solution.py:50
  89.2 11.5 %all-to-all-start.4 = ((bf16[4,144,512]{2,1,0:T(8,128)(2,1)}), bf16[4,144,512]{2,1,0:T(8,128)(2,1)S(1)}, u32[]{:S(2)}, u32[]{:S(2)}) async-start(bf16[4,144,512]{2,1,0:T(8,128)(2,1)} %broadcast_in_dim.10), calls=%async_computation.4 | async-start | bytes 1179648 | tf_op jit(solution)/shard_map/all_to_all | solution.py:492
  100.6 7.4 %collective-permute-start = (bf16[4,144,512]{2,1,0:T(8,128)(2,1)S(1)}, bf16[4,144,512]{2,1,0:T(8,128)(2,1)S(1)}, u32[]{:S(2)}, u32[]{:S(2)}) collective-permute-start(bf16[4,144,512]{2,1,0:T(8,128)(2,1)S(1)} %all-to-all-done.4.mine), channel_id=1, source_target_pairs={{0,1},{1,0},{2,3},{3,2},{4,5},{5,4},{6,7},{7,6},{8,9},{9,8},{10,11... | collective-permute-start | bytes 1769480 | tf_op jit(solution)/shard_map/ppermute | solution.py:419
  113.1 15.0 %all-to-all-start.5 = ((bf16[128,8,128]{2,1,0:T(8,128)(2,1)}), bf16[128,8,128]{2,1,0:T(8,128)(2,1)S(1)}, u32[]{:S(2)}, u32[]{:S(2)}) async-start(bf16[128,8,128]{2,1,0:T(8,128)(2,1)} %project.2), calls=%async_computation.5 | async-start | bytes 524288 | tf_op jit(solution)/shard_map/all_to_all | solution.py:504
  139.7 20.2 %all-to-all-start.7 = ((bf16[4,32,8192]{2,1,0:T(8,128)(2,1)}), bf16[4,32,8192]{2,1,0:T(8,128)(2,1)S(1)}, u32[]{:S(2)}, u32[]{:S(2)}) async-start(bf16[4,32,8192]{2,1,0:T(8,128)(2,1)} %broadcast_in_dim.13), calls=%async_computation.7 | async-start | bytes 4194304 | tf_op jit(solution)/shard_map/all_to_all | solution.py:50
  143.3 11.9 %collective-permute-start.2 = (bf16[512,512]{1,0:T(8,128)(2,1)}, bf16[512,512]{1,0:T(8,128)(2,1)S(1)}, u32[]{:S(2)}, u32[]{:S(2)}) collective-permute-start(bf16[512,512]{1,0:T(8,128)(2,1)} %bitcast.78), channel_id=1, source_target_pairs={{0,6},{2,0},{4,2},{6,4},{1,7},{3,1},{5,3},{7,5},{8,14},{10,8},{12,... | collective-permute-start | bytes 1572872 | tf_op jit(solution)/shard_map/ppermute | solution.py:423
  144.6 14.4 %collective-permute-start.1 = (bf16[512,512]{1,0:T(8,128)(2,1)}, bf16[512,512]{1,0:T(8,128)(2,1)S(1)}, u32[]{:S(2)}, u32[]{:S(2)}) collective-permute-start(bf16[512,512]{1,0:T(8,128)(2,1)} %bitcast.79), channel_id=1, source_target_pairs={{0,2},{2,4},{4,6},{6,0},{1,3},{3,5},{5,7},{7,1},{8,10},{10,12},{12... | collective-permute-start | bytes 1572872 | tf_op jit(solution)/shard_map/ppermute | solution.py:423
  155.2 4.6 %copy-start.3 = (bf16[512,512]{1,0:T(8,128)(2,1)}, bf16[512,512]{1,0:T(8,128)(2,1)S(1)}, u32[]{:S(2)}) copy-start(bf16[512,512]{1,0:T(8,128)(2,1)S(1)} %collective-permute-done.2) | copy-start | bytes 1572868
  156.0 15.7 %collective-permute-start.4 = (bf16[256,512]{1,0:T(8,128)(2,1)}, bf16[256,512]{1,0:T(8,128)(2,1)}, u32[]{:S(2)}, u32[]{:S(2)}) collective-permute-start(bf16[256,512]{1,0:T(8,128)(2,1)} %slice.44), channel_id=1, source_target_pairs={{0,6},{2,0},{4,2},{6,4},{1,7},{3,1},{5,3},{7,5},{8,14},{10,8},{12,... | collective-permute-start | bytes 786440 | tf_op jit(solution)/shard_map/ppermute | solution.py:423
  159.0 0.9 copy-start.4
  159.9 11.7 %collective-permute-start.3 = (bf16[256,512]{1,0:T(8,128)(2,1)}, bf16[256,512]{1,0:T(8,128)(2,1)}, u32[]{:S(2)}, u32[]{:S(2)}) collective-permute-start(bf16[256,512]{1,0:T(8,128)(2,1)} %slice.43), channel_id=1, source_target_pairs={{0,2},{2,4},{4,6},{6,0},{1,3},{3,5},{5,7},{7,1},{8,10},{10,12},{12... | collective-permute-start | bytes 786440 | tf_op jit(solution)/shard_map/ppermute | solution.py:423
  166.0 21.3 %all-to-all-start.8 = ((bf16[4,32,8192]{2,1,0:T(8,128)(2,1)}), bf16[4,32,8192]{2,1,0:T(8,128)(2,1)S(1)}, u32[]{:S(2)}, u32[]{:S(2)}) async-start(bf16[4,32,8192]{2,1,0:T(8,128)(2,1)} %bitcast.73), calls=%async_computation.8 | async-start | bytes 4194304 | tf_op jit(solution)/shard_map/all_to_all | solution.py:50
  172.7 3.4 %copy-start.8 = (s32[4]{0:T(128)S(1)}, s32[4]{0:T(128)}, u32[]{:S(2)}) copy-start(s32[4]{0:T(128)} %constant.144.clone) | copy-start | bytes 52
  175.6 24.1 %collective-permute-start.5 = (bf16[4,512,512]{2,1,0:T(8,128)(2,1)}, bf16[4,512,512]{2,1,0:T(8,128)(2,1)}, u32[]{:S(2)}, u32[]{:S(2)}) collective-permute-start(bf16[4,512,512]{2,1,0:T(8,128)(2,1)} %pad_maximum_fusion.mine), channel_id=1, source_target_pairs={{0,1},{1,0},{2,3},{3,2},{4,5},{5,4},{6,7},{7,6},{8,9},{9,8},{10,11... | collective-permute-start | bytes 6291464 | tf_op jit(solution)/shard_map/ppermute | solution.py:419
  188.9 10.4 %all-to-all-start.9 = ((bf16[4,8,8192]{2,1,0:T(8,128)(2,1)}), bf16[4,8,8192]{2,1,0:T(8,128)(2,1)S(1)}, u32[]{:S(2)}, u32[]{:S(2)}) async-start(bf16[4,8,8192]{2,1,0:T(8,128)(2,1)} %bitcast.20), calls=%async_computation.9 | async-start | bytes 1048576 | tf_op jit(solution)/shard_map/all_to_all | solution.py:50
  200.5 19.5 %all-to-all-start.10 = ((bf16[128,8,128]{2,1,0:T(8,128)(2,1)}), bf16[128,8,128]{2,1,0:T(8,128)(2,1)S(1)}, u32[]{:S(2)}, u32[]{:S(2)}) async-start(bf16[128,8,128]{2,1,0:T(8,128)(2,1)} %reshape.114), calls=%async_computation.10 | async-start | bytes 524288 | tf_op jit(solution)/shard_map/all_to_all | solution.py:535
